TPU v7x, 128 devices: a whole 4x4x4 slice. The times are simulated.
128 devices in a mesh: sub: 16 (over x, y), rep: 8 (over z, core).
Axes of the slice: x: 4, y: 4, z: 4, core: 2. Of those that a mesh axis runs over, the one named last changes fastest.
Arguments:
- rhs: float32 [4096, 128], P('sub'), may hold values from -31 to 31
- schur_diag: bfloat16 [4096, 256], P('sub'), may hold values from -0.375 to 0.375
- precond: bfloat16 [4096, 512], P('sub'), may hold values from -0.25 to 0.25
- halo_ids: int32 [16, 2], P('sub'), may hold values from 0 to 31, as said below
- factors: bfloat16 [256, 1024, 1024], P(('sub', 'rep')), may hold values from -0.1875 to 0.1875
- couplings: bfloat16 [256, 1024, 512], P(('sub', 'rep')), may hold values from -0.09375 to 0.09375
- block_ids: int32 [256, 4], P(('sub', 'rep')), may hold values from 0 to 31
- counts: int32 [128], P(('sub', 'rep')), may hold values from 1 to 2, 160 in all
Outputs:
- solution: float32 [4096, 128], P('sub')
Inputs may be any that keep to these rules, and one draw needn't show every extreme that they name: `halo_ids`: in row d the first 1 entries name blocks owned by index d - 1 of sub and the others blocks owned by index d + 1, cyclically; block b is owned by index b // 2. counts[i] belongs to device i of sub+rep, sub slowest; slots k with k % 2 >= counts[k // 2] are not part of the operator.
All inputs are finite; a program needn't handle non-finite values.
Results may differ from a plain program's by a relative error of at most 0.0031.
Values may be sent and summed in bfloat16 or wider, within the bound.
No kernel may reach another device: no remote copies, remote signals or barrier semaphores. Data moves between devices by JAX's collectives and lax.ppermute only.
A program may use at most 64 MiB of HBM per device.

v0:
```python
import functools

import jax
import jax.numpy as jnp
from jax import lax
from jax.sharding import Mesh
from jax.sharding import PartitionSpec as P

BI = 128
GB_DEV = 2
SUB = ("sub_0", "sub_1")
SUB_REP = ("sub_0", "sub_1", "rep")


def laid_out(blocks, dim):
    shape = list(blocks.shape[1:])
    shape[dim] *= blocks.shape[0]
    return jnp.moveaxis(blocks, 0, dim).reshape(shape)


def from_everyone(array, axis):
    copies = jnp.broadcast_to(array, (lax.axis_size(axis), *array.shape))
    return lax.all_to_all(copies, axis, split_axis=0, concat_axis=0, tiled=True)


def collect(array, axis, dim):
    return laid_out(from_everyone(array, axis), dim)


def cut_along(array, dim, count):
    shape = array.shape
    blocks = array.reshape(*shape[:dim], count, shape[dim] // count, *shape[dim + 1 :])
    return jnp.moveaxis(blocks, dim, 0)


def sum_at_owner(array, axis, dim):
    blocks = cut_along(array, dim, lax.axis_size(axis))
    arrived = lax.all_to_all(blocks, axis, split_axis=0, concat_axis=0, tiled=True)
    return arrived.sum(axis=0)


def over_copies(array, axis):
    everything = from_everyone(array, axis)
    return jnp.sum(everything, axis=0)


def padded_2(cells, sides, width):
    for axis, dim in sides:
        count = lax.axis_size(axis)
        head = lax.slice_in_dim(cells, 0, width, axis=dim)
        tail = lax.slice_in_dim(cells, cells.shape[dim] - width, cells.shape[dim], axis=dim)
        cells = jnp.concatenate(
            [
                lax.ppermute(tail, axis, [(i, (i + 1) % count) for i in range(count)]),
                cells,
                lax.ppermute(head, axis, [((i + 1) % count, i) for i in range(count)]),
            ],
            axis=dim,
        )
    return cells


def gathered_total(array, axis):
    blocks = lax.all_gather(array, axis)
    return blocks.sum(axis=0)


def by_axis(array, axes):
    return functools.reduce(lax.psum, axes, array)


def column_sums(left, right):
    return jnp.sum(left * right, axis=0)


def on_device(rhs, schur_diag, precond, halo_ids, factors, couplings, block_ids, counts):
    rows_here = rhs.shape[0]
    columns = rhs.shape[1]
    sub_count = lax.axis_size(SUB)
    transposed = (((0,), (0,)), ((), ()))

    def apply_schur(field):
        rounded = field.astype(jnp.bfloat16)
        whole = collect(rounded, SUB, 0)
        blocks = whole.reshape(-1, BI, columns)
        width = block_ids.shape[1] * BI

        def slot_step(slot, total):
            listed = block_ids[slot]
            picked = blocks[listed].reshape(width, columns)
            factor = factors[slot]
            coupling = couplings[slot]
            first = jnp.dot(coupling, picked, preferred_element_type=jnp.float32).astype(
                jnp.bfloat16
            )
            second = jnp.dot(factor, first, preferred_element_type=jnp.float32).astype(jnp.bfloat16)
            third = lax.dot_general(
                factor, second, transposed, preferred_element_type=jnp.float32
            ).astype(jnp.bfloat16)
            fourth = lax.dot_general(
                coupling, third, transposed, preferred_element_type=jnp.float32
            )
            return total.at[listed].add(fourth.reshape(-1, BI, columns))

        total = lax.fori_loop(0, counts[0], slot_step, jnp.zeros(blocks.shape, jnp.float32))
        flat = total.reshape(-1, columns)
        coupled = over_copies(sum_at_owner(flat, SUB, 0), "rep")
        local = jnp.dot(schur_diag, rounded, preferred_element_type=jnp.float32)
        return 3.0 * field + local - coupled

    def precondition(field):
        listed = halo_ids[0]
        rounded = field.astype(jnp.bfloat16)
        padded = padded_2(rounded, ((SUB, 0),), rows_here)
        owner = listed // GB_DEV
        place = (owner - lax.axis_index(SUB) + 1) % sub_count * GB_DEV + listed % GB_DEV
        halo_rows = padded.reshape(-1, BI, columns)[place]
        extended = jnp.concatenate([rounded, halo_rows.reshape(-1, columns)], axis=0)
        return field + jnp.dot(precond, extended, preferred_element_type=jnp.float32)

    def orthogonal(field, basis):
        stacked = jnp.stack(basis)
        local_sums = jnp.concatenate(
            [jnp.sum(stacked * field[None], axis=1), column_sums(field, field)[None]], axis=0
        )
        totals = by_axis(local_sums, SUB)
        coeffs = totals[:-1]
        rest = field - jnp.sum(coeffs[:, None, :] * stacked, axis=0)
        length = jnp.sqrt(totals[-1] - jnp.sum(coeffs * coeffs, axis=0))
        return (coeffs, rest, length)

    start_norm = jnp.sqrt(gathered_total(column_sums(rhs, rhs), SUB))
    first_basis = rhs / start_norm
    first_dir = precondition(first_basis)
    coeffs_one, rest_one, length_one = orthogonal(apply_schur(first_dir), [first_basis])
    second_basis = rest_one / length_one
    second_dir = precondition(second_basis)
    coeffs_two, rest_two, length_two = orthogonal(
        apply_schur(second_dir), [first_basis, second_basis]
    )
    upper_one = coeffs_one[0]
    upper_two = coeffs_two[0]
    middle = coeffs_two[1]
    radius_one = jnp.sqrt(upper_one * upper_one + length_one * length_one)
    cosine_one = upper_one / radius_one
    sine_one = length_one / radius_one
    rotated_top = cosine_one * upper_two + sine_one * middle
    rotated_low = cosine_one * middle - sine_one * upper_two
    weight_two = (
        -rotated_low * sine_one * start_norm / (rotated_low * rotated_low + length_two * length_two)
    )
    weight_one = (cosine_one * start_norm - rotated_top * weight_two) / radius_one
    return weight_one * first_dir + weight_two * second_dir


def solution(mesh):
    torus = Mesh(mesh.devices.reshape(4, 4, mesh.shape["rep"]), ("sub_0", "sub_1", "rep"))
    placed = (
        P(SUB, None),
        P(SUB, None),
        P(SUB, None),
        P(SUB, None),
        P(SUB_REP, None, None),
        P(SUB_REP, None, None),
        P(SUB_REP, None),
        P(SUB_REP),
    )
    return jax.shard_map(
        on_device, mesh=torus, in_specs=placed, out_specs=P(SUB, None), check_vma=False
    )
```

profile of v0, /device:TPU:0, one launch (start us, length us, event | category | flops | bytes accessed | tf_op | source)
XLA Modules:
  0.0 271.2 jit_solution(4384670608795092577)
XLA Ops:
  2.1 21.1 %all-gather.1 = f32[16,1,128]{2,1,0:T(1,128)S(1)} all-gather(f32[1,1,128]{2,1,0:T(1,128)S(1)} %bitcast.219), channel_id=2, replica_groups=mesh['sub_0'=4,'sub_1'=4,'rep'=8] {'sub_0','sub_1'}, dimensions={0}, use_global_device_ids=true | all-gather | bytes 8704 | tf_op jit(solution)/shard_map/all_gather | solution.py:64
  23.3 2.1 collective-permute-start.1
  27.6 5.4 %collective-permute-done = bf16[256,128]{0,1:T(8,128)(2,1)S(1)} collective-permute-done((bf16[256,128]{0,1:T(8,128)(2,1)S(1)}, bf16[256,128]{0,1:T(8,128)(2,1)S(1)}, u32[]{:S(2)}, u32[]{:S(2)}) %collective-permute-start) | collective-permute-done | bytes 65568 | tf_op jit(solution)/shard_map/ppermute | solution.py:54
  36.1 4.3 %all-to-all-start = ((bf16[16,256,128]{2,1,0:T(8,128)(2,1)}), bf16[16,256,128]{2,1,0:T(8,128)(2,1)}, u32[]{:S(2)}, u32[]{:S(2)}) async-start(bf16[16,256,128]{2,1,0:T(8,128)(2,1)} %broadcast_in_dim.14), calls=%async_computation | async-start | bytes 2097152 | tf_op jit(solution)/shard_map/all_to_all | solution.py:23
  40.4 3.0 %copy.39 = bf16[2,1024,512]{1,2,0:T(8,128)(2,1)S(1)} copy(bf16[2,1024,512]{2,1,0:T(8,128)(2,1)} %param.17) | data formatting | bytes 4194304 | tf_op jit(solution)/shard_map/while | solution.py:105
  43.4 9.9 %all-to-all-done = bf16[16,256,128]{2,1,0:T(8,128)(2,1)} async-done(((bf16[16,256,128]{2,1,0:T(8,128)(2,1)}), bf16[16,256,128]{2,1,0:T(8,128)(2,1)}, u32[]{:S(2)}, u32[]{:S(2)}) %all-to-all-start) | async-done | bytes 1048608 | tf_op jit(solution)/shard_map/all_to_all | solution.py:23
  53.3 1.6 broadcast.217.clone
  54.9 13.9 %while.20 = (s32[]{:T(128)}, f32[32,128,128]{2,1,0:T(8,128)}, s32[]{:T(128)}, s32[2,4]{1,0:T(2,128)}, bf16[2,1024,512]{1,2,0:T(8,128)(2,1)S(1)}, /*index=5*/bf16...) while((s32[]{:T(128)}, f32[32,128,128]{2,1,0:T(8,128)}, ...), condition=%wide.region_4.5_spmd, body=%wide.region_2.4_spmd.sunk | while | flops 805766144 | bytes 10360043 | solution.py:105
  56.4 1.8 gather_fusion
  58.2 3.8 %fusion.120 = bf16[1024,128]{1,0:T(8,128)(2,1)} fusion(bf16[2,1024,1024]{2,1,0:T(8,128)(2,1)} %get-tuple-element.295, s32[]{:T(128)S(6)} %select_n.120, bf16[512,128]{1,0:T(8,128)(2,1)S(1)} %bitcast.210, bf16[2,1024,512]{1,2,0:T(8,128)(2,1)S(1)} %get-tuple-element.294), kind=kOutput, calls=%fused_computation.12.clone.1 | convolution fusion | flops 402915328 | bytes 3539968 | tf_op jit(solution)/shard_map/while/body/dot_general | solution.py:96
  62.0 3.8 %fusion.121 = f32[4,128,128]{2,1,0:T(8,128)} fusion(bf16[4,128,1024]{2,1,0:T(8,128)(2,1)S(1)} %bitcast.206, bf16[1024,128]{1,0:T(8,128)(2,1)} %fusion.120, bf16[2,1024,1024]{2,1,0:T(8,128)(2,1)} %get-tuple-element.295, s32[]{:T(128)S(6)} %select_n.120), kind=kOutput, calls=%fused_computation.17.clone.1 | convolution fusion | flops 402784256 | bytes 3670020 | tf_op jit(solution)/shard_map/while/body/dot_general | solution.py:100
  65.7 2.4 scatter_fusion
  68.8 37.2 %all_to_all.30 = f32[16,256,128]{2,1,0:T(8,128)} all-to-all(f32[16,256,128]{2,1,0:T(8,128)} %bitcast.208), channel_id=1, replica_groups=mesh['sub_0'=4,'sub_1'=4,'rep'=8] {'sub_0','sub_1'}, dimensions={0} | all-to-all | bytes 4194304 | tf_op jit(solution)/shard_map/all_to_all | solution.py:38
  106.1 1.7 reduce_sum.113
  107.9 21.3 %all_to_all.31 = f32[8,256,128]{2,1,0:T(8,128)S(1)} all-to-all(f32[8,256,128]{2,1,0:T(8,128)S(1)} %broadcast_in_dim.15), channel_id=1, replica_groups=mesh['sub_0'=4,'sub_1'=4,'rep'=8] {'rep'}, dimensions={0} | all-to-all | bytes 2097152 | tf_op jit(solution)/shard_map/all_to_all | solution.py:23
  132.9 8.9 %psum.28 = f32[2,128]{1,0:T(2,128)S(1)} all-reduce(f32[2,128]{1,0:T(2,128)S(1)} %pad_maximum_fusion.3), channel_id=1, replica_groups=mesh['sub_0'=4,'sub_1'=4,'rep'=8] {'sub_0'}, use_global_device_ids=true, to_apply=%region_9.10 | all-reduce | flops 256 | bytes 2048 | tf_op jit(solution)/shard_map/psum | solution.py:69
  141.8 8.3 %psum.29 = f32[2,128]{1,0:T(2,128)S(1)} all-reduce(f32[2,128]{1,0:T(2,128)S(1)} %psum.28), channel_id=1, replica_groups=mesh['sub_0'=4,'sub_1'=4,'rep'=8] {'sub_1'}, use_global_device_ids=true, to_apply=%region_10.11 | all-reduce | flops 256 | bytes 2048 | tf_op jit(solution)/shard_map/psum | solution.py:69
  150.9 1.8 collective-permute-start.3
  153.0 2.2 collective-permute-done.3
  155.2 5.1 %collective-permute-done.2 = bf16[256,128]{0,1:T(8,128)(2,1)S(1)} collective-permute-done((bf16[256,128]{0,1:T(8,128)(2,1)S(1)}, bf16[256,128]{0,1:T(8,128)(2,1)S(1)}, u32[]{:S(2)}, u32[]{:S(2)}) %collective-permute-start.2) | collective-permute-done | bytes 65568 | tf_op jit(solution)/shard_map/ppermute | solution.py:54
  163.3 4.3 %all-to-all-start.3 = ((bf16[16,256,128]{2,1,0:T(8,128)(2,1)}), bf16[16,256,128]{2,1,0:T(8,128)(2,1)}, u32[]{:S(2)}, u32[]{:S(2)}) async-start(bf16[16,256,128]{2,1,0:T(8,128)(2,1)} %broadcast_in_dim.19), calls=%async_computation.3 | async-start | bytes 2097152 | tf_op jit(solution)/shard_map/all_to_all | solution.py:23
  167.7 12.9 %all-to-all-done.3 = bf16[16,256,128]{2,1,0:T(8,128)(2,1)} async-done(((bf16[16,256,128]{2,1,0:T(8,128)(2,1)}), bf16[16,256,128]{2,1,0:T(8,128)(2,1)}, u32[]{:S(2)}, u32[]{:S(2)}) %all-to-all-start.3) | async-done | bytes 1048608 | tf_op jit(solution)/shard_map/all_to_all | solution.py:23
  180.6 1.6 broadcast.217
  182.2 13.9 %while.21 = (s32[]{:T(128)}, f32[32,128,128]{2,1,0:T(8,128)}, s32[]{:T(128)}, s32[2,4]{1,0:T(2,128)}, bf16[2,1024,512]{1,2,0:T(8,128)(2,1)S(1)}, /*index=5*/bf16...) while((s32[]{:T(128)}, f32[32,128,128]{2,1,0:T(8,128)}, ...), condition=%wide.region_13.14_spmd, body=%wide.region_11.13_spmd.sunk | while | flops 805766144 | bytes 10360043 | solution.py:105
  183.6 1.8 gather_fusion.1
  185.4 3.8 %fusion.129 = bf16[1024,128]{1,0:T(8,128)(2,1)} fusion(bf16[2,1024,1024]{2,1,0:T(8,128)(2,1)} %get-tuple-element.325, s32[]{:T(128)S(6)} %select_n.122, bf16[512,128]{1,0:T(8,128)(2,1)S(1)} %bitcast.211, bf16[2,1024,512]{1,2,0:T(8,128)(2,1)S(1)} %get-tuple-element.324), kind=kOutput, calls=%fused_computation.32.clone.1 | convolution fusion | flops 402915328 | bytes 3539968 | tf_op jit(solution)/shard_map/while/body/dot_general | solution.py:96
  189.3 3.8 %fusion.130 = f32[4,128,128]{2,1,0:T(8,128)} fusion(bf16[4,128,1024]{2,1,0:T(8,128)(2,1)S(1)} %bitcast.207, bf16[1024,128]{1,0:T(8,128)(2,1)} %fusion.129, bf16[2,1024,1024]{2,1,0:T(8,128)(2,1)} %get-tuple-element.325, s32[]{:T(128)S(6)} %select_n.122), kind=kOutput, calls=%fused_computation.37.clone.1 | convolution fusion | flops 402784256 | bytes 3670020 | tf_op jit(solution)/shard_map/while/body/dot_general | solution.py:100
  193.0 2.4 scatter_fusion.1
  196.1 37.6 %all_to_all.32 = f32[16,256,128]{2,1,0:T(8,128)S(1)} all-to-all(f32[16,256,128]{2,1,0:T(8,128)} %bitcast.209), channel_id=1, replica_groups=mesh['sub_0'=4,'sub_1'=4,'rep'=8] {'sub_0','sub_1'}, dimensions={0} | all-to-all | bytes 4194304 | tf_op jit(solution)/shard_map/all_to_all | solution.py:38
  234.0 18.5 %all_to_all.33 = f32[8,256,128]{2,1,0:T(8,128)S(1)} all-to-all(f32[8,256,128]{2,1,0:T(8,128)S(1)} %broadcast_in_dim.20), channel_id=1, replica_groups=mesh['sub_0'=4,'sub_1'=4,'rep'=8] {'rep'}, dimensions={0} | all-to-all | bytes 2097152 | tf_op jit(solution)/shard_map/all_to_all | solution.py:23
  253.1 8.8 %psum.30 = f32[3,128]{1,0:T(4,128)S(1)} all-reduce(f32[3,128]{1,0:T(4,128)S(1)} %pad_maximum_fusion.2), channel_id=1, replica_groups=mesh['sub_0'=4,'sub_1'=4,'rep'=8] {'sub_0'}, use_global_device_ids=true, to_apply=%region_18.19 | all-reduce | flops 384 | bytes 3072 | tf_op jit(solution)/shard_map/psum | solution.py:69
  262.0 8.3 %psum.31 = f32[3,128]{1,0:T(4,128)S(1)} all-reduce(f32[3,128]{1,0:T(4,128)S(1)} %psum.30), channel_id=1, replica_groups=mesh['sub_0'=4,'sub_1'=4,'rep'=8] {'sub_1'}, use_global_device_ids=true, to_apply=%region_19.20 | all-reduce | flops 384 | bytes 3072 | tf_op jit(solution)/shard_map/psum | solution.py:69
  (83 shorter events, 18.5 us)
Async XLA Ops:
  0.0 33.9 %copy-start = (bf16[256,512]{1,0:T(8,128)(2,1)S(1)}, bf16[256,512]{1,0:T(8,128)(2,1)}, u32[]{:S(2)}) copy-start(bf16[256,512]{1,0:T(8,128)(2,1)} %param.14) | copy-start | bytes 786436
  1.1 35.0 %copy-start.1 = (f32[256,128]{0,1:T(8,128)}, f32[256,128]{0,1:T(8,128)S(1)}, u32[]{:S(2)}) copy-start(f32[256,128]{0,1:T(8,128)S(1)} %copy.35) | copy-start | bytes 393220
  23.2 4.5 %copy-start.15 = (f32[128]{0:T(128)}, f32[128]{0:T(128)S(1)}, u32[]{:S(2)}) copy-start(f32[128]{0:T(128)S(1)} %reduce_sum.112) | copy-start | bytes 1540
  23.2 108.9 %copy-start.12 = (f32[128]{0:T(128)}, f32[128]{0:T(128)S(1)}, u32[]{:S(2)}) copy-start(f32[128]{0:T(128)S(1)} %sqrt.32) | copy-start | bytes 1540
  23.3 4.3 %collective-permute-start.1 = (bf16[256,128]{0,1:T(8,128)(2,1)S(1)}, bf16[256,128]{0,1:T(8,128)(2,1)S(1)}, u32[]{:S(2)}, u32[]{:S(2)}) collective-permute-start(bf16[256,128]{0,1:T(8,128)(2,1)S(1)} %fusion.78), channel_id=1, source_target_pairs={{8,0},{16,8},{24,16},{32,24},{40,32},{48,40},{56,48},{64,56},{72,6... | collective-permute-start | bytes 196616 | tf_op jit(solution)/shard_map/ppermute | solution.py:56
  25.4 7.6 %collective-permute-start = (bf16[256,128]{0,1:T(8,128)(2,1)S(1)}, bf16[256,128]{0,1:T(8,128)(2,1)S(1)}, u32[]{:S(2)}, u32[]{:S(2)}) collective-permute-start(bf16[256,128]{0,1:T(8,128)(2,1)S(1)} %fusion.78), channel_id=1, source_target_pairs={{0,8},{8,16},{16,24},{24,32},{32,40},{40,48},{48,56},{56,64},{64,7... | collective-permute-start | bytes 196616 | tf_op jit(solution)/shard_map/ppermute | solution.py:54
  34.8 5.7 %copy-start.11 = (bf16[256,128]{0,1:T(8,128)(2,1)}, bf16[256,128]{0,1:T(8,128)(2,1)S(1)}, u32[]{:S(2)}) copy-start(bf16[256,128]{0,1:T(8,128)(2,1)S(1)} %get-tuple-element.176) | copy-start | bytes 196612
  36.1 17.3 %all-to-all-start = ((bf16[16,256,128]{2,1,0:T(8,128)(2,1)}), bf16[16,256,128]{2,1,0:T(8,128)(2,1)}, u32[]{:S(2)}, u32[]{:S(2)}) async-start(bf16[16,256,128]{2,1,0:T(8,128)(2,1)} %broadcast_in_dim.14), calls=%async_computation | async-start | bytes 2097152 | tf_op jit(solution)/shard_map/all_to_all | solution.py:23
  107.9 24.3 %copy-start.2 = (f32[256,128]{0,1:T(8,128)S(1)}, f32[256,128]{0,1:T(8,128)}, u32[]{:S(2)}) copy-start(f32[256,128]{0,1:T(8,128)} %copy-done.1) | copy-start | bytes 393220
  150.1 13.3 %copy-start.13 = (f32[1,128]{1,0:T(1,128)}, f32[1,128]{1,0:T(1,128)S(1)}, u32[]{:S(2)}) copy-start(f32[1,128]{1,0:T(1,128)S(1)} %get-tuple-element.175) | copy-start | bytes 1540
  150.9 12.5 %copy-start.3 = (f32[256,128]{0,1:T(8,128)}, f32[256,128]{0,1:T(8,128)S(1)}, u32[]{:S(2)}) copy-start(f32[256,128]{0,1:T(8,128)S(1)} %get-tuple-element.172) | copy-start | bytes 393220
  150.9 4.3 %collective-permute-start.3 = (bf16[256,128]{0,1:T(8,128)(2,1)S(1)}, bf16[256,128]{0,1:T(8,128)(2,1)S(1)}, u32[]{:S(2)}, u32[]{:S(2)}) collective-permute-start(bf16[256,128]{0,1:T(8,128)(2,1)S(1)} %get-tuple-element.171), channel_id=1, source_target_pairs={{8,0},{16,8},{24,16},{32,24},{40,32},{48,40},{56,48},{64,56},{72,6... | collective-permute-start | bytes 196616 | tf_op jit(solution)/shard_map/ppermute | solution.py:56
  152.7 7.6 %collective-permute-start.2 = (bf16[256,128]{0,1:T(8,128)(2,1)S(1)}, bf16[256,128]{0,1:T(8,128)(2,1)S(1)}, u32[]{:S(2)}, u32[]{:S(2)}) collective-permute-start(bf16[256,128]{0,1:T(8,128)(2,1)S(1)} %get-tuple-element.171), channel_id=1, source_target_pairs={{0,8},{8,16},{16,24},{24,32},{32,40},{40,48},{48,56},{56,64},{64,7... | collective-permute-start | bytes 196616 | tf_op jit(solution)/shard_map/ppermute | solution.py:54
  162.0 20.2 %copy-start.6 = (bf16[256,128]{0,1:T(8,128)(2,1)}, bf16[256,128]{0,1:T(8,128)(2,1)S(1)}, u32[]{:S(2)}) copy-start(bf16[256,128]{0,1:T(8,128)(2,1)S(1)} %get-tuple-element.178) | copy-start | bytes 196612
  163.3 17.3 %all-to-all-start.3 = ((bf16[16,256,128]{2,1,0:T(8,128)(2,1)}), bf16[16,256,128]{2,1,0:T(8,128)(2,1)}, u32[]{:S(2)}, u32[]{:S(2)}) async-start(bf16[16,256,128]{2,1,0:T(8,128)(2,1)} %broadcast_in_dim.19), calls=%async_computation.3 | async-start | bytes 2097152 | tf_op jit(solution)/shard_map/all_to_all | solution.py:23
  233.8 18.9 %copy-start.5 = (f32[256,128]{0,1:T(8,128)S(1)}, f32[256,128]{0,1:T(8,128)}, u32[]{:S(2)}) copy-start(f32[256,128]{0,1:T(8,128)} %get-tuple-element.179) | copy-start | bytes 393220
  233.8 18.9 %copy-start.7 = (bf16[256,128]{0,1:T(8,128)(2,1)S(1)}, bf16[256,128]{0,1:T(8,128)(2,1)}, u32[]{:S(2)}) copy-start(bf16[256,128]{0,1:T(8,128)(2,1)} %copy-done.6) | copy-start | bytes 196612
  233.8 18.9 %copy-start.10 = (bf16[256,256]{1,0:T(8,128)(2,1)S(1)}, bf16[256,256]{1,0:T(8,128)(2,1)}, u32[]{:S(2)}) copy-start(bf16[256,256]{1,0:T(8,128)(2,1)} %param.13) | copy-start | bytes 393220
  233.9 19.1 %copy-start.4 = (f32[256,128]{0,1:T(8,128)S(1)}, f32[256,128]{0,1:T(8,128)}, u32[]{:S(2)}) copy-start(f32[256,128]{0,1:T(8,128)} %copy-done.3) | copy-start | bytes 393220
  233.9 19.1 %copy-start.8 = (f32[1,256,128]{1,2,0:T(8,128)S(1)}, f32[1,256,128]{1,2,0:T(8,128)}, u32[]{:S(2)}) copy-start(f32[1,256,128]{1,2,0:T(8,128)} %get-tuple-element.173) | copy-start | bytes 393220
  233.9 36.4 %copy-start.14 = (f32[1,128]{1,0:T(1,128)S(1)}, f32[1,128]{1,0:T(1,128)}, u32[]{:S(2)}) copy-start(f32[1,128]{1,0:T(1,128)} %copy-done.13) | copy-start | bytes 1540
  233.9 36.4 %copy-start.16 = (f32[128]{0:T(128)S(1)}, f32[128]{0:T(128)}, u32[]{:S(2)}) copy-start(f32[128]{0:T(128)} %copy-done.15) | copy-start | bytes 1540
  233.9 36.4 %copy-start.9 = (f32[256,128]{0,1:T(8,128)S(1)}, f32[256,128]{0,1:T(8,128)}, u32[]{:S(2)}) copy-start(f32[256,128]{0,1:T(8,128)} %get-tuple-element.177) | copy-start | bytes 393220
where the time goes:
time: 274 us; the launch traced here: 271 us
  blocking collectives  170 us (62%)
  waiting for transfers between devices  37 us (14%)
  matrix products  18.4 us (7%)
  local copies, waits for them, and re-layouts  17.3 us (6%)
  starting transfers between devices  12.9 us (5%)
  other arithmetic  12.5 us (5%)
    all_to_all x2, blocking collectives, sum_at_owner(): lax.all_to_all(blocks, axis, split_axis=0, concat_axis=0, tiled=True)  74.8 us
    all_to_all x2, blocking collectives, from_everyone(): return lax.all_to_all(copies, axis, split_axis=0, concat_axis=0, tiled=True)  39.9 us
    psum x4, blocking collectives, by_axis(): return functools.reduce(lax.psum, axes, array)  34.4 us
    all_to_all x2, waiting for transfers between devices, from_everyone(): return lax.all_to_all(copies, axis, split_axis=0, concat_axis=0, tiled=True)  22.8 us
    all_gather x1, blocking collectives, gathered_total(): blocks = lax.all_gather(array, axis)  21.1 us
    ppermute x2, waiting for transfers between devices, padded_2(): lax.ppermute(tail, axis, [(i, (i + 1) % count) for i in range(count)])  10.4 us
    all_to_all x2, starting transfers between devices, from_everyone(): return lax.all_to_all(copies, axis, split_axis=0, concat_axis=0, tiled=True)  8.67 us
    dot_general x2, matrix products, slot_step(): jnp.dot(factor, first, preferred_element_type=jnp.float32)  7.64 us
  transfers between devices with their start and end apart: 6, of which 6 were waited for; matrix products, arithmetic and copies ran while one was open for 1% of the time, Pallas kernels for 0%

commit v1 on v0

v1 whole, which is shorter than its diff:
```python
import jax
import jax.numpy as jnp
from jax import lax
from jax.experimental import pallas as pl
from jax.experimental.pallas import tpu as pltpu
from jax.sharding import Mesh
from jax.sharding import PartitionSpec as P

BI = 128
ROWS = 256
COLS = 128
HALF = 64
PART = 16
GROUPS = 16
BLOCKS = 32
SUB = ("x", "y")
XYZ = ("x", "y", "z")
ALL = ("x", "y", "z", "c")
F32 = jnp.float32
BF16 = jnp.bfloat16
SHRINK = 2.0**-31
VMEM = pl.BlockSpec(memory_space=pltpu.VMEM)
SMEM = pl.BlockSpec(memory_space=pltpu.SMEM)
ANY = pl.BlockSpec(memory_space=pl.ANY)
NT = (((1,), (1,)), ((), ()))
NN = (((1,), (0,)), ((), ()))


def dot(left, right, dims=NN):
    return lax.dot_general(left, right, dims, preferred_element_type=F32)


def call(body, name, outs, specs, scratch=(), flops=0, moved=1 << 20):
    return pl.pallas_call(
        body,
        name=name,
        out_shape=outs,
        in_specs=specs,
        out_specs=[VMEM] * len(outs),
        scratch_shapes=list(scratch),
        cost_estimate=pl.CostEstimate(flops=flops, bytes_accessed=moved, transcendentals=0),
        compiler_params=pltpu.CompilerParams(vmem_limit_bytes=40 << 20),
    )


def out(shape, dtype):
    return jax.ShapeDtypeStruct(shape, dtype)


def opening(rhs, halo, sent):
    field = rhs[...]
    sums = jnp.sum(field * field, axis=0, keepdims=True)
    row = lax.broadcasted_iota(jnp.int32, (8, COLS), 0)
    left = (halo[0, 0] & 1).astype(F32)
    right = (halo[0, 1] & 1).astype(F32)
    tile = jnp.where(row == 0, sums, jnp.where(row == 1, left, jnp.where(row == 2, right, 0.0)))
    sent[...] = jnp.broadcast_to(tile[None], sent.shape)


def first_direction(
    pos, halo, rhs, before, after, facts, precond, diag, sent, z_nat, base, basis, turned
):
    beta = jnp.sqrt(jnp.sum(facts[:, 0:1, :], axis=0))
    v = rhs[...] / beta
    left = before[pl.ds(pl.multiple_of((halo[0, 0] & 1) * BI, BI), BI), :] / beta
    right = after[pl.ds(pl.multiple_of((halo[0, 1] & 1) * BI, BI), BI), :] / beta
    patch = jnp.concatenate([v, left, right], axis=0).astype(BF16)
    z = v + dot(precond[...], patch)
    z_nat[...] = z
    half = pl.ds(pl.multiple_of(pos[2] * HALF, HALF), HALF)
    part = pl.ds(pl.multiple_of(pos[2] * HALF + pos[1] * PART, PART), PART)
    turned[...] = z.T
    mine = turned[half, :].astype(BF16)
    sent[...] = jnp.broadcast_to(mine[None], sent.shape)
    turned[...] = (3.0 * z + dot(diag[...], z.astype(BF16))).T
    base[...] = turned[part, :]
    turned[...] = v.T
    basis[...] = turned[part, :]


def slots(
    ids, counts, near, far, couplings, factors, kept, given, coup, fact, picked, one, two, sems
):
    live = counts[0]

    def fetch(slot):
        return (
            pltpu.make_async_copy(couplings.at[slot], coup.at[slot], sems.at[slot, 0]),
            pltpu.make_async_copy(factors.at[slot], fact.at[slot], sems.at[slot, 1]),
        )

    for copy in fetch(0):
        copy.start()

    @pl.when(live > 1)
    def _():
        for copy in fetch(1):
            copy.start()

    @pl.when(live < 2)
    def _():
        kept[4:8] = jnp.zeros((4, HALF, BI), F32)
        given[4:8] = jnp.zeros((4, HALF, BI), F32)

    def step(slot, carry):
        for j in range(4):
            block = ids[slot, j]
            lanes = pl.ds(pl.multiple_of((block & 1) * BI, BI), BI)
            picked[0:HALF, j * BI : (j + 1) * BI] = near[block >> 1, :, lanes]
            picked[HALF:COLS, j * BI : (j + 1) * BI] = far[block >> 1, :, lanes]
        get_coup, get_fact = fetch(slot)
        get_coup.wait()
        for n in range(4):
            span = slice(n * 256, (n + 1) * 256)
            one[:, span] = dot(picked[...], coup[slot, span, :], NT).astype(BF16)
        get_fact.wait()
        for n in range(4):
            span = slice(n * 256, (n + 1) * 256)
            two[:, span] = dot(one[...], fact[slot, span, :], NT).astype(BF16)
        for n in range(4):
            span = slice(n * 256, (n + 1) * 256)
            one[:, span] = dot(two[...], fact[slot, :, span]).astype(BF16)
        for n in range(2):
            piece = dot(one[...], coup[slot, :, n * 256 : (n + 1) * 256])
            for m in range(2):
                lanes = slice(m * BI, (m + 1) * BI)
                kept[slot * 4 + n * 2 + m] = piece[0:HALF, lanes]
                given[slot * 4 + n * 2 + m] = piece[HALF:COLS, lanes]
        return carry

    lax.fori_loop(0, live, step, 0)


def parcels(ids, ids_far, kept, got, facts, sent, total):
    total[...] = jnp.zeros_like(total)
    for i in range(8):
        block = ids[i // 4, i % 4]
        total[block] = total[block] + kept[i]
    for i in range(8):
        block = ids_far[i // 4, i % 4]
        total[block] = total[block] + got[i]
    with_halo = sent.shape[2] > ROWS

    def group(d, carry):
        lower = 2 * ((d + GROUPS - 1) % GROUPS)
        upper = 2 * ((d + 1) % GROUPS)
        blocks = [total[2 * d], total[2 * d + 1]]
        if with_halo:
            left = facts[d, 1:2, :] > 0.5
            right = facts[d, 2:3, :] > 0.5
            blocks.append(jnp.where(left, total[lower + 1], total[lower]))
            blocks.append(jnp.where(right, total[upper + 1], total[upper]))
        for j, block in enumerate(blocks):
            low = block.astype(BF16)
            for z in range(4):
                sent[d * 4 + z, :, j * BI : (j + 1) * BI] = low[z * PART : (z + 1) * PART]
        return carry

    lax.fori_loop(0, GROUPS, group, 0)


def summed(arrived):
    def add(i, total):
        for j in range(8):
            total = total + arrived[i * 8 + j].astype(F32)
        return total

    return lax.fori_loop(0, 8, add, jnp.zeros(arrived.shape[1:], F32))


def second_direction(halo, arrived, base, before, after, precond, diag, sent, base_two, w):
    coupled = summed(arrived)
    left = before[:, pl.ds(pl.multiple_of((halo[0, 0] & 1) * BI, BI), BI)]
    right = after[:, pl.ds(pl.multiple_of((halo[0, 1] & 1) * BI, BI), BI)]
    image = base[...] - coupled[:, :ROWS]
    patch = jnp.concatenate(
        [
            image,
            left - coupled[:, ROWS : ROWS + BI],
            right - coupled[:, ROWS + BI :],
        ],
        axis=1,
    ).astype(BF16)
    z = image + dot(patch, precond[...], NT)
    low = z.astype(BF16)
    w[...] = image
    base_two[...] = 3.0 * z + dot(low, diag[...], NT)
    sent[...] = jnp.broadcast_to(low[None], sent.shape)


def products(pos, arrived, base, w, basis, sent):
    image = (base[...] - summed(arrived)) * SHRINK
    one = w[...]
    v = basis[...]
    lane = lax.broadcasted_iota(jnp.int32, (PART, COLS), 1)
    row = lax.broadcasted_iota(jnp.int32, (PART, COLS), 0)
    here = lane == row + (pos[2] * HALF + pos[1] * PART)
    rank = lax.broadcasted_iota(jnp.int32, (8, COLS), 0)
    tile = jnp.zeros((8, COLS), F32)
    pairs = [(v, one), (one, one), (v, image), (one, image), (image, image)]
    for k, (left, right) in enumerate(pairs):
        value = jnp.sum(left * right, axis=1, keepdims=True)
        spread = jnp.sum(jnp.where(here, value, 0.0), axis=0, keepdims=True)
        tile = jnp.where(rank == k, spread, tile)
    sent[...] = jnp.broadcast_to(tile[None], sent.shape)


def closing(pos, near, far, facts, z_one, z_near, z_far, answer):
    sums = jnp.sum(near[...], axis=0) + jnp.sum(far[...], axis=0)
    beta = jnp.sqrt(jnp.sum(facts[:, 0:1, :], axis=0))
    h11, ww, vx, wx, xx = (sums[k : k + 1] for k in range(5))
    h21 = jnp.sqrt(ww - h11 * h11)
    small = SHRINK * h11
    h12 = (vx - small * h11) / (SHRINK * h21)
    h22 = ((wx - h11 * vx) - small * ww + small * h11 * h11) / (SHRINK * h21) / h21
    scaled = SHRINK * h21
    norm = ((xx - 2.0 * small * wx) + small * small * ww) / scaled / scaled
    low_square = norm - h12 * h12 - h22 * h22
    rho = jnp.sqrt(h11 * h11 + h21 * h21)
    cosine = h11 / rho
    sine = h21 / rho
    top = cosine * h12 + sine * h22
    low = cosine * h22 - sine * h12
    y2 = -low * sine * beta / (low * low + low_square)
    y1 = (cosine * beta - top * y2) / rho
    second = y2 / h21
    first = y1 - second * h11
    a = z_near[0].astype(F32)
    b = z_far[0].astype(F32)
    swap = pos[2] == 1
    stacked = jnp.concatenate([jnp.where(swap, b, a), jnp.where(swap, a, b)], axis=0)
    answer[...] = first * z_one[...] + second * stacked.T


def other_core(array):
    return lax.ppermute(array, "c", [(0, 1), (1, 0)])


def swap_all(array, axes):
    return lax.all_to_all(array, axes, split_axis=0, concat_axis=0, tiled=True)


def neighbours(array):
    forward = lax.ppermute(array, SUB, [(i, (i + 1) % GROUPS) for i in range(GROUPS)])
    backward = lax.ppermute(array, SUB, [((i + 1) % GROUPS, i) for i in range(GROUPS)])
    return forward, backward


def on_device(rhs, schur_diag, precond, halo_ids, factors, couplings, block_ids, counts):
    group = lax.axis_index(SUB)
    pos = jnp.stack([group, lax.axis_index("z"), lax.axis_index("c")]).astype(jnp.int32)
    ids_far = other_core(block_ids)

    def apply_slots(near, far):
        return call(
            slots,
            "slots",
            [out((8, HALF, BI), F32), out((8, HALF, BI), F32)],
            [SMEM, SMEM, VMEM, VMEM, ANY, ANY],
            [
                pltpu.VMEM((2, 1024, 512), BF16),
                pltpu.VMEM((2, 1024, 1024), BF16),
                pltpu.VMEM((COLS, 512), BF16),
                pltpu.VMEM((COLS, 1024), BF16),
                pltpu.VMEM((COLS, 1024), BF16),
                pltpu.SemaphoreType.DMA((2, 2)),
            ],
            flops=2 * 805306368,
            moved=8 << 20,
        )(block_ids, counts, near, far, couplings, factors)

    def to_owners(kept, given, width):
        got = other_core(given)
        (sent,) = call(
            parcels,
            "parcels",
            [out((64, PART, width), BF16)],
            [SMEM, SMEM, VMEM, VMEM, VMEM],
            [pltpu.VMEM((BLOCKS, HALF, BI), F32)],
        )(block_ids, ids_far, kept, got, facts)
        return swap_all(sent, XYZ)

    before, after = neighbours(rhs)
    (opened,) = call(opening, "opening", [out((GROUPS, 8, COLS), F32)], [VMEM, SMEM])(
        rhs, halo_ids
    )
    facts = swap_all(opened, SUB)
    sent, z_one, base, basis = call(
        first_direction,
        "first_direction",
        [
            out((GROUPS, HALF, ROWS), BF16),
            out((ROWS, COLS), F32),
            out((PART, ROWS), F32),
            out((PART, ROWS), F32),
        ],
        [SMEM, SMEM, VMEM, VMEM, VMEM, VMEM, VMEM, VMEM],
        [pltpu.VMEM((COLS, ROWS), F32)],
        flops=1 << 26,
    )(pos, halo_ids, rhs, before, after, facts, precond, schur_diag)
    base_before, base_after = neighbours(base)
    near = swap_all(sent, SUB)
    far = other_core(near)
    kept, given = apply_slots(near, far)
    arrived = to_owners(kept, given, 2 * ROWS)
    sent, base, w = call(
        second_direction,
        "second_direction",
        [out((64, PART, ROWS), BF16), out((PART, ROWS), F32), out((PART, ROWS), F32)],
        [SMEM, VMEM, VMEM, VMEM, VMEM, VMEM, VMEM],
        flops=1 << 26,
    )(halo_ids, arrived, base, base_before, base_after, precond, schur_diag)
    near = swap_all(sent, XYZ).reshape(GROUPS, HALF, ROWS)
    far = other_core(near)
    kept, given = apply_slots(near, far)
    arrived = to_owners(kept, given, ROWS)
    (sent,) = call(
        products, "products", [out((64, 8, COLS), F32)], [SMEM, VMEM, VMEM, VMEM, VMEM]
    )(pos, arrived, base, w, basis)
    sums = swap_all(sent, XYZ)
    sums_far = other_core(sums)
    own = [lax.dynamic_slice_in_dim(half, group, 1, 0) for half in (near, far)]
    (answer,) = call(
        closing, "closing", [out((ROWS, COLS), F32)], [SMEM] + [VMEM] * 6
    )(pos, sums, sums_far, facts, z_one, *own)
    return answer


def solution(mesh):
    torus = Mesh(mesh.devices.reshape(4, 4, 4, 2), ALL)
    placed = (
        P(SUB, None),
        P(SUB, None),
        P(SUB, None),
        P(SUB, None),
        P(ALL, None, None),
        P(ALL, None, None),
        P(ALL, None),
        P(ALL),
    )
    return jax.shard_map(
        on_device, mesh=torus, in_specs=placed, out_specs=P(SUB, None), check_vma=False
    )
```

time: 274 us -> 147 us (0.54)
  blocking collectives: 170 us -> 63.2 us
  matrix products: 18.4 us -> 0 us
  Pallas kernels: 0 us -> 17.5 us
  other arithmetic: 12.5 us -> 0.08 us
  starting transfers between devices: 12.9 us -> 23.1 us
  waiting for transfers between devices: 37 us -> 28.3 us
  local copies, waits for them, and re-layouts: 17.3 us -> 12.6 us
    all_to_all x4, blocking collectives: 115 us -> 63.2 us  [swap_all(): return lax.all_to_all(array, axes, split_axis=0, concat_axis=0, tiled=True)]
    psum x4 -> x0, blocking collectives: 34.4 us -> none  [by_axis(): return functools.reduce(lax.psum, axes, array)]
    all_gather x1 -> x0, blocking collectives: 21.1 us -> none  [gathered_total(): blocks = lax.all_gather(array, axis)]
    dot_general x8 -> x0, matrix products: 18.4 us -> none  [the longest x2 7.64 us: slot_step(): jnp.dot(factor, first, preferred_element_type=jnp.float32)]
    pallas_call x0 -> x9, Pallas kernels: none -> 17.5 us  [the longest x2 9.19 us: apply_slots(): call(slots, 'slots', [out((8, HALF, BI), F32), out((8, HALF, BI), F32)],...]
    all_to_all x2, waiting for transfers between devices: 22.8 us -> 9.64 us  [swap_all(): return lax.all_to_all(array, axes, split_axis=0, concat_axis=0, tiled=True)]
    unnamed x35 -> x34, local copies, waits for them, and re-layouts: 1.11 us -> 12.6 us
    ppermute x4 -> x10, starting transfers between devices: 4.21 us -> 11.4 us  [the longest x2 7.43 us: neighbours(): lax.ppermute(array, SUB, [((i + 1) % GROUPS, i) for i in range(GROUPS)])]
  transfers between devices with their start and end apart: 6 -> 12, of which waited for: 6 -> 8; matrix products, arithmetic and copies ran while one was open for 1% -> 0% of each run, Pallas kernels for 0% -> 1%
where the time goes in v1:
time: 147 us; the launch traced here: 146 us
  blocking collectives  63.2 us (43%)
  waiting for transfers between devices  28.3 us (19%)
  starting transfers between devices  23.1 us (16%)
  Pallas kernels  17.5 us (12%)
  local copies, waits for them, and re-layouts  12.6 us (9%)
    all_to_all x4, blocking collectives, swap_all(): return lax.all_to_all(array, axes, split_axis=0, concat_axis=0, tiled=True)  63.2 us
    unnamed x34, local copies, waits for them, and re-layouts  12.6 us
    all_to_all x2, starting transfers between devices, swap_all(): return lax.all_to_all(array, axes, split_axis=0, concat_axis=0, tiled=True)  11.7 us
    ppermute x2, waiting for transfers between devices, neighbours(): lax.ppermute(array, SUB, [(i, (i + 1) % GROUPS) for i in range(GROUPS)])  11.4 us
    all_to_all x2, waiting for transfers between devices, swap_all(): return lax.all_to_all(array, axes, split_axis=0, concat_axis=0, tiled=True)  9.64 us
    pallas_call x2, Pallas kernels, apply_slots(): call(slots, 'slots', [out((8, HALF, BI), F32), out((8, HALF, BI), F32)],...  9.19 us
    ppermute x2, starting transfers between devices, neighbours(): lax.ppermute(array, SUB, [((i + 1) % GROUPS, i) for i in range(GROUPS)])  7.43 us
    ppermute x6, waiting for transfers between devices, other_core(): return lax.ppermute(array, 'c', [(0, 1), (1, 0)])  7.23 us
  transfers between devices with their start and end apart: 12, of which 8 were waited for; matrix products, arithmetic and copies ran while one was open for 0% of the time, Pallas kernels for 1%

profile of v1, /device:TPU:0, one launch (start us, length us, event | category | flops | bytes accessed | tf_op | source)
XLA Modules:
  0.0 145.6 jit_solution(17666811920486234073)
XLA Ops:
  0.0 1.7 %collective-permute-start.1 = (f32[256,128]{1,0:T(8,128)}, f32[256,128]{1,0:T(8,128)S(1)}, u32[]{:S(2)}, u32[]{:S(2)}) collective-permute-start(f32[256,128]{1,0:T(8,128)} %rhs.3), channel_id=1, source_target_pairs={{0,8},{8,16},{16,24},{24,32},{32,40},{40,48},{48,56},{56,64},{64,7... | collective-permute-start | bytes 393224 | tf_op jit(solution)/shard_map/ppermute | solution.py:244
  1.7 3.7 %collective-permute-start.2 = (f32[256,128]{1,0:T(8,128)}, f32[256,128]{1,0:T(8,128)S(1)}, u32[]{:S(2)}, u32[]{:S(2)}) collective-permute-start(f32[256,128]{1,0:T(8,128)} %rhs.3), channel_id=1, source_target_pairs={{8,0},{16,8},{24,16},{32,24},{40,32},{48,40},{56,48},{64,56},{72,6... | collective-permute-start | bytes 393224 | tf_op jit(solution)/shard_map/ppermute | solution.py:245
  5.3 0.9 copy-done.6
  6.9 1.2 opening.1
  8.2 3.8 %all-to-all-start = ((f32[16,8,128]{2,1,0:T(8,128)}), f32[16,8,128]{2,1,0:T(8,128)S(1)}, u32[]{:S(2)}, u32[]{:S(2)}) async-start(f32[16,8,128]{2,1,0:T(8,128)} %opening.1), calls=%async_computation | async-start | bytes 131072 | tf_op jit(solution)/shard_map/all_to_all | solution.py:240
  12.1 7.6 %all-to-all-done.facts = f32[16,8,128]{2,1,0:T(8,128)S(1)} async-done(((f32[16,8,128]{2,1,0:T(8,128)}), f32[16,8,128]{2,1,0:T(8,128)S(1)}, u32[]{:S(2)}, u32[]{:S(2)}) %all-to-all-start) | async-done | bytes 65568 | tf_op jit(solution)/shard_map/all_to_all | solution.py:240
  19.7 0.9 copy-done.4
  20.6 0.9 copy-done.7
  23.1 1.1 first_direction.1
  24.2 13.3 %all_to_all.30.near = bf16[16,64,256]{2,1,0:T(8,128)(2,1)S(1)} all-to-all(bf16[16,64,256]{2,1,0:T(8,128)(2,1)S(1)} %get-tuple-element.16), channel_id=1, replica_groups=mesh['x'=4,'y'=4,'z'=4,'c'=2] {'x','y'}, dimensions={0} | all-to-all | bytes 1048576 | tf_op jit(solution)/shard_map/all_to_all | solution.py:240
  38.2 1.2 collective-permute-done.3.far
  39.5 2.2 %copy-done = bf16[2,1024,1024]{2,1,0:T(8,128)(2,1)S(1)} copy-done((bf16[2,1024,1024]{2,1,0:T(8,128)(2,1)S(1)}, bf16[2,1024,1024]{2,1,0:T(8,128)(2,1)}, u32[]{:S(2)}) %copy-start) | copy-done | bytes 4194328
  41.6 1.6 %copy-done.2 = bf16[2,1024,512]{2,1,0:T(8,128)(2,1)S(1)} copy-done((bf16[2,1024,512]{2,1,0:T(8,128)(2,1)S(1)}, bf16[2,1024,512]{2,1,0:T(8,128)(2,1)}, u32[]{:S(2)}) %copy-start.2) | copy-done | bytes 2097176
  43.9 4.6 %slots.2 = (f32[8,64,128]{2,1,0:T(8,128)S(1)}, f32[8,64,128]{2,1,0:T(8,128)S(1)}) custom-call(s32[2,4]{1,0:T(2,128)S(1)} %copy-done.12, s32[1]{0:T(128)S(6)} %copy.9.counts, bf16[16,64,256]{2,1,0:T(8,128)(2,1)S(1)} %all_to_all.30.near, bf16[16,64,256]{2,1,0:T(8,128)(2,1)S(1)} %collective-permute-done.3.far, bf16[2,1024,512]{2,1,0:T(8,128)(2,1)S(1)} %copy-done.2, ...), custom_call_target="tpu_custom_call" | custom-call | flops 1610612736 | bytes 8388608 | tf_op jit(solution)/shard_map/slots/pallas_call | solution.py:255
  49.1 1.0 collective-permute-done.ids_far
  50.2 2.0 %parcels.2 = bf16[64,16,512]{2,1,0:T(8,128)(2,1)} custom-call(s32[2,4]{1,0:T(2,128)S(1)} %copy-done.12, s32[2,4]{1,0:T(2,128)S(1)} %collective-permute-done.ids_far, f32[8,64,128]{2,1,0:T(8,128)S(1)} %get-tuple-element.17.kept, f32[8,64,128]{2,1,0:T(8,128)S(1)} %collective-permute-done.4.got, f32[16,8,128]{2,1,0:T(8,128)S(1)} %all-to-all-done.facts), custom_call_target="tpu_custom_call" | custom-call | bytes 1048576 | tf_op jit(solution)/shard_map/parcels/pallas_call | solution.py:274
  52.1 7.8 %all-to-all-start.2 = ((bf16[64,16,512]{2,1,0:T(8,128)(2,1)}), bf16[64,16,512]{2,1,0:T(8,128)(2,1)S(1)}, u32[]{:S(2)}, u32[]{:S(2)}) async-start(bf16[64,16,512]{2,1,0:T(8,128)(2,1)} %parcels.2), calls=%async_computation.2 | async-start | bytes 2097152 | tf_op jit(solution)/shard_map/all_to_all | solution.py:240
  60.0 1.6 %collective-permute-start.5 = (f32[16,256]{1,0:T(8,128)S(1)}, f32[16,256]{1,0:T(8,128)S(1)}, u32[]{:S(2)}, u32[]{:S(2)}) collective-permute-start(f32[16,256]{1,0:T(8,128)S(1)} %get-tuple-element.19.base), channel_id=1, source_target_pairs={{0,8},{8,16},{16,24},{24,32},{32,40},{40,48},{48,56},{56,64},{64,7... | collective-permute-start | bytes 49160 | tf_op jit(solution)/shard_map/ppermute | solution.py:244
  61.6 3.8 %collective-permute-start.6 = (f32[16,256]{1,0:T(8,128)S(1)}, f32[16,256]{1,0:T(8,128)S(1)}, u32[]{:S(2)}, u32[]{:S(2)}) collective-permute-start(f32[16,256]{1,0:T(8,128)S(1)} %get-tuple-element.19.base), channel_id=1, source_target_pairs={{8,0},{16,8},{24,16},{32,24},{40,32},{48,40},{56,48},{64,56},{72,6... | collective-permute-start | bytes 49160 | tf_op jit(solution)/shard_map/ppermute | solution.py:245
  65.4 11.4 %collective-permute-done.5.before = f32[16,256]{1,0:T(8,128)S(1)} collective-permute-done((f32[16,256]{1,0:T(8,128)S(1)}, f32[16,256]{1,0:T(8,128)S(1)}, u32[]{:S(2)}, u32[]{:S(2)}) %collective-permute-start.5) | collective-permute-done | bytes 16416 | tf_op jit(solution)/shard_map/ppermute | solution.py:244
  76.8 2.1 %all-to-all-done.2.arrived = bf16[64,16,512]{2,1,0:T(8,128)(2,1)S(1)} async-done(((bf16[64,16,512]{2,1,0:T(8,128)(2,1)}), bf16[64,16,512]{2,1,0:T(8,128)(2,1)S(1)}, u32[]{:S(2)}, u32[]{:S(2)}) %all-to-all-start.2) | async-done | bytes 1048608 | tf_op jit(solution)/shard_map/all_to_all | solution.py:240
  78.9 0.9 copy-done.9
  79.8 1.1 second_direction.1
  80.9 16.9 %all_to_all.31 = bf16[64,16,256]{2,1,0:T(8,128)(2,1)S(1)} all-to-all(bf16[64,16,256]{2,1,0:T(8,128)(2,1)S(1)} %get-tuple-element.20), channel_id=1, replica_groups=mesh['x'=4,'y'=4,'z'=4,'c'=2] {'x','y','z'}, dimensions={0} | all-to-all | bytes 1048576 | tf_op jit(solution)/shard_map/all_to_all | solution.py:240
  97.8 1.9 %collective-permute-done.7.far = bf16[16,64,256]{2,1,0:T(8,128)(2,1)S(1)} collective-permute-done((bf16[16,64,256]{2,1,0:T(8,128)(2,1)S(1)}, bf16[16,64,256]{2,1,0:T(8,128)(2,1)S(1)}, u32[]{:S(2)}, u32[]{:S(2)}) %collective-permute-start.7) | collective-permute-done | bytes 524320 | tf_op jit(solution)/shard_map/ppermute | solution.py:236
  99.7 2.2 %copy-done.1 = bf16[2,1024,1024]{2,1,0:T(8,128)(2,1)S(1)} copy-done((bf16[2,1024,1024]{2,1,0:T(8,128)(2,1)S(1)}, bf16[2,1024,1024]{2,1,0:T(8,128)(2,1)}, u32[]{:S(2)}) %copy-start.1) | copy-done | bytes 4194328
  101.9 4.6 %slots.3 = (f32[8,64,128]{2,1,0:T(8,128)S(1)}, f32[8,64,128]{2,1,0:T(8,128)S(1)}) custom-call(s32[2,4]{1,0:T(2,128)S(1)} %copy-done.13, s32[1]{0:T(128)S(6)} %copy.9.counts, bf16[16,64,256]{2,1,0:T(8,128)(2,1)S(1)} %bitcast.5, bf16[16,64,256]{2,1,0:T(8,128)(2,1)S(1)} %collective-permute-done.7.far, bf16[2,1024,512]{2,1,0:T(8,128)(2,1)S(1)} %copy-done.3, ...), custom_call_target="tpu_custom_call" | custom-call | flops 1610612736 | bytes 8388608 | tf_op jit(solution)/shard_map/slots/pallas_call | solution.py:255
  106.6 1.5 %collective-permute-done.8.got = f32[8,64,128]{2,1,0:T(8,128)S(1)} collective-permute-done((f32[8,64,128]{2,1,0:T(8,128)S(1)}, f32[8,64,128]{2,1,0:T(8,128)S(1)}, u32[]{:S(2)}, u32[]{:S(2)}) %collective-permute-start.8) | collective-permute-done | bytes 262176 | tf_op jit(solution)/shard_map/ppermute | solution.py:236
  108.9 17.9 %all_to_all.32.arrived = bf16[64,16,256]{2,1,0:T(8,128)(2,1)S(1)} all-to-all(bf16[64,16,256]{2,1,0:T(8,128)(2,1)S(1)} %parcels.3), channel_id=1, replica_groups=mesh['x'=4,'y'=4,'z'=4,'c'=2] {'x','y','z'}, dimensions={0} | all-to-all | bytes 1048576 | tf_op jit(solution)/shard_map/all_to_all | solution.py:240
  127.6 15.1 %all_to_all.33.near = f32[64,8,128]{2,1,0:T(8,128)S(1)} all-to-all(f32[64,8,128]{2,1,0:T(8,128)S(1)} %products.1), channel_id=1, replica_groups=mesh['x'=4,'y'=4,'z'=4,'c'=2] {'x','y','z'}, dimensions={0} | all-to-all | bytes 524288 | tf_op jit(solution)/shard_map/all_to_all | solution.py:240
  142.7 1.5 %collective-permute-done.9.far = f32[64,8,128]{2,1,0:T(8,128)S(1)} collective-permute-done((f32[64,8,128]{2,1,0:T(8,128)S(1)}, f32[64,8,128]{2,1,0:T(8,128)S(1)}, u32[]{:S(2)}, u32[]{:S(2)}) %collective-permute-start.9) | collective-permute-done | bytes 262176 | tf_op jit(solution)/shard_map/ppermute | solution.py:236
  144.2 1.3 closing.1
  (42 shorter events, 5.3 us)
Async XLA Ops:
  0.0 19.7 %collective-permute-start.1 = (f32[256,128]{1,0:T(8,128)}, f32[256,128]{1,0:T(8,128)S(1)}, u32[]{:S(2)}, u32[]{:S(2)}) collective-permute-start(f32[256,128]{1,0:T(8,128)} %rhs.3), channel_id=1, source_target_pairs={{0,8},{8,16},{16,24},{24,32},{32,40},{40,48},{48,56},{56,64},{64,7... | collective-permute-start | bytes 393224 | tf_op jit(solution)/shard_map/ppermute | solution.py:244
  1.7 18.0 %collective-permute-start.2 = (f32[256,128]{1,0:T(8,128)}, f32[256,128]{1,0:T(8,128)S(1)}, u32[]{:S(2)}, u32[]{:S(2)}) collective-permute-start(f32[256,128]{1,0:T(8,128)} %rhs.3), channel_id=1, source_target_pairs={{8,0},{16,8},{24,16},{32,24},{40,32},{48,40},{56,48},{64,56},{72,6... | collective-permute-start | bytes 393224 | tf_op jit(solution)/shard_map/ppermute | solution.py:245
  5.3 0.9 copy-start.6
  6.3 0.7 copy-start.14
  8.2 11.5 %all-to-all-start = ((f32[16,8,128]{2,1,0:T(8,128)}), f32[16,8,128]{2,1,0:T(8,128)S(1)}, u32[]{:S(2)}, u32[]{:S(2)}) async-start(f32[16,8,128]{2,1,0:T(8,128)} %opening.1), calls=%async_computation | async-start | bytes 131072 | tf_op jit(solution)/shard_map/all_to_all | solution.py:240
  19.7 1.0 copy-start.4
  20.6 0.9 copy-start.7
  21.5 0.9 copy-start.8
  22.4 0.7 copy-start.15
  24.2 14.0 %copy-start.10 = (f32[256,128]{1,0:T(8,128)}, f32[256,128]{1,0:T(8,128)S(1)}, u32[]{:S(2)}) copy-start(f32[256,128]{1,0:T(8,128)S(1)} %get-tuple-element.26.z_one) | copy-start | bytes 393220
  37.5 1.9 %collective-permute-start.3 = (bf16[16,64,256]{2,1,0:T(8,128)(2,1)S(1)}, bf16[16,64,256]{2,1,0:T(8,128)(2,1)S(1)}, u32[]{:S(2)}, u32[]{:S(2)}) collective-permute-start(bf16[16,64,256]{2,1,0:T(8,128)(2,1)S(1)} %all_to_all.30.near), channel_id=1, source_target_pairs={{0,1},{1,0},{2,3},{3,2},{4,5},{5,4},{6,7},{7,6},{8,9},{9,8},{10,11... | collective-permute-start | bytes 1572872 | tf_op jit(solution)/shard_map/ppermute | solution.py:236
  39.5 2.2 %copy-start = (bf16[2,1024,1024]{2,1,0:T(8,128)(2,1)S(1)}, bf16[2,1024,1024]{2,1,0:T(8,128)(2,1)}, u32[]{:S(2)}) copy-start(bf16[2,1024,1024]{2,1,0:T(8,128)(2,1)} %factors.3) | copy-start | bytes 12582916
  41.6 1.6 %copy-start.2 = (bf16[2,1024,512]{2,1,0:T(8,128)(2,1)S(1)}, bf16[2,1024,512]{2,1,0:T(8,128)(2,1)}, u32[]{:S(2)}) copy-start(bf16[2,1024,512]{2,1,0:T(8,128)(2,1)} %couplings.3) | copy-start | bytes 6291460
  43.2 0.7 copy-start.12
  43.9 35.0 %copy-start.5 = (bf16[256,512]{1,0:T(8,128)(2,1)S(1)}, bf16[256,512]{1,0:T(8,128)(2,1)}, u32[]{:S(2)}) copy-start(bf16[256,512]{1,0:T(8,128)(2,1)} %precond.3) | copy-start | bytes 786436
  43.9 35.0 %copy-start.16 = (s32[1,2]{1,0:T(1,128)S(1)}, s32[1,2]{1,0:T(1,128)}, u32[]{:S(2)}) copy-start(s32[1,2]{1,0:T(1,128)} %halo.5) | copy-start | bytes 28
  48.5 51.2 %copy-start.3 = (bf16[2,1024,512]{2,1,0:T(8,128)(2,1)S(1)}, bf16[2,1024,512]{2,1,0:T(8,128)(2,1)}, u32[]{:S(2)}) copy-start(bf16[2,1024,512]{2,1,0:T(8,128)(2,1)} %couplings.3) | copy-start | bytes 6291460
  48.5 51.1 %copy-start.13 = (s32[2,4]{1,0:T(2,128)S(1)}, s32[2,4]{1,0:T(2,128)}, u32[]{:S(2)}) copy-start(s32[2,4]{1,0:T(2,128)} %ids.7) | copy-start | bytes 100
  48.5 1.6 %collective-permute-start.4 = (f32[8,64,128]{2,1,0:T(8,128)S(1)}, f32[8,64,128]{2,1,0:T(8,128)S(1)}, u32[]{:S(2)}, u32[]{:S(2)}) collective-permute-start(f32[8,64,128]{2,1,0:T(8,128)S(1)} %get-tuple-element.18), channel_id=1, source_target_pairs={{0,1},{1,0},{2,3},{3,2},{4,5},{5,4},{6,7},{7,6},{8,9},{9,8},{10,11... | collective-permute-start | bytes 786440 | tf_op jit(solution)/shard_map/ppermute | solution.py:236
  48.6 1.5 %collective-permute-start = (s32[2,4]{1,0:T(2,128)S(1)}, s32[2,4]{1,0:T(2,128)S(1)}, u32[]{:S(2)}, u32[]{:S(2)}) collective-permute-start(s32[2,4]{1,0:T(2,128)S(1)} %copy-done.12), channel_id=1, source_target_pairs={{0,1},{1,0},{2,3},{3,2},{4,5},{5,4},{6,7},{7,6},{8,9},{9,8},{10,11... | collective-permute-start | bytes 104 | tf_op jit(solution)/shard_map/ppermute | solution.py:236
  52.1 26.8 %all-to-all-start.2 = ((bf16[64,16,512]{2,1,0:T(8,128)(2,1)}), bf16[64,16,512]{2,1,0:T(8,128)(2,1)S(1)}, u32[]{:S(2)}, u32[]{:S(2)}) async-start(bf16[64,16,512]{2,1,0:T(8,128)(2,1)} %parcels.2), calls=%async_computation.2 | async-start | bytes 2097152 | tf_op jit(solution)/shard_map/all_to_all | solution.py:240
  60.0 16.9 %collective-permute-start.5 = (f32[16,256]{1,0:T(8,128)S(1)}, f32[16,256]{1,0:T(8,128)S(1)}, u32[]{:S(2)}, u32[]{:S(2)}) collective-permute-start(f32[16,256]{1,0:T(8,128)S(1)} %get-tuple-element.19.base), channel_id=1, source_target_pairs={{0,8},{8,16},{16,24},{24,32},{32,40},{40,48},{48,56},{56,64},{64,7... | collective-permute-start | bytes 49160 | tf_op jit(solution)/shard_map/ppermute | solution.py:244
  61.6 15.2 %collective-permute-start.6 = (f32[16,256]{1,0:T(8,128)S(1)}, f32[16,256]{1,0:T(8,128)S(1)}, u32[]{:S(2)}, u32[]{:S(2)}) collective-permute-start(f32[16,256]{1,0:T(8,128)S(1)} %get-tuple-element.19.base), channel_id=1, source_target_pairs={{8,0},{16,8},{24,16},{32,24},{40,32},{48,40},{56,48},{64,56},{72,6... | collective-permute-start | bytes 49160 | tf_op jit(solution)/shard_map/ppermute | solution.py:245
  78.9 0.9 copy-start.9
  97.8 1.9 %collective-permute-start.7 = (bf16[16,64,256]{2,1,0:T(8,128)(2,1)S(1)}, bf16[16,64,256]{2,1,0:T(8,128)(2,1)S(1)}, u32[]{:S(2)}, u32[]{:S(2)}) collective-permute-start(bf16[16,64,256]{2,1,0:T(8,128)(2,1)S(1)} %bitcast.4), channel_id=1, source_target_pairs={{0,1},{1,0},{2,3},{3,2},{4,5},{5,4},{6,7},{7,6},{8,9},{9,8},{10,11... | collective-permute-start | bytes 1572872 | tf_op jit(solution)/shard_map/ppermute | solution.py:236
  99.7 2.2 %copy-start.1 = (bf16[2,1024,1024]{2,1,0:T(8,128)(2,1)S(1)}, bf16[2,1024,1024]{2,1,0:T(8,128)(2,1)}, u32[]{:S(2)}) copy-start(bf16[2,1024,1024]{2,1,0:T(8,128)(2,1)} %factors.3) | copy-start | bytes 12582916
  101.9 42.4 %copy-start.11 = (f32[256,128]{1,0:T(8,128)S(1)}, f32[256,128]{1,0:T(8,128)}, u32[]{:S(2)}) copy-start(f32[256,128]{1,0:T(8,128)} %copy-done.10) | copy-start | bytes 393220
  106.5 1.6 %collective-permute-start.8 = (f32[8,64,128]{2,1,0:T(8,128)S(1)}, f32[8,64,128]{2,1,0:T(8,128)S(1)}, u32[]{:S(2)}, u32[]{:S(2)}) collective-permute-start(f32[8,64,128]{2,1,0:T(8,128)S(1)} %get-tuple-element.22), channel_id=1, source_target_pairs={{0,1},{1,0},{2,3},{3,2},{4,5},{5,4},{6,7},{7,6},{8,9},{9,8},{10,11... | collective-permute-start | bytes 786440 | tf_op jit(solution)/shard_map/ppermute | solution.py:236
  142.7 1.5 %collective-permute-start.9 = (f32[64,8,128]{2,1,0:T(8,128)S(1)}, f32[64,8,128]{2,1,0:T(8,128)S(1)}, u32[]{:S(2)}, u32[]{:S(2)}) collective-permute-start(f32[64,8,128]{2,1,0:T(8,128)S(1)} %all_to_all.33.near), channel_id=1, source_target_pairs={{0,1},{1,0},{2,3},{3,2},{4,5},{5,4},{6,7},{7,6},{8,9},{9,8},{10,11... | collective-permute-start | bytes 786440 | tf_op jit(solution)/shard_map/ppermute | solution.py:236

commit v2 on v1

v2 whole, which is shorter than its diff:
```python
import jax
import jax.numpy as jnp
from jax import lax
from jax.experimental import pallas as pl
from jax.experimental.pallas import tpu as pltpu
from jax.sharding import Mesh
from jax.sharding import PartitionSpec as P

BI = 128
ROWS = 256
COLS = 128
HALF = 64
PART = 16
GROUPS = 16
BLOCKS = 32
SUB = ("x", "y")
XYZ = ("x", "y", "z")
ALL = ("x", "y", "z", "c")
F32 = jnp.float32
BF16 = jnp.bfloat16
SHRINK = 2.0**-31
VMEM = pl.BlockSpec(memory_space=pltpu.VMEM)
SMEM = pl.BlockSpec(memory_space=pltpu.SMEM)
ANY = pl.BlockSpec(memory_space=pl.ANY)
HBM = pl.BlockSpec(memory_space=pltpu.HBM)
GROUP, DEPTH, CORE, LIVE, HALO, IDS = 0, 1, 2, 3, 4, 6
NT = (((1,), (1,)), ((), ()))
NN = (((1,), (0,)), ((), ()))


def dot(left, right, dims=NN):
    return lax.dot_general(left, right, dims, preferred_element_type=F32)


def call(body, outs, specs, scratch=(), flops=0, moved=1 << 20, room=4 << 20):
    return pl.pallas_call(
        body,
        out_shape=outs,
        in_specs=specs,
        out_specs=[VMEM] * len(outs),
        scratch_shapes=list(scratch),
        cost_estimate=pl.CostEstimate(flops=flops, bytes_accessed=moved, transcendentals=0),
        compiler_params=pltpu.CompilerParams(vmem_limit_bytes=room),
    )


def out(shape, dtype):
    return jax.ShapeDtypeStruct(shape, dtype)


def parity(table, place):
    return table[place] & 1


def block_at(table, place):
    return pl.ds(pl.multiple_of(parity(table, place) * BI, BI), BI)


def opening(table, rhs, sent, held):
    field = rhs[...]
    held[...] = field
    sums = jnp.sum(field * field, axis=0, keepdims=True)
    row = lax.broadcasted_iota(jnp.int32, (8, COLS), 0)
    left = parity(table, HALO).astype(F32)
    right = parity(table, HALO + 1).astype(F32)
    tile = jnp.where(row == 0, sums, jnp.where(row == 1, left, jnp.where(row == 2, right, 0.0)))
    sent[...] = jnp.broadcast_to(tile[None], sent.shape)


def bring_owned(precond, diag, precond_v, diag_v, sems):
    copies = [
        pltpu.make_async_copy(precond, precond_v, sems.at[0]),
        pltpu.make_async_copy(diag, diag_v, sems.at[1]),
    ]
    for copy in copies:
        copy.start()
    for copy in copies:
        copy.wait()


def bring_couplings(table, after, couplings, coup_v, sems):
    def copy(slot):
        return pltpu.make_async_copy(couplings.at[slot], coup_v.at[slot], sems.at[slot])

    copy(0).start()

    @pl.when(table[LIVE] > 1)
    def _():
        copy(1).start()
        copy(1).wait()

    copy(0).wait()


def first_direction(
    table, table_far, rhs, before, after, facts, precond, diag, sent, z_nat, base, basis, turned
):
    beta = jnp.sqrt(jnp.sum(facts[:, 0:1, :], axis=0))
    v = rhs[...] / beta
    left = before[block_at(table, HALO), :] / beta
    right = after[block_at(table, HALO + 1), :] / beta
    patch = jnp.concatenate([v, left, right], axis=0).astype(BF16)
    z = v + dot(precond[...], patch)
    z_nat[...] = z
    half = pl.ds(pl.multiple_of(table[CORE] * HALF, HALF), HALF)
    part = pl.ds(pl.multiple_of(table[CORE] * HALF + table[DEPTH] * PART, PART), PART)
    turned[...] = z.T
    mine = turned[half, :].astype(BF16)
    sent[...] = jnp.broadcast_to(mine[None], sent.shape)
    turned[...] = (3.0 * z + dot(diag[...], z.astype(BF16))).T
    base[...] = turned[part, :]
    turned[...] = v.T
    basis[...] = turned[part, :]


def slots(table, near, far, coup, factors, kept, given, fact, picked, one, two, sems):
    live = table[LIVE]

    def fetch(slot, n):
        span = pl.ds(n * 256, 256)
        return pltpu.make_async_copy(
            factors.at[slot, span], fact.at[slot, span], sems.at[slot, n]
        )

    for n in range(4):
        fetch(0, n).start()

    @pl.when(live > 1)
    def _():
        for n in range(4):
            fetch(1, n).start()

    @pl.when(live < 2)
    def _():
        kept[4:8] = jnp.zeros((4, HALF, BI), F32)
        given[4:8] = jnp.zeros((4, HALF, BI), F32)

    def step(slot, carry):
        for j in range(4):
            block = table[IDS + slot * 4 + j]
            lanes = pl.ds(pl.multiple_of((block & 1) * BI, BI), BI)
            picked[0:HALF, j * BI : (j + 1) * BI] = near[block >> 1, :, lanes]
            picked[HALF:COLS, j * BI : (j + 1) * BI] = far[block >> 1, :, lanes]
        for n in range(4):
            span = slice(n * 256, (n + 1) * 256)
            one[:, span] = dot(picked[...], coup[slot, span, :], NT).astype(BF16)
        for n in range(4):
            span = slice(n * 256, (n + 1) * 256)
            fetch(slot, n).wait()
            two[:, span] = dot(one[...], fact[slot, span, :], NT).astype(BF16)
        for n in range(4):
            span = slice(n * 256, (n + 1) * 256)
            one[:, span] = dot(two[...], fact[slot, :, span]).astype(BF16)
        for n in range(2):
            piece = dot(one[...], coup[slot, :, n * 256 : (n + 1) * 256])
            for m in range(2):
                lanes = slice(m * BI, (m + 1) * BI)
                kept[slot * 4 + n * 2 + m] = piece[0:HALF, lanes]
                given[slot * 4 + n * 2 + m] = piece[HALF:COLS, lanes]
        return carry

    lax.fori_loop(0, live, step, 0)


def parcels(table, table_far, kept, got, facts, base, sent, total):
    total[...] = jnp.zeros_like(total)
    for i in range(8):
        block = table[IDS + i]
        total[block] = total[block] + kept[i]
    for i in range(8):
        block = table_far[IDS + i]
        total[block] = total[block] + got[i]
    with_halo = sent.shape[2] > ROWS

    def group(d, carry):
        lower = 2 * ((d + GROUPS - 1) & (GROUPS - 1))
        upper = 2 * ((d + 1) & (GROUPS - 1))
        blocks = [total[2 * d], total[2 * d + 1]]
        if with_halo:
            left = facts[d, 1:2, :] > 0.5
            right = facts[d, 2:3, :] > 0.5
            blocks.append(jnp.where(left, total[lower + 1], total[lower]))
            blocks.append(jnp.where(right, total[upper + 1], total[upper]))
        for j, block in enumerate(blocks):
            low = block.astype(BF16)
            for z in range(4):
                sent[d * 4 + z, :, j * BI : (j + 1) * BI] = low[z * PART : (z + 1) * PART]
        return carry

    lax.fori_loop(0, GROUPS, group, 0)
    if with_halo:
        mine = table[GROUP]
        depth = table[DEPTH]
        part = pl.ds(pl.multiple_of(depth * PART, PART), PART)
        for side, other in ((0, mine + 1), (1, mine + GROUPS - 1)):
            other = other & (GROUPS - 1)
            upper = facts[other, side + 1 : side + 2, :] > 0.5
            block = jnp.where(upper, total[2 * mine + 1, part, :], total[2 * mine, part, :])
            stays = jnp.where(upper, base[:, BI:], base[:, :BI])
            lanes = slice(ROWS + side * BI, ROWS + (side + 1) * BI)
            sent[other * 4 + depth, :, lanes] = (block - stays).astype(BF16)


def summed(arrived):
    def add(i, total):
        for j in range(8):
            total = total + arrived[i * 8 + j].astype(F32)
        return total

    return lax.fori_loop(0, 8, add, jnp.zeros(arrived.shape[1:], F32))


def second_direction(arrived, base, precond, diag, sent, base_two, w):
    coupled = summed(arrived)
    image = base[...] - coupled[:, :ROWS]
    patch = jnp.concatenate([image, -coupled[:, ROWS:]], axis=1).astype(BF16)
    z = image + dot(patch, precond[...], NT)
    low = z.astype(BF16)
    w[...] = image
    base_two[...] = 3.0 * z + dot(low, diag[...], NT)
    sent[...] = jnp.broadcast_to(low[None], sent.shape)


def products(table, arrived, base, w, basis, sent):
    image = (base[...] - summed(arrived)) * SHRINK
    one = w[...]
    v = basis[...]
    lane = lax.broadcasted_iota(jnp.int32, (PART, COLS), 1)
    row = lax.broadcasted_iota(jnp.int32, (PART, COLS), 0)
    here = lane == row + (table[CORE] * HALF + table[DEPTH] * PART)
    rank = lax.broadcasted_iota(jnp.int32, (8, COLS), 0)
    tile = jnp.zeros((8, COLS), F32)
    pairs = [(v, one), (one, one), (v, image), (one, image), (image, image)]
    for k, (left, right) in enumerate(pairs):
        value = jnp.sum(left * right, axis=1, keepdims=True)
        spread = jnp.sum(jnp.where(here, value, 0.0), axis=0, keepdims=True)
        tile = jnp.where(rank == k, spread, tile)
    sent[...] = jnp.broadcast_to(tile[None], sent.shape)


def closing(table, near, far, facts, z_one, z_near, z_far, answer):
    sums = jnp.sum(near[...], axis=0) + jnp.sum(far[...], axis=0)
    beta = jnp.sqrt(jnp.sum(facts[:, 0:1, :], axis=0))
    h11, ww, vx, wx, xx = (sums[k : k + 1] for k in range(5))
    h21 = jnp.sqrt(ww - h11 * h11)
    small = SHRINK * h11
    h12 = (vx - small * h11) / (SHRINK * h21)
    h22 = ((wx - h11 * vx) - small * ww + small * h11 * h11) / (SHRINK * h21) / h21
    scaled = SHRINK * h21
    norm = ((xx - 2.0 * small * wx) + small * small * ww) / scaled / scaled
    low_square = norm - h12 * h12 - h22 * h22
    rho = jnp.sqrt(h11 * h11 + h21 * h21)
    cosine = h11 / rho
    sine = h21 / rho
    top = cosine * h12 + sine * h22
    low = cosine * h22 - sine * h12
    y2 = -low * sine * beta / (low * low + low_square)
    y1 = (cosine * beta - top * y2) / rho
    second = y2 / h21
    first = y1 - second * h11
    a = z_near[0].astype(F32)
    b = z_far[0].astype(F32)
    swap = table[CORE] == 1
    stacked = jnp.concatenate([jnp.where(swap, b, a), jnp.where(swap, a, b)], axis=0)
    answer[...] = first * z_one[...] + second * stacked.T


def other_core(array):
    return lax.ppermute(array, "c", [(0, 1), (1, 0)])


def swap_all(array, axes):
    return lax.all_to_all(array, axes, split_axis=0, concat_axis=0, tiled=True)


def neighbours(array):
    forward = lax.ppermute(array, SUB, [(i, (i + 1) % GROUPS) for i in range(GROUPS)])
    backward = lax.ppermute(array, SUB, [((i + 1) % GROUPS, i) for i in range(GROUPS)])
    return forward, backward


def on_device(rhs, schur_diag, precond, halo_ids, factors, couplings, block_ids, counts):
    group = lax.axis_index(SUB)
    place = jnp.stack([group, lax.axis_index("z"), lax.axis_index("c")]).astype(jnp.int32)
    table = jnp.concatenate([place, counts, halo_ids.reshape(-1), block_ids.reshape(-1)])
    table_far = other_core(table)

    def apply_slots(near, far):
        return call(
            slots,
            [out((8, HALF, BI), F32), out((8, HALF, BI), F32)],
            [SMEM, VMEM, VMEM, VMEM, HBM],
            [
                pltpu.VMEM((2, 1024, 1024), BF16),
                pltpu.VMEM((COLS, 512), BF16),
                pltpu.VMEM((COLS, 1024), BF16),
                pltpu.VMEM((COLS, 1024), BF16),
                pltpu.SemaphoreType.DMA((2, 4)),
            ],
            flops=2 * 805306368,
            moved=8 << 20,
            room=50000 << 10,
        )(table, near, far, coup_v, factors)

    def to_owners(kept, given, width):
        got = other_core(given)
        (sent,) = call(
            parcels,
            [out((64, PART, width), BF16)],
            [SMEM, SMEM, VMEM, VMEM, VMEM, VMEM],
            [pltpu.VMEM((BLOCKS, HALF, BI), F32)],
        )(table, table_far, kept, got, facts, base)
        return swap_all(sent, XYZ)

    opened, held = call(
        opening, [out((GROUPS, 8, COLS), F32), out((ROWS, COLS), F32)], [SMEM, VMEM]
    )(table, rhs)
    facts = swap_all(opened, SUB)
    before, after = neighbours(held)
    precond_v, diag_v = call(
        bring_owned,
        [out(a.shape, BF16) for a in (precond, schur_diag)],
        [HBM, HBM],
        [pltpu.SemaphoreType.DMA((2,))],
    )(precond, schur_diag)
    sent, z_one, base, basis = call(
        first_direction,
        [
            out((GROUPS, HALF, ROWS), BF16),
            out((ROWS, COLS), F32),
            out((PART, ROWS), F32),
            out((PART, ROWS), F32),
        ],
        [SMEM, SMEM, VMEM, VMEM, VMEM, VMEM, VMEM, VMEM],
        [pltpu.VMEM((COLS, ROWS), F32)],
        flops=1 << 26,
    )(table, table_far, held, before, after, facts, precond_v, diag_v)
    (coup_v,) = call(
        bring_couplings,
        [out(couplings.shape, BF16)],
        [SMEM, ANY, HBM],
        [pltpu.SemaphoreType.DMA((2,))],
        moved=12 << 20,
    )(table, base, couplings)
    near = swap_all(sent, SUB)
    far = other_core(near)
    kept, given = apply_slots(near, far)
    arrived = to_owners(kept, given, 2 * ROWS)
    sent, base, w = call(
        second_direction,
        [out((64, PART, ROWS), BF16), out((PART, ROWS), F32), out((PART, ROWS), F32)],
        [VMEM, VMEM, VMEM, VMEM],
        flops=1 << 26,
    )(arrived, base, precond_v, diag_v)
    near = swap_all(sent, XYZ).reshape(GROUPS, HALF, ROWS)
    far = other_core(near)
    kept, given = apply_slots(near, far)
    arrived = to_owners(kept, given, ROWS)
    (sent,) = call(
        products, [out((64, 8, COLS), F32)], [SMEM, VMEM, VMEM, VMEM, VMEM]
    )(table, arrived, base, w, basis)
    sums = swap_all(sent, XYZ)
    sums_far = other_core(sums)
    own = [lax.dynamic_slice_in_dim(half, group, 1, 0) for half in (near, far)]
    (answer,) = call(
        closing, [out((ROWS, COLS), F32)], [SMEM] + [VMEM] * 6
    )(table, sums, sums_far, facts, z_one, *own)
    return answer


def solution(mesh):
    torus = Mesh(mesh.devices.reshape(4, 4, 4, 2), ALL)
    placed = (
        P(SUB, None),
        P(SUB, None),
        P(SUB, None),
        P(SUB, None),
        P(ALL, None, None),
        P(ALL, None, None),
        P(ALL, None),
        P(ALL),
    )

    return jax.shard_map(
        on_device, mesh=torus, in_specs=placed, out_specs=P(SUB, None), check_vma=False
    )
```

time: 147 us -> 142 us (0.966)
  blocking collectives: 63.2 us -> 89.9 us
  waiting for transfers between devices: 28.3 us -> 13.2 us
  starting transfers between devices: 23.1 us -> 12.3 us
  local copies, waits for them, and re-layouts: 12.6 us -> 4.26 us
  Pallas kernels: 17.5 us -> 20.4 us
    all_to_all x4 -> x5, blocking collectives: 63.2 us -> 89.9 us  [swap_all(): return lax.all_to_all(array, axes, split_axis=0, concat_axis=0, tiled=True)]
    ppermute x2 -> x1, waiting for transfers between devices: 11.4 us -> 0.01 us  [neighbours(): lax.ppermute(array, SUB, [(i, (i + 1) % GROUPS) for i in range(GROUPS)])]
    unnamed x34 -> x8, local copies, waits for them, and re-layouts: 12.6 us -> 2.76 us
    all_to_all x2 -> x1, starting transfers between devices: 11.7 us -> 6.72 us  [swap_all(): return lax.all_to_all(array, axes, split_axis=0, concat_axis=0, tiled=True)]
    all_to_all x2 -> x1, waiting for transfers between devices: 9.64 us -> 5.49 us  [swap_all(): return lax.all_to_all(array, axes, split_axis=0, concat_axis=0, tiled=True)]
    ppermute x2 -> x1, starting transfers between devices: 3.33 us -> 0.01 us  [neighbours(): lax.ppermute(array, SUB, [(i, (i + 1) % GROUPS) for i in range(GROUPS)])]
    pallas_call x9 -> x11, Pallas kernels: 17.5 us -> 20.4 us  [the longest x2 12.8 us: apply_slots(): call(slots, [out((8, HALF, BI), F32), out((8, HALF, BI), F32)], [SMEM, VM...]
    ppermute x2 -> x1, starting transfers between devices: 7.43 us -> 5.32 us  [neighbours(): lax.ppermute(array, SUB, [((i + 1) % GROUPS, i) for i in range(GROUPS)])]
  transfers between devices with their start and end apart: 12 -> 9, of which waited for: 8 -> 6; matrix products, arithmetic and copies ran while one was open for 0% -> 0% of each run, Pallas kernels for 1% -> 1%
where the time goes in v2:
time: 142 us; the launch traced here: 141 us
  blocking collectives  89.9 us (63%)
  Pallas kernels  20.4 us (14%)
  waiting for transfers between devices  13.2 us (9%)
  starting transfers between devices  12.3 us (9%)
  local copies, waits for them, and re-layouts  4.26 us (3%)
    all_to_all x5, blocking collectives, swap_all(): return lax.all_to_all(array, axes, split_axis=0, concat_axis=0, tiled=True)  89.9 us
    pallas_call x2, Pallas kernels, apply_slots(): call(slots, [out((8, HALF, BI), F32), out((8, HALF, BI), F32)], [SMEM, VM...  12.8 us
    ppermute x6, waiting for transfers between devices, other_core(): return lax.ppermute(array, 'c', [(0, 1), (1, 0)])  7.66 us
    all_to_all x1, starting transfers between devices, swap_all(): return lax.all_to_all(array, axes, split_axis=0, concat_axis=0, tiled=True)  6.72 us
    all_to_all x1, waiting for transfers between devices, swap_all(): return lax.all_to_all(array, axes, split_axis=0, concat_axis=0, tiled=True)  5.49 us
    ppermute x1, starting transfers between devices, neighbours(): lax.ppermute(array, SUB, [((i + 1) % GROUPS, i) for i in range(GROUPS)])  5.32 us
  transfers between devices with their start and end apart: 9, of which 6 were waited for; matrix products, arithmetic and copies ran while one was open for 0% of the time, Pallas kernels for 1%

profile of v2, /device:TPU:0, one launch (start us, length us, event | category | flops | bytes accessed | tf_op | source)
XLA Modules:
  0.0 141.0 jit_solution(17663785580040966630)
XLA Ops:
  0.8 0.8 reshape.10
  1.6 0.7 concatenate.3.table
  2.3 0.9 copy-done.3
  3.2 1.2 shard_map.82
  4.4 5.3 %collective-permute-start.2 = (f32[256,128]{1,0:T(8,128)S(1)}, f32[256,128]{1,0:T(8,128)S(1)}, u32[]{:S(2)}, u32[]{:S(2)}) collective-permute-start(f32[256,128]{1,0:T(8,128)S(1)} %get-tuple-element.20.rhs), channel_id=1, source_target_pairs={{8,0},{16,8},{24,16},{32,24},{40,32},{48,40},{56,48},{64,56},{72,6... | collective-permute-start | bytes 393224 | tf_op jit(solution)/shard_map/ppermute | solution.py:278
  9.7 6.7 %all-to-all-start = ((f32[16,8,128]{2,1,0:T(8,128)}), f32[16,8,128]{2,1,0:T(8,128)S(1)}, u32[]{:S(2)}, u32[]{:S(2)}) async-start(f32[16,8,128]{2,1,0:T(8,128)} %get-tuple-element.21), calls=%async_computation | async-start | bytes 131072 | tf_op jit(solution)/shard_map/all_to_all | solution.py:273
  16.5 0.1 collective-permute-start
  16.6 0.9 copy-done.1
  17.5 0.9 copy-done.2
  18.4 0.2 shard_map.83
  18.6 5.5 %all-to-all-done.facts = f32[16,8,128]{2,1,0:T(8,128)S(1)} async-done(((f32[16,8,128]{2,1,0:T(8,128)}), f32[16,8,128]{2,1,0:T(8,128)S(1)}, u32[]{:S(2)}, u32[]{:S(2)}) %all-to-all-start) | async-done | bytes 65568 | tf_op jit(solution)/shard_map/all_to_all | solution.py:273
  24.1 1.1 shard_map.84
  25.3 13.6 %all_to_all.30.near = bf16[16,64,256]{2,1,0:T(8,128)(2,1)S(1)} all-to-all(bf16[16,64,256]{2,1,0:T(8,128)(2,1)S(1)} %get-tuple-element.24), channel_id=1, replica_groups=mesh['x'=4,'y'=4,'z'=4,'c'=2] {'x','y'}, dimensions={0} | all-to-all | bytes 1048576 | tf_op jit(solution)/shard_map/all_to_all | solution.py:273
  38.9 0.7 shard_map.85.coup
  39.6 1.2 collective-permute-done.3.far
  40.8 6.4 %shard_map.86 = (f32[8,64,128]{2,1,0:T(8,128)S(1)}, f32[8,64,128]{2,1,0:T(8,128)S(1)}) custom-call(s32[14]{0:T(128)S(1)} %concatenate.3.table, bf16[16,64,256]{2,1,0:T(8,128)(2,1)S(1)} %all_to_all.30.near, bf16[16,64,256]{2,1,0:T(8,128)(2,1)S(1)} %collective-permute-done.3.far, bf16[2,1024,512]{2,1,0:T(8,128)(2,1)S(1)} %shard_map.85.coup, ...), custom_call_target="tpu_custom_call" | custom-call | flops 1610612736 | bytes 8388608 | tf_op jit(solution)/shard_map/pallas_call | solution.py:289
  47.2 0.1 collective-permute-start.4
  47.3 1.5 %collective-permute-done.4.got = f32[8,64,128]{2,1,0:T(8,128)S(1)} collective-permute-done((f32[8,64,128]{2,1,0:T(8,128)S(1)}, f32[8,64,128]{2,1,0:T(8,128)S(1)}, u32[]{:S(2)}, u32[]{:S(2)}) %collective-permute-start.4) | collective-permute-done | bytes 262176 | tf_op jit(solution)/shard_map/ppermute | solution.py:269
  48.8 1.0 shard_map.87
  49.8 26.3 %all_to_all.31.arrived = bf16[64,16,512]{2,1,0:T(8,128)(2,1)S(1)} all-to-all(bf16[64,16,512]{2,1,0:T(8,128)(2,1)S(1)} %shard_map.87), channel_id=1, replica_groups=mesh['x'=4,'y'=4,'z'=4,'c'=2] {'x','y','z'}, dimensions={0} | all-to-all | bytes 2097152 | tf_op jit(solution)/shard_map/all_to_all | solution.py:273
  76.1 0.5 shard_map.88
  76.6 16.7 %all_to_all.32 = bf16[64,16,256]{2,1,0:T(8,128)(2,1)S(1)} all-to-all(bf16[64,16,256]{2,1,0:T(8,128)(2,1)S(1)} %get-tuple-element.28), channel_id=1, replica_groups=mesh['x'=4,'y'=4,'z'=4,'c'=2] {'x','y','z'}, dimensions={0} | all-to-all | bytes 1048576 | tf_op jit(solution)/shard_map/all_to_all | solution.py:273
  93.3 1.9 %collective-permute-done.5.far = bf16[16,64,256]{2,1,0:T(8,128)(2,1)S(1)} collective-permute-done((bf16[16,64,256]{2,1,0:T(8,128)(2,1)S(1)}, bf16[16,64,256]{2,1,0:T(8,128)(2,1)S(1)}, u32[]{:S(2)}, u32[]{:S(2)}) %collective-permute-start.5) | collective-permute-done | bytes 524320 | tf_op jit(solution)/shard_map/ppermute | solution.py:269
  95.2 6.4 %shard_map.89 = (f32[8,64,128]{2,1,0:T(8,128)S(1)}, f32[8,64,128]{2,1,0:T(8,128)S(1)}) custom-call(s32[14]{0:T(128)S(1)} %concatenate.3.table, bf16[16,64,256]{2,1,0:T(8,128)(2,1)S(1)} %bitcast.6, bf16[16,64,256]{2,1,0:T(8,128)(2,1)S(1)} %collective-permute-done.5.far, bf16[2,1024,512]{2,1,0:T(8,128)(2,1)S(1)} %shard_map.85.coup, bf16[2,1024,1024]{2,1,0:T(8,128)(2,1)} %factors.3), custom_call_target="tpu_custom_call" | custom-call | flops 1610612736 | bytes 8388608 | tf_op jit(solution)/shard_map/pallas_call | solution.py:289
  101.7 0.1 collective-permute-start.6
  101.8 1.5 %collective-permute-done.6.got = f32[8,64,128]{2,1,0:T(8,128)S(1)} collective-permute-done((f32[8,64,128]{2,1,0:T(8,128)S(1)}, f32[8,64,128]{2,1,0:T(8,128)S(1)}, u32[]{:S(2)}, u32[]{:S(2)}) %collective-permute-start.6) | collective-permute-done | bytes 262176 | tf_op jit(solution)/shard_map/ppermute | solution.py:269
  103.3 0.8 shard_map.90
  104.1 18.1 %all_to_all.33.arrived = bf16[64,16,256]{2,1,0:T(8,128)(2,1)S(1)} all-to-all(bf16[64,16,256]{2,1,0:T(8,128)(2,1)S(1)} %shard_map.90), channel_id=1, replica_groups=mesh['x'=4,'y'=4,'z'=4,'c'=2] {'x','y','z'}, dimensions={0} | all-to-all | bytes 1048576 | tf_op jit(solution)/shard_map/all_to_all | solution.py:273
  122.2 0.7 shard_map.91
  123.0 15.1 %all_to_all.34.near = f32[64,8,128]{2,1,0:T(8,128)S(1)} all-to-all(f32[64,8,128]{2,1,0:T(8,128)S(1)} %shard_map.91), channel_id=1, replica_groups=mesh['x'=4,'y'=4,'z'=4,'c'=2] {'x','y','z'}, dimensions={0} | all-to-all | bytes 524288 | tf_op jit(solution)/shard_map/all_to_all | solution.py:273
  138.1 1.5 %collective-permute-done.7.far = f32[64,8,128]{2,1,0:T(8,128)S(1)} collective-permute-done((f32[64,8,128]{2,1,0:T(8,128)S(1)}, f32[64,8,128]{2,1,0:T(8,128)S(1)}, u32[]{:S(2)}, u32[]{:S(2)}) %collective-permute-start.7) | collective-permute-done | bytes 262176 | tf_op jit(solution)/shard_map/ppermute | solution.py:269
  139.6 1.3 shard_map.92
  (14 shorter events, 0.0 us)
Async XLA Ops:
  0.0 38.9 %copy-start = (bf16[2,1024,512]{2,1,0:T(8,128)(2,1)S(1)}, bf16[2,1024,512]{2,1,0:T(8,128)(2,1)}, u32[]{:S(2)}) copy-start(bf16[2,1024,512]{2,1,0:T(8,128)(2,1)} %couplings.1) | copy-start | bytes 6291460
  2.3 0.9 copy-start.3
  4.4 19.7 %collective-permute-start.2 = (f32[256,128]{1,0:T(8,128)S(1)}, f32[256,128]{1,0:T(8,128)S(1)}, u32[]{:S(2)}, u32[]{:S(2)}) collective-permute-start(f32[256,128]{1,0:T(8,128)S(1)} %get-tuple-element.20.rhs), channel_id=1, source_target_pairs={{8,0},{16,8},{24,16},{32,24},{40,32},{48,40},{56,48},{64,56},{72,6... | collective-permute-start | bytes 393224 | tf_op jit(solution)/shard_map/ppermute | solution.py:278
  9.7 14.4 %collective-permute-start.1 = (f32[256,128]{1,0:T(8,128)S(1)}, f32[256,128]{1,0:T(8,128)S(1)}, u32[]{:S(2)}, u32[]{:S(2)}) collective-permute-start(f32[256,128]{1,0:T(8,128)S(1)} %get-tuple-element.20.rhs), channel_id=1, source_target_pairs={{0,8},{8,16},{16,24},{24,32},{32,40},{40,48},{48,56},{56,64},{64,7... | collective-permute-start | bytes 393224 | tf_op jit(solution)/shard_map/ppermute | solution.py:277
  9.7 14.4 %all-to-all-start = ((f32[16,8,128]{2,1,0:T(8,128)}), f32[16,8,128]{2,1,0:T(8,128)S(1)}, u32[]{:S(2)}, u32[]{:S(2)}) async-start(f32[16,8,128]{2,1,0:T(8,128)} %get-tuple-element.21), calls=%async_computation | async-start | bytes 131072 | tf_op jit(solution)/shard_map/all_to_all | solution.py:273
  16.5 2.2 %collective-permute-start = (s32[14]{0:T(128)S(1)}, s32[14]{0:T(128)S(1)}, u32[]{:S(2)}, u32[]{:S(2)}) collective-permute-start(s32[14]{0:T(128)S(1)} %concatenate.3.table), channel_id=1, source_target_pairs={{0,1},{1,0},{2,3},{3,2},{4,5},{5,4},{6,7},{7,6},{8,9},{9,8},{10,11... | collective-permute-start | bytes 176 | tf_op jit(solution)/shard_map/ppermute | solution.py:269
  16.6 1.0 copy-start.1
  17.5 0.9 copy-start.2
  38.9 1.9 %collective-permute-start.3 = (bf16[16,64,256]{2,1,0:T(8,128)(2,1)S(1)}, bf16[16,64,256]{2,1,0:T(8,128)(2,1)S(1)}, u32[]{:S(2)}, u32[]{:S(2)}) collective-permute-start(bf16[16,64,256]{2,1,0:T(8,128)(2,1)S(1)} %all_to_all.30.near), channel_id=1, source_target_pairs={{0,1},{1,0},{2,3},{3,2},{4,5},{5,4},{6,7},{7,6},{8,9},{9,8},{10,11... | collective-permute-start | bytes 1572872 | tf_op jit(solution)/shard_map/ppermute | solution.py:269
  47.2 1.6 %collective-permute-start.4 = (f32[8,64,128]{2,1,0:T(8,128)S(1)}, f32[8,64,128]{2,1,0:T(8,128)S(1)}, u32[]{:S(2)}, u32[]{:S(2)}) collective-permute-start(f32[8,64,128]{2,1,0:T(8,128)S(1)} %get-tuple-element.27), channel_id=1, source_target_pairs={{0,1},{1,0},{2,3},{3,2},{4,5},{5,4},{6,7},{7,6},{8,9},{9,8},{10,11... | collective-permute-start | bytes 786440 | tf_op jit(solution)/shard_map/ppermute | solution.py:269
  93.3 1.9 %collective-permute-start.5 = (bf16[16,64,256]{2,1,0:T(8,128)(2,1)S(1)}, bf16[16,64,256]{2,1,0:T(8,128)(2,1)S(1)}, u32[]{:S(2)}, u32[]{:S(2)}) collective-permute-start(bf16[16,64,256]{2,1,0:T(8,128)(2,1)S(1)} %bitcast.5), channel_id=1, source_target_pairs={{0,1},{1,0},{2,3},{3,2},{4,5},{5,4},{6,7},{7,6},{8,9},{9,8},{10,11... | collective-permute-start | bytes 1572872 | tf_op jit(solution)/shard_map/ppermute | solution.py:269
  101.7 1.6 %collective-permute-start.6 = (f32[8,64,128]{2,1,0:T(8,128)S(1)}, f32[8,64,128]{2,1,0:T(8,128)S(1)}, u32[]{:S(2)}, u32[]{:S(2)}) collective-permute-start(f32[8,64,128]{2,1,0:T(8,128)S(1)} %get-tuple-element.30), channel_id=1, source_target_pairs={{0,1},{1,0},{2,3},{3,2},{4,5},{5,4},{6,7},{7,6},{8,9},{9,8},{10,11... | collective-permute-start | bytes 786440 | tf_op jit(solution)/shard_map/ppermute | solution.py:269
  138.1 1.5 %collective-permute-start.7 = (f32[64,8,128]{2,1,0:T(8,128)S(1)}, f32[64,8,128]{2,1,0:T(8,128)S(1)}, u32[]{:S(2)}, u32[]{:S(2)}) collective-permute-start(f32[64,8,128]{2,1,0:T(8,128)S(1)} %all_to_all.34.near), channel_id=1, source_target_pairs={{0,1},{1,0},{2,3},{3,2},{4,5},{5,4},{6,7},{7,6},{8,9},{9,8},{10,11... | collective-permute-start | bytes 786440 | tf_op jit(solution)/shard_map/ppermute | solution.py:269

commit v3 on v2

--- a/solution.py
+++ b/solution.py
@@ -56,19 +56,28 @@
     return pl.ds(pl.multiple_of(parity(table, place) * BI, BI), BI)
 
 
-def opening(table, rhs, sent, held):
-    field = rhs[...]
-    held[...] = field
-    sums = jnp.sum(field * field, axis=0, keepdims=True)
+def opening(halo, rhs, sent, held, sems):
+    copies = [
+        pltpu.make_async_copy(rhs.at[pl.ds(i * 64, 64)], held.at[pl.ds(i * 64, 64)], sems.at[i])
+        for i in range(4)
+    ]
+    for copy in copies:
+        copy.start()
+    sums = jnp.zeros((1, COLS), F32)
+    for i, copy in enumerate(copies):
+        copy.wait()
+        field = held[i * 64 : (i + 1) * 64, :]
+        sums = sums + jnp.sum(field * field, axis=0, keepdims=True)
     row = lax.broadcasted_iota(jnp.int32, (8, COLS), 0)
-    left = parity(table, HALO).astype(F32)
-    right = parity(table, HALO + 1).astype(F32)
+    left = (halo[0, 0] & 1).astype(F32)
+    right = (halo[0, 1] & 1).astype(F32)
     tile = jnp.where(row == 0, sums, jnp.where(row == 1, left, jnp.where(row == 2, right, 0.0)))
     sent[...] = jnp.broadcast_to(tile[None], sent.shape)
 
 
-def bring_owned(precond, diag, precond_v, diag_v, sems):
+def bring_owned(rhs, precond, diag, rhs_v, precond_v, diag_v, sems):
     copies = [
+        pltpu.make_async_copy(rhs, rhs_v, sems.at[2]),
         pltpu.make_async_copy(precond, precond_v, sems.at[0]),
         pltpu.make_async_copy(diag, diag_v, sems.at[1]),
     ]
@@ -78,27 +87,22 @@
         copy.wait()
 
 
-def bring_couplings(table, after, couplings, coup_v, sems):
-    def copy(slot):
-        return pltpu.make_async_copy(couplings.at[slot], coup_v.at[slot], sems.at[slot])
-
-    copy(0).start()
-
-    @pl.when(table[LIVE] > 1)
-    def _():
-        copy(1).start()
-        copy(1).wait()
-
-    copy(0).wait()
+def bring_coupling(after, couplings, coup, sem):
+    copy = pltpu.make_async_copy(couplings.at[0], coup, sem)
+    copy.start()
+    copy.wait()
 
 
 def first_direction(
-    table, table_far, rhs, before, after, facts, precond, diag, sent, z_nat, base, basis, turned
+    table, table_far, rhs, paired, linked, facts, precond, diag, sent, z_nat, base, basis, turned
 ):
     beta = jnp.sqrt(jnp.sum(facts[:, 0:1, :], axis=0))
     v = rhs[...] / beta
-    left = before[block_at(table, HALO), :] / beta
-    right = after[block_at(table, HALO + 1), :] / beta
+    odd = (table[GROUP] & 1) == 1
+    lower = block_at(table, HALO)
+    upper = block_at(table, HALO + 1)
+    left = jnp.where(odd, paired[lower, :], linked[lower, :]) / beta
+    right = jnp.where(odd, linked[upper, :], paired[upper, :]) / beta
     patch = jnp.concatenate([v, left, right], axis=0).astype(BF16)
     z = v + dot(precond[...], patch)
     z_nat[...] = z
@@ -113,53 +117,74 @@
     basis[...] = turned[part, :]
 
 
-def slots(table, near, far, coup, factors, kept, given, fact, picked, one, two, sems):
-    live = table[LIVE]
-
-    def fetch(slot, n):
-        span = pl.ds(n * 256, 256)
-        return pltpu.make_async_copy(
-            factors.at[slot, span], fact.at[slot, span], sems.at[slot, n]
-        )
-
-    for n in range(4):
-        fetch(0, n).start()
-
-    @pl.when(live > 1)
+def slots(
+    table,
+    near,
+    far,
+    coup_a,
+    couplings,
+    factors,
+    kept,
+    given,
+    coup_b,
+    fact_a,
+    fact_b,
+    picked,
+    one,
+    two,
+    sems,
+):
+    spans = [pl.ds(n * 256, 256) for n in range(4)]
+    first = [
+        pltpu.make_async_copy(factors.at[0, span], fact_a.at[span], sems.at[n])
+        for n, span in enumerate(spans)
+    ]
+    second = [pltpu.make_async_copy(couplings.at[1], coup_b, sems.at[4])] + [
+        pltpu.make_async_copy(factors.at[1, span], fact_b.at[span], sems.at[5 + n])
+        for n, span in enumerate(spans)
+    ]
+    for copy in first:
+        copy.start()
+
+    @pl.when(table[LIVE] > 1)
     def _():
-        for n in range(4):
-            fetch(1, n).start()
-
-    @pl.when(live < 2)
-    def _():
-        kept[4:8] = jnp.zeros((4, HALF, BI), F32)
-        given[4:8] = jnp.zeros((4, HALF, BI), F32)
-
-    def step(slot, carry):
+        for copy in second:
+            copy.start()
+
+    def slot(number, coup, fact, copies):
         for j in range(4):
-            block = table[IDS + slot * 4 + j]
+            block = table[IDS + number * 4 + j]
             lanes = pl.ds(pl.multiple_of((block & 1) * BI, BI), BI)
             picked[0:HALF, j * BI : (j + 1) * BI] = near[block >> 1, :, lanes]
             picked[HALF:COLS, j * BI : (j + 1) * BI] = far[block >> 1, :, lanes]
         for n in range(4):
             span = slice(n * 256, (n + 1) * 256)
-            one[:, span] = dot(picked[...], coup[slot, span, :], NT).astype(BF16)
+            one[:, span] = dot(picked[...], coup[span, :], NT).astype(BF16)
         for n in range(4):
             span = slice(n * 256, (n + 1) * 256)
-            fetch(slot, n).wait()
-            two[:, span] = dot(one[...], fact[slot, span, :], NT).astype(BF16)
+            copies[n].wait()
+            two[:, span] = dot(one[...], fact[span, :], NT).astype(BF16)
         for n in range(4):
             span = slice(n * 256, (n + 1) * 256)
-            one[:, span] = dot(two[...], fact[slot, :, span]).astype(BF16)
+            one[:, span] = dot(two[...], fact[:, span]).astype(BF16)
         for n in range(2):
-            piece = dot(one[...], coup[slot, :, n * 256 : (n + 1) * 256])
+            piece = dot(one[...], coup[:, n * 256 : (n + 1) * 256])
             for m in range(2):
                 lanes = slice(m * BI, (m + 1) * BI)
-                kept[slot * 4 + n * 2 + m] = piece[0:HALF, lanes]
-                given[slot * 4 + n * 2 + m] = piece[HALF:COLS, lanes]
-        return carry
-
-    lax.fori_loop(0, live, step, 0)
+                kept[number * 4 + n * 2 + m] = piece[0:HALF, lanes]
+                given[number * 4 + n * 2 + m] = piece[HALF:COLS, lanes]
+
+    slot(0, coup_a, fact_a, first)
+
+    @pl.when(table[LIVE] > 1)
+    def _():
+        second[0].wait()
+        slot(1, coup_b, fact_b, second[1:])
+
+    @pl.when(table[LIVE] < 2)
+    def _():
+        kept[4:8] = jnp.zeros((4, HALF, BI), F32)
+        given[4:8] = jnp.zeros((4, HALF, BI), F32)
 
 
 def parcels(table, table_far, kept, got, facts, base, sent, total):
@@ -274,9 +299,9 @@
 
 
 def neighbours(array):
-    forward = lax.ppermute(array, SUB, [(i, (i + 1) % GROUPS) for i in range(GROUPS)])
-    backward = lax.ppermute(array, SUB, [((i + 1) % GROUPS, i) for i in range(GROUPS)])
-    return forward, backward
+    paired = lax.ppermute(array, SUB, [(i, i ^ 1) for i in range(GROUPS)])
+    linked = lax.ppermute(array, SUB, [(i, (i - 1 + 2 * (i & 1)) % GROUPS) for i in range(GROUPS)])
+    return paired, linked
 
 
 def on_device(rhs, schur_diag, precond, halo_ids, factors, couplings, block_ids, counts):
@@ -289,18 +314,20 @@
         return call(
             slots,
             [out((8, HALF, BI), F32), out((8, HALF, BI), F32)],
-            [SMEM, VMEM, VMEM, VMEM, HBM],
+            [SMEM] + [VMEM] * 3 + [HBM] * 2,
             [
-                pltpu.VMEM((2, 1024, 1024), BF16),
+                pltpu.VMEM((1024, 512), BF16),
+                pltpu.VMEM((1024, 1024), BF16),
+                pltpu.VMEM((1024, 1024), BF16),
                 pltpu.VMEM((COLS, 512), BF16),
                 pltpu.VMEM((COLS, 1024), BF16),
                 pltpu.VMEM((COLS, 1024), BF16),
-                pltpu.SemaphoreType.DMA((2, 4)),
+                pltpu.SemaphoreType.DMA((9,)),
             ],
             flops=2 * 805306368,
             moved=8 << 20,
-            room=50000 << 10,
-        )(table, near, far, coup_v, factors)
+            room=51000 << 10,
+        )(table, near, far, coupling, couplings, factors)
 
     def to_owners(kept, given, width):
         got = other_core(given)
@@ -312,17 +339,21 @@
         )(table, table_far, kept, got, facts, base)
         return swap_all(sent, XYZ)
 
-    opened, held = call(
-        opening, [out((GROUPS, 8, COLS), F32), out((ROWS, COLS), F32)], [SMEM, VMEM]
-    )(table, rhs)
+    paired, linked = neighbours(rhs)
+    (opened,) = call(
+        opening,
+        [out((GROUPS, 8, COLS), F32)],
+        [SMEM, HBM],
+        [pltpu.VMEM((ROWS, COLS), F32), pltpu.SemaphoreType.DMA((4,))],
+        room=67043328,
+    )(halo_ids, rhs)
     facts = swap_all(opened, SUB)
-    before, after = neighbours(held)
-    precond_v, diag_v = call(
+    rhs_v, precond_v, diag_v = call(
         bring_owned,
-        [out(a.shape, BF16) for a in (precond, schur_diag)],
-        [HBM, HBM],
-        [pltpu.SemaphoreType.DMA((2,))],
-    )(precond, schur_diag)
+        [out(rhs.shape, F32), out(precond.shape, BF16), out(schur_diag.shape, BF16)],
+        [HBM, HBM, HBM],
+        [pltpu.SemaphoreType.DMA((3,))],
+    )(rhs, precond, schur_diag)
     sent, z_one, base, basis = call(
         first_direction,
         [
@@ -334,14 +365,14 @@
         [SMEM, SMEM, VMEM, VMEM, VMEM, VMEM, VMEM, VMEM],
         [pltpu.VMEM((COLS, ROWS), F32)],
         flops=1 << 26,
-    )(table, table_far, held, before, after, facts, precond_v, diag_v)
-    (coup_v,) = call(
-        bring_couplings,
-        [out(couplings.shape, BF16)],
-        [SMEM, ANY, HBM],
-        [pltpu.SemaphoreType.DMA((2,))],
+    )(table, table_far, rhs_v, paired, linked, facts, precond_v, diag_v)
+    (coupling,) = call(
+        bring_coupling,
+        [out((1024, 512), BF16)],
+        [ANY, HBM],
+        [pltpu.SemaphoreType.DMA],
         moved=12 << 20,
-    )(table, base, couplings)
+    )(base, couplings)
     near = swap_all(sent, SUB)
     far = other_core(near)
     kept, given = apply_slots(near, far)

time: 142 us -> 142 us (level)
  waiting for transfers between devices: 13.2 us -> 9 us
  blocking collectives: 89.9 us -> 93.2 us
  starting transfers between devices: 12.3 us -> 9.78 us
  local copies, waits for them, and re-layouts: 4.26 us -> 5.84 us
    all_to_all x5, blocking collectives: 89.9 us -> 93.2 us  [swap_all(): return lax.all_to_all(array, axes, split_axis=0, concat_axis=0, tiled=True)]
    all_to_all x1, starting transfers between devices: 6.72 us -> 3.51 us  [swap_all(): return lax.all_to_all(array, axes, split_axis=0, concat_axis=0, tiled=True)]
    all_to_all x1, waiting for transfers between devices: 5.49 us -> 2.29 us  [swap_all(): return lax.all_to_all(array, axes, split_axis=0, concat_axis=0, tiled=True)]
    unnamed x8, local copies, waits for them, and re-layouts: 2.76 us -> 4.34 us
  transfers between devices with their start and end apart: 9 -> 9, of which waited for: 6 -> 6; matrix products, arithmetic and copies ran while one was open for 0% -> 1% of each run, Pallas kernels for 1% -> 2%
where the time goes in v3:
time: 142 us; the launch traced here: 140 us
  blocking collectives  93.2 us (66%)
  Pallas kernels  21.5 us (15%)
  starting transfers between devices  9.78 us (7%)
  waiting for transfers between devices  9 us (6%)
  local copies, waits for them, and re-layouts  5.84 us (4%)
    all_to_all x5, blocking collectives, swap_all(): return lax.all_to_all(array, axes, split_axis=0, concat_axis=0, tiled=True)  93.2 us
    pallas_call x2, Pallas kernels, apply_slots(): call(slots, [out((8, HALF, BI), F32), out((8, HALF, BI), F32)], [SMEM] +...  13 us
    ppermute x6, waiting for transfers between devices, other_core(): return lax.ppermute(array, 'c', [(0, 1), (1, 0)])  6.7 us
    ppermute x1, starting transfers between devices, neighbours(): lax.ppermute(array, SUB, [(i, (i - 1 + 2 * (i & 1)) % GROUPS) for i in ra...  4.38 us
    unnamed x8, local copies, waits for them, and re-layouts  4.34 us
    all_to_all x1, starting transfers between devices, swap_all(): return lax.all_to_all(array, axes, split_axis=0, concat_axis=0, tiled=True)  3.51 us
  transfers between devices with their start and end apart: 9, of which 6 were waited for; matrix products, arithmetic and copies ran while one was open for 1% of the time, Pallas kernels for 2%

profile of v3, /device:TPU:0, one launch (start us, length us, event | category | flops | bytes accessed | tf_op | source)
XLA Modules:
  0.0 140.2 jit_solution(9792733532436430916)
XLA Ops:
  0.0 1.7 %collective-permute-start.1 = (f32[256,128]{1,0:T(8,128)}, f32[256,128]{1,0:T(8,128)}, u32[]{:S(2)}, u32[]{:S(2)}) collective-permute-start(f32[256,128]{1,0:T(8,128)} %rhs.3), channel_id=1, source_target_pairs={{0,8},{8,0},{16,24},{24,16},{32,40},{40,32},{48,56},{56,48},{64,72... | collective-permute-start | bytes 393224 | tf_op jit(solution)/shard_map/ppermute | solution.py:302
  1.7 4.4 %collective-permute-start.2 = (f32[256,128]{1,0:T(8,128)}, f32[256,128]{1,0:T(8,128)}, u32[]{:S(2)}, u32[]{:S(2)}) collective-permute-start(f32[256,128]{1,0:T(8,128)} %rhs.3), channel_id=1, source_target_pairs={{0,120},{8,16},{16,8},{24,32},{32,24},{40,48},{48,40},{56,64},{64,... | collective-permute-start | bytes 393224 | tf_op jit(solution)/shard_map/ppermute | solution.py:303
  6.1 2.2 %shard_map.83 = f32[16,8,128]{2,1,0:T(8,128)} custom-call(s32[1,2]{1,0:T(1,128)} %halo.1, f32[256,128]{1,0:T(8,128)} %rhs.3), custom_call_target="tpu_custom_call" | custom-call | bytes 1048576 | tf_op jit(solution)/shard_map/pallas_call | solution.py:343
  8.2 3.5 %all-to-all-start = ((f32[16,8,128]{2,1,0:T(8,128)}), f32[16,8,128]{2,1,0:T(8,128)S(1)}, u32[]{:S(2)}, u32[]{:S(2)}) async-start(f32[16,8,128]{2,1,0:T(8,128)} %shard_map.83), calls=%async_computation | async-start | bytes 131072 | tf_op jit(solution)/shard_map/all_to_all | solution.py:298
  12.4 0.8 reshape.10
  13.2 0.7 concatenate.3.table
  13.9 0.9 copy-done.1
  14.8 0.9 copy-done.2
  15.8 0.9 copy-done.3
  16.7 0.4 shard_map.82
  17.1 2.3 %all-to-all-done.facts = f32[16,8,128]{2,1,0:T(8,128)S(1)} async-done(((f32[16,8,128]{2,1,0:T(8,128)}), f32[16,8,128]{2,1,0:T(8,128)S(1)}, u32[]{:S(2)}, u32[]{:S(2)}) %all-to-all-start) | async-done | bytes 65568 | tf_op jit(solution)/shard_map/all_to_all | solution.py:298
  19.4 1.6 %shard_map.84 = (bf16[16,64,256]{2,1,0:T(8,128)(2,1)S(1)}, f32[256,128]{1,0:T(8,128)S(1)}, f32[16,256]{1,0:T(8,128)S(1)}, f32[16,256]{1,0:T(8,128)S(1)}) custom-call(s32[14]{0:T(128)S(1)} %concatenate.3.table, s32[14]{0:T(128)S(1)} %collective-permute-done.table_far, f32[256,128]{1,0:T(8,128)S(1)} %get-tuple-element.19.rhs, ...), custom_call_target="tpu_custom_call" | custom-call | flops 67108864 | bytes 1048576 | tf_op jit(solution)/shard_map/pallas_call | solution.py:357
  20.9 16.8 %all_to_all.30.near = bf16[16,64,256]{2,1,0:T(8,128)(2,1)S(1)} all-to-all(bf16[16,64,256]{2,1,0:T(8,128)(2,1)S(1)} %get-tuple-element.22), channel_id=1, replica_groups=mesh['x'=4,'y'=4,'z'=4,'c'=2] {'x','y'}, dimensions={0} | all-to-all | bytes 1048576 | tf_op jit(solution)/shard_map/all_to_all | solution.py:298
  37.8 1.6 %copy-done = bf16[2,1024,512]{2,1,0:T(8,128)(2,1)S(1)} copy-done((bf16[2,1024,512]{2,1,0:T(8,128)(2,1)S(1)}, bf16[2,1024,512]{2,1,0:T(8,128)(2,1)}, u32[]{:S(2)}) %copy-start) | copy-done | bytes 2097176
  39.5 0.2 collective-permute-done.3.far
  39.7 6.5 %shard_map.86 = (f32[8,64,128]{2,1,0:T(8,128)S(1)}, f32[8,64,128]{2,1,0:T(8,128)S(1)}) custom-call(s32[14]{0:T(128)S(1)} %concatenate.3.table, bf16[16,64,256]{2,1,0:T(8,128)(2,1)S(1)} %all_to_all.30.near, bf16[16,64,256]{2,1,0:T(8,128)(2,1)S(1)} %collective-permute-done.3.far, bf16[1024,512]{1,0:T(8,128)(2,1)S(1)} %shard_map.85.coup_a, ...), custom_call_target="tpu_custom_call" | custom-call | flops 1610612736 | bytes 8388608 | tf_op jit(solution)/shard_map/pallas_call | solution.py:314
  46.2 0.1 collective-permute-start.4
  46.3 1.5 %collective-permute-done.4.got = f32[8,64,128]{2,1,0:T(8,128)S(1)} collective-permute-done((f32[8,64,128]{2,1,0:T(8,128)S(1)}, f32[8,64,128]{2,1,0:T(8,128)S(1)}, u32[]{:S(2)}, u32[]{:S(2)}) %collective-permute-start.4) | collective-permute-done | bytes 262176 | tf_op jit(solution)/shard_map/ppermute | solution.py:294
  47.8 1.0 shard_map.87
  48.8 26.5 %all_to_all.31.arrived = bf16[64,16,512]{2,1,0:T(8,128)(2,1)S(1)} all-to-all(bf16[64,16,512]{2,1,0:T(8,128)(2,1)S(1)} %shard_map.87), channel_id=1, replica_groups=mesh['x'=4,'y'=4,'z'=4,'c'=2] {'x','y','z'}, dimensions={0} | all-to-all | bytes 2097152 | tf_op jit(solution)/shard_map/all_to_all | solution.py:298
  75.2 0.5 shard_map.88
  75.8 16.7 %all_to_all.32 = bf16[64,16,256]{2,1,0:T(8,128)(2,1)S(1)} all-to-all(bf16[64,16,256]{2,1,0:T(8,128)(2,1)S(1)} %get-tuple-element.26), channel_id=1, replica_groups=mesh['x'=4,'y'=4,'z'=4,'c'=2] {'x','y','z'}, dimensions={0} | all-to-all | bytes 1048576 | tf_op jit(solution)/shard_map/all_to_all | solution.py:298
  92.5 1.9 %collective-permute-done.5.far = bf16[16,64,256]{2,1,0:T(8,128)(2,1)S(1)} collective-permute-done((bf16[16,64,256]{2,1,0:T(8,128)(2,1)S(1)}, bf16[16,64,256]{2,1,0:T(8,128)(2,1)S(1)}, u32[]{:S(2)}, u32[]{:S(2)}) %collective-permute-start.5) | collective-permute-done | bytes 524320 | tf_op jit(solution)/shard_map/ppermute | solution.py:294
  94.4 6.5 %shard_map.89 = (f32[8,64,128]{2,1,0:T(8,128)S(1)}, f32[8,64,128]{2,1,0:T(8,128)S(1)}) custom-call(s32[14]{0:T(128)S(1)} %concatenate.3.table, bf16[16,64,256]{2,1,0:T(8,128)(2,1)S(1)} %bitcast.6, bf16[16,64,256]{2,1,0:T(8,128)(2,1)S(1)} %collective-permute-done.5.far, bf16[1024,512]{1,0:T(8,128)(2,1)S(1)} %shard_map.85.coup_a, ...), custom_call_target="tpu_custom_call" | custom-call | flops 1610612736 | bytes 8388608 | tf_op jit(solution)/shard_map/pallas_call | solution.py:314
  100.9 0.1 collective-permute-start.6
  101.0 1.5 %collective-permute-done.6.got = f32[8,64,128]{2,1,0:T(8,128)S(1)} collective-permute-done((f32[8,64,128]{2,1,0:T(8,128)S(1)}, f32[8,64,128]{2,1,0:T(8,128)S(1)}, u32[]{:S(2)}, u32[]{:S(2)}) %collective-permute-start.6) | collective-permute-done | bytes 262176 | tf_op jit(solution)/shard_map/ppermute | solution.py:294
  102.5 0.8 shard_map.90
  103.3 18.1 %all_to_all.33.arrived = bf16[64,16,256]{2,1,0:T(8,128)(2,1)S(1)} all-to-all(bf16[64,16,256]{2,1,0:T(8,128)(2,1)S(1)} %shard_map.90), channel_id=1, replica_groups=mesh['x'=4,'y'=4,'z'=4,'c'=2] {'x','y','z'}, dimensions={0} | all-to-all | bytes 1048576 | tf_op jit(solution)/shard_map/all_to_all | solution.py:298
  121.4 0.7 shard_map.91
  122.2 15.1 %all_to_all.34.near = f32[64,8,128]{2,1,0:T(8,128)S(1)} all-to-all(f32[64,8,128]{2,1,0:T(8,128)S(1)} %shard_map.91), channel_id=1, replica_groups=mesh['x'=4,'y'=4,'z'=4,'c'=2] {'x','y','z'}, dimensions={0} | all-to-all | bytes 524288 | tf_op jit(solution)/shard_map/all_to_all | solution.py:298
  137.3 1.5 %collective-permute-done.7.far = f32[64,8,128]{2,1,0:T(8,128)S(1)} collective-permute-done((f32[64,8,128]{2,1,0:T(8,128)S(1)}, f32[64,8,128]{2,1,0:T(8,128)S(1)}, u32[]{:S(2)}, u32[]{:S(2)}) %collective-permute-start.7) | collective-permute-done | bytes 262176 | tf_op jit(solution)/shard_map/ppermute | solution.py:294
  138.8 1.3 shard_map.92
  (14 shorter events, 0.1 us)
Async XLA Ops:
  0.0 19.4 %collective-permute-start.1 = (f32[256,128]{1,0:T(8,128)}, f32[256,128]{1,0:T(8,128)}, u32[]{:S(2)}, u32[]{:S(2)}) collective-permute-start(f32[256,128]{1,0:T(8,128)} %rhs.3), channel_id=1, source_target_pairs={{0,8},{8,0},{16,24},{24,16},{32,40},{40,32},{48,56},{56,48},{64,72... | collective-permute-start | bytes 393224 | tf_op jit(solution)/shard_map/ppermute | solution.py:302
  1.7 17.7 %collective-permute-start.2 = (f32[256,128]{1,0:T(8,128)}, f32[256,128]{1,0:T(8,128)}, u32[]{:S(2)}, u32[]{:S(2)}) collective-permute-start(f32[256,128]{1,0:T(8,128)} %rhs.3), channel_id=1, source_target_pairs={{0,120},{8,16},{16,8},{24,32},{32,24},{40,48},{48,40},{56,64},{64,... | collective-permute-start | bytes 393224 | tf_op jit(solution)/shard_map/ppermute | solution.py:303
  8.2 11.1 %all-to-all-start = ((f32[16,8,128]{2,1,0:T(8,128)}), f32[16,8,128]{2,1,0:T(8,128)S(1)}, u32[]{:S(2)}, u32[]{:S(2)}) async-start(f32[16,8,128]{2,1,0:T(8,128)} %shard_map.83), calls=%async_computation | async-start | bytes 131072 | tf_op jit(solution)/shard_map/all_to_all | solution.py:298
  13.9 3.2 %collective-permute-start = (s32[14]{0:T(128)S(1)}, s32[14]{0:T(128)S(1)}, u32[]{:S(2)}, u32[]{:S(2)}) collective-permute-start(s32[14]{0:T(128)S(1)} %concatenate.3.table), channel_id=1, source_target_pairs={{0,1},{1,0},{2,3},{3,2},{4,5},{5,4},{6,7},{7,6},{8,9},{9,8},{10,11... | collective-permute-start | bytes 176 | tf_op jit(solution)/shard_map/ppermute | solution.py:294
  13.9 0.9 copy-start.1
  14.8 0.9 copy-start.2
  15.8 0.9 copy-start.3
  37.8 1.9 %collective-permute-start.3 = (bf16[16,64,256]{2,1,0:T(8,128)(2,1)S(1)}, bf16[16,64,256]{2,1,0:T(8,128)(2,1)S(1)}, u32[]{:S(2)}, u32[]{:S(2)}) collective-permute-start(bf16[16,64,256]{2,1,0:T(8,128)(2,1)S(1)} %all_to_all.30.near), channel_id=1, source_target_pairs={{0,1},{1,0},{2,3},{3,2},{4,5},{5,4},{6,7},{7,6},{8,9},{9,8},{10,11... | collective-permute-start | bytes 1572872 | tf_op jit(solution)/shard_map/ppermute | solution.py:294
  37.8 1.6 %copy-start = (bf16[2,1024,512]{2,1,0:T(8,128)(2,1)S(1)}, bf16[2,1024,512]{2,1,0:T(8,128)(2,1)}, u32[]{:S(2)}) copy-start(bf16[2,1024,512]{2,1,0:T(8,128)(2,1)} %couplings.5) | copy-start | bytes 6291460
  46.2 1.6 %collective-permute-start.4 = (f32[8,64,128]{2,1,0:T(8,128)S(1)}, f32[8,64,128]{2,1,0:T(8,128)S(1)}, u32[]{:S(2)}, u32[]{:S(2)}) collective-permute-start(f32[8,64,128]{2,1,0:T(8,128)S(1)} %get-tuple-element.25), channel_id=1, source_target_pairs={{0,1},{1,0},{2,3},{3,2},{4,5},{5,4},{6,7},{7,6},{8,9},{9,8},{10,11... | collective-permute-start | bytes 786440 | tf_op jit(solution)/shard_map/ppermute | solution.py:294
  92.5 1.9 %collective-permute-start.5 = (bf16[16,64,256]{2,1,0:T(8,128)(2,1)S(1)}, bf16[16,64,256]{2,1,0:T(8,128)(2,1)S(1)}, u32[]{:S(2)}, u32[]{:S(2)}) collective-permute-start(bf16[16,64,256]{2,1,0:T(8,128)(2,1)S(1)} %bitcast.5), channel_id=1, source_target_pairs={{0,1},{1,0},{2,3},{3,2},{4,5},{5,4},{6,7},{7,6},{8,9},{9,8},{10,11... | collective-permute-start | bytes 1572872 | tf_op jit(solution)/shard_map/ppermute | solution.py:294
  100.9 1.6 %collective-permute-start.6 = (f32[8,64,128]{2,1,0:T(8,128)S(1)}, f32[8,64,128]{2,1,0:T(8,128)S(1)}, u32[]{:S(2)}, u32[]{:S(2)}) collective-permute-start(f32[8,64,128]{2,1,0:T(8,128)S(1)} %get-tuple-element.28), channel_id=1, source_target_pairs={{0,1},{1,0},{2,3},{3,2},{4,5},{5,4},{6,7},{7,6},{8,9},{9,8},{10,11... | collective-permute-start | bytes 786440 | tf_op jit(solution)/shard_map/ppermute | solution.py:294
  137.3 1.5 %collective-permute-start.7 = (f32[64,8,128]{2,1,0:T(8,128)S(1)}, f32[64,8,128]{2,1,0:T(8,128)S(1)}, u32[]{:S(2)}, u32[]{:S(2)}) collective-permute-start(f32[64,8,128]{2,1,0:T(8,128)S(1)} %all_to_all.34.near), channel_id=1, source_target_pairs={{0,1},{1,0},{2,3},{3,2},{4,5},{5,4},{6,7},{7,6},{8,9},{9,8},{10,11... | collective-permute-start | bytes 786440 | tf_op jit(solution)/shard_map/ppermute | solution.py:294

commit v4 on v3

--- a/solution.py
+++ b/solution.py
@@ -14,7 +14,8 @@
 GROUPS = 16
 BLOCKS = 32
 SUB = ("x", "y")
-XYZ = ("x", "y", "z")
+YX = ("y", "x")
+YXZ = ("y", "x", "z")
 ALL = ("x", "y", "z", "c")
 F32 = jnp.float32
 BF16 = jnp.bfloat16
@@ -32,9 +33,10 @@
     return lax.dot_general(left, right, dims, preferred_element_type=F32)
 
 
-def call(body, outs, specs, scratch=(), flops=0, moved=1 << 20, room=4 << 20):
+def call(body, name, outs, specs, scratch=(), flops=0, moved=1 << 20, room=4 << 20):
     return pl.pallas_call(
         body,
+        name=name,
         out_shape=outs,
         in_specs=specs,
         out_specs=[VMEM] * len(outs),
@@ -48,26 +50,18 @@
     return jax.ShapeDtypeStruct(shape, dtype)
 
 
-def parity(table, place):
-    return table[place] & 1
+def partner(group):
+    return ((group & 3) << 2) | (group >> 2)
 
 
 def block_at(table, place):
-    return pl.ds(pl.multiple_of(parity(table, place) * BI, BI), BI)
-
-
-def opening(halo, rhs, sent, held, sems):
-    copies = [
-        pltpu.make_async_copy(rhs.at[pl.ds(i * 64, 64)], held.at[pl.ds(i * 64, 64)], sems.at[i])
-        for i in range(4)
-    ]
-    for copy in copies:
-        copy.start()
-    sums = jnp.zeros((1, COLS), F32)
-    for i, copy in enumerate(copies):
-        copy.wait()
-        field = held[i * 64 : (i + 1) * 64, :]
-        sums = sums + jnp.sum(field * field, axis=0, keepdims=True)
+    return pl.ds(pl.multiple_of((table[place] & 1) * BI, BI), BI)
+
+
+def opening(halo, rhs, sent, held):
+    field = rhs[...]
+    held[...] = field
+    sums = jnp.sum(field * field, axis=0, keepdims=True)
     row = lax.broadcasted_iota(jnp.int32, (8, COLS), 0)
     left = (halo[0, 0] & 1).astype(F32)
     right = (halo[0, 1] & 1).astype(F32)
@@ -75,9 +69,8 @@
     sent[...] = jnp.broadcast_to(tile[None], sent.shape)
 
 
-def bring_owned(rhs, precond, diag, rhs_v, precond_v, diag_v, sems):
+def bring_owned(precond, diag, precond_v, diag_v, sems):
     copies = [
-        pltpu.make_async_copy(rhs, rhs_v, sems.at[2]),
         pltpu.make_async_copy(precond, precond_v, sems.at[0]),
         pltpu.make_async_copy(diag, diag_v, sems.at[1]),
     ]
@@ -87,7 +80,7 @@
         copy.wait()
 
 
-def bring_coupling(after, couplings, coup, sem):
+def bring_coupling(couplings, coup, sem):
     copy = pltpu.make_async_copy(couplings.at[0], coup, sem)
     copy.start()
     copy.wait()
@@ -134,35 +127,31 @@
     two,
     sems,
 ):
-    spans = [pl.ds(n * 256, 256) for n in range(4)]
-    first = [
-        pltpu.make_async_copy(factors.at[0, span], fact_a.at[span], sems.at[n])
-        for n, span in enumerate(spans)
+    first = pltpu.make_async_copy(factors.at[0], fact_a, sems.at[0])
+    second = [
+        pltpu.make_async_copy(couplings.at[1], coup_b, sems.at[1]),
+        pltpu.make_async_copy(factors.at[1], fact_b, sems.at[2]),
     ]
-    second = [pltpu.make_async_copy(couplings.at[1], coup_b, sems.at[4])] + [
-        pltpu.make_async_copy(factors.at[1, span], fact_b.at[span], sems.at[5 + n])
-        for n, span in enumerate(spans)
-    ]
-    for copy in first:
-        copy.start()
+    first.start()
 
     @pl.when(table[LIVE] > 1)
     def _():
         for copy in second:
             copy.start()
 
-    def slot(number, coup, fact, copies):
+    def slot(number, coup, fact, copy):
         for j in range(4):
             block = table[IDS + number * 4 + j]
+            place = partner(block >> 1)
             lanes = pl.ds(pl.multiple_of((block & 1) * BI, BI), BI)
-            picked[0:HALF, j * BI : (j + 1) * BI] = near[block >> 1, :, lanes]
-            picked[HALF:COLS, j * BI : (j + 1) * BI] = far[block >> 1, :, lanes]
+            picked[0:HALF, j * BI : (j + 1) * BI] = near[place, :, lanes]
+            picked[HALF:COLS, j * BI : (j + 1) * BI] = far[place, :, lanes]
         for n in range(4):
             span = slice(n * 256, (n + 1) * 256)
             one[:, span] = dot(picked[...], coup[span, :], NT).astype(BF16)
+        copy.wait()
         for n in range(4):
             span = slice(n * 256, (n + 1) * 256)
-            copies[n].wait()
             two[:, span] = dot(one[...], fact[span, :], NT).astype(BF16)
         for n in range(4):
             span = slice(n * 256, (n + 1) * 256)
@@ -179,7 +168,7 @@
     @pl.when(table[LIVE] > 1)
     def _():
         second[0].wait()
-        slot(1, coup_b, fact_b, second[1:])
+        slot(1, coup_b, fact_b, second[1])
 
     @pl.when(table[LIVE] < 2)
     def _():
@@ -198,18 +187,19 @@
     with_halo = sent.shape[2] > ROWS
 
     def group(d, carry):
+        place = partner(d)
         lower = 2 * ((d + GROUPS - 1) & (GROUPS - 1))
         upper = 2 * ((d + 1) & (GROUPS - 1))
         blocks = [total[2 * d], total[2 * d + 1]]
         if with_halo:
-            left = facts[d, 1:2, :] > 0.5
-            right = facts[d, 2:3, :] > 0.5
+            left = facts[place, 1:2, :] > 0.5
+            right = facts[place, 2:3, :] > 0.5
             blocks.append(jnp.where(left, total[lower + 1], total[lower]))
             blocks.append(jnp.where(right, total[upper + 1], total[upper]))
         for j, block in enumerate(blocks):
             low = block.astype(BF16)
             for z in range(4):
-                sent[d * 4 + z, :, j * BI : (j + 1) * BI] = low[z * PART : (z + 1) * PART]
+                sent[place * 4 + z, :, j * BI : (j + 1) * BI] = low[z * PART : (z + 1) * PART]
         return carry
 
     lax.fori_loop(0, GROUPS, group, 0)
@@ -218,7 +208,7 @@
         depth = table[DEPTH]
         part = pl.ds(pl.multiple_of(depth * PART, PART), PART)
         for side, other in ((0, mine + 1), (1, mine + GROUPS - 1)):
-            other = other & (GROUPS - 1)
+            other = partner(other & (GROUPS - 1))
             upper = facts[other, side + 1 : side + 2, :] > 0.5
             block = jnp.where(upper, total[2 * mine + 1, part, :], total[2 * mine, part, :])
             stays = jnp.where(upper, base[:, BI:], base[:, :BI])
@@ -313,6 +303,7 @@
     def apply_slots(near, far):
         return call(
             slots,
+            "slots",
             [out((8, HALF, BI), F32), out((8, HALF, BI), F32)],
             [SMEM] + [VMEM] * 3 + [HBM] * 2,
             [
@@ -322,7 +313,7 @@
                 pltpu.VMEM((COLS, 512), BF16),
                 pltpu.VMEM((COLS, 1024), BF16),
                 pltpu.VMEM((COLS, 1024), BF16),
-                pltpu.SemaphoreType.DMA((9,)),
+                pltpu.SemaphoreType.DMA((3,)),
             ],
             flops=2 * 805306368,
             moved=8 << 20,
@@ -333,29 +324,38 @@
         got = other_core(given)
         (sent,) = call(
             parcels,
+            "parcels",
             [out((64, PART, width), BF16)],
             [SMEM, SMEM, VMEM, VMEM, VMEM, VMEM],
             [pltpu.VMEM((BLOCKS, HALF, BI), F32)],
         )(table, table_far, kept, got, facts, base)
-        return swap_all(sent, XYZ)
+        return swap_all(sent, YXZ)
 
     paired, linked = neighbours(rhs)
-    (opened,) = call(
+    opened, held = call(
         opening,
-        [out((GROUPS, 8, COLS), F32)],
-        [SMEM, HBM],
-        [pltpu.VMEM((ROWS, COLS), F32), pltpu.SemaphoreType.DMA((4,))],
-        room=67043328,
+        "opening",
+        [out((GROUPS, 8, COLS), F32), out((ROWS, COLS), F32)],
+        [SMEM, VMEM],
     )(halo_ids, rhs)
-    facts = swap_all(opened, SUB)
-    rhs_v, precond_v, diag_v = call(
+    facts = swap_all(opened, YX)
+    precond_v, diag_v = call(
         bring_owned,
-        [out(rhs.shape, F32), out(precond.shape, BF16), out(schur_diag.shape, BF16)],
-        [HBM, HBM, HBM],
-        [pltpu.SemaphoreType.DMA((3,))],
-    )(rhs, precond, schur_diag)
+        "bring_owned",
+        [out(precond.shape, BF16), out(schur_diag.shape, BF16)],
+        [HBM, HBM],
+        [pltpu.SemaphoreType.DMA((2,))],
+    )(precond, schur_diag)
+    (coupling,) = call(
+        bring_coupling,
+        "bring_coupling",
+        [out((1024, 512), BF16)],
+        [HBM],
+        [pltpu.SemaphoreType.DMA],
+    )(couplings)
     sent, z_one, base, basis = call(
         first_direction,
+        "first_direction",
         [
             out((GROUPS, HALF, ROWS), BF16),
             out((ROWS, COLS), F32),
@@ -365,36 +365,30 @@
         [SMEM, SMEM, VMEM, VMEM, VMEM, VMEM, VMEM, VMEM],
         [pltpu.VMEM((COLS, ROWS), F32)],
         flops=1 << 26,
-    )(table, table_far, rhs_v, paired, linked, facts, precond_v, diag_v)
-    (coupling,) = call(
-        bring_coupling,
-        [out((1024, 512), BF16)],
-        [ANY, HBM],
-        [pltpu.SemaphoreType.DMA],
-        moved=12 << 20,
-    )(base, couplings)
-    near = swap_all(sent, SUB)
+    )(table, table_far, held, paired, linked, facts, precond_v, diag_v)
+    near = swap_all(sent, YX)
     far = other_core(near)
     kept, given = apply_slots(near, far)
     arrived = to_owners(kept, given, 2 * ROWS)
     sent, base, w = call(
         second_direction,
+        "second_direction",
         [out((64, PART, ROWS), BF16), out((PART, ROWS), F32), out((PART, ROWS), F32)],
         [VMEM, VMEM, VMEM, VMEM],
         flops=1 << 26,
     )(arrived, base, precond_v, diag_v)
-    near = swap_all(sent, XYZ).reshape(GROUPS, HALF, ROWS)
+    near = swap_all(sent, YXZ).reshape(GROUPS, HALF, ROWS)
     far = other_core(near)
     kept, given = apply_slots(near, far)
     arrived = to_owners(kept, given, ROWS)
     (sent,) = call(
-        products, [out((64, 8, COLS), F32)], [SMEM, VMEM, VMEM, VMEM, VMEM]
+        products, "products", [out((64, 8, COLS), F32)], [SMEM, VMEM, VMEM, VMEM, VMEM]
     )(table, arrived, base, w, basis)
-    sums = swap_all(sent, XYZ)
+    sums = swap_all(sent, YXZ)
     sums_far = other_core(sums)
-    own = [lax.dynamic_slice_in_dim(half, group, 1, 0) for half in (near, far)]
+    own = [lax.dynamic_slice_in_dim(half, partner(group), 1, 0) for half in (near, far)]
     (answer,) = call(
-        closing, [out((ROWS, COLS), F32)], [SMEM] + [VMEM] * 6
+        closing, "closing", [out((ROWS, COLS), F32)], [SMEM] + [VMEM] * 6
     )(table, sums, sums_far, facts, z_one, *own)
     return answer
 
@@ -411,7 +405,6 @@
         P(ALL, None),
         P(ALL),
     )
-
     return jax.shard_map(
         on_device, mesh=torus, in_specs=placed, out_specs=P(SUB, None), check_vma=False
     )

time: 142 us -> 138 us (0.972)
  Pallas kernels: 21.5 us -> 14 us
  starting transfers between devices: 9.78 us -> 13.4 us
    pallas_call x11, Pallas kernels: 21.5 us -> 14 us  [the longest x2 7.02 us: apply_slots(): call(slots, 'slots', [out((8, HALF, BI), F32), out((8, HALF, BI), F32)],...]
    ppermute x6, starting transfers between devices: 0.2 us -> 4.14 us  [other_core(): return lax.ppermute(array, 'c', [(0, 1), (1, 0)])]
    ppermute x1, starting transfers between devices: 1.69 us -> 0.01 us  [neighbours(): paired = lax.ppermute(array, SUB, [(i, i ^ 1) for i in range(GROUPS)])]
    unnamed x8 -> x10, local copies, waits for them, and re-layouts: 4.34 us -> 5.06 us
  transfers between devices with their start and end apart: 9 -> 9, of which waited for: 6 -> 6; matrix products, arithmetic and copies ran while one was open for 1% -> 1% of each run, Pallas kernels for 2% -> 1%
where the time goes in v4:
time: 138 us; the launch traced here: 136 us
  blocking collectives  92 us (67%)
  Pallas kernels  14 us (10%)
  starting transfers between devices  13.4 us (10%)
  waiting for transfers between devices  9.4 us (7%)
  local copies, waits for them, and re-layouts  6.57 us (5%)
    all_to_all x5, blocking collectives, swap_all(): return lax.all_to_all(array, axes, split_axis=0, concat_axis=0, tiled=True)  92 us
    pallas_call x2, Pallas kernels, apply_slots(): call(slots, 'slots', [out((8, HALF, BI), F32), out((8, HALF, BI), F32)],...  7.02 us
    ppermute x6, waiting for transfers between devices, other_core(): return lax.ppermute(array, 'c', [(0, 1), (1, 0)])  5.98 us
    ppermute x1, starting transfers between devices, neighbours(): lax.ppermute(array, SUB, [(i, (i - 1 + 2 * (i & 1)) % GROUPS) for i in ra...  5.32 us
    unnamed x10, local copies, waits for them, and re-layouts  5.06 us
    ppermute x6, starting transfers between devices, other_core(): return lax.ppermute(array, 'c', [(0, 1), (1, 0)])  4.14 us
    all_to_all x1, starting transfers between devices, swap_all(): return lax.all_to_all(array, axes, split_axis=0, concat_axis=0, tiled=True)  3.93 us
    all_to_all x1, waiting for transfers between devices, swap_all(): return lax.all_to_all(array, axes, split_axis=0, concat_axis=0, tiled=True)  3.41 us
  transfers between devices with their start and end apart: 9, of which 6 were waited for; matrix products, arithmetic and copies ran while one was open for 1% of the time, Pallas kernels for 1%

profile of v4, /device:TPU:0, one launch (start us, length us, event | category | flops | bytes accessed | tf_op | source)
XLA Modules:
  0.0 136.1 jit_solution(909415853485830938)
XLA Ops:
  0.0 5.3 %collective-permute-start.2 = (f32[256,128]{1,0:T(8,128)}, f32[256,128]{1,0:T(8,128)S(1)}, u32[]{:S(2)}, u32[]{:S(2)}) collective-permute-start(f32[256,128]{1,0:T(8,128)} %rhs.1), channel_id=1, source_target_pairs={{0,120},{8,16},{16,8},{24,32},{32,24},{40,48},{48,40},{56,64},{64,... | collective-permute-start | bytes 393224 | tf_op jit(solution)/shard_map/ppermute | solution.py:293
  5.3 1.0 copy-done.3
  6.3 0.7 copy-done.4
  7.0 1.2 opening.1
  8.2 3.9 %all-to-all-start = ((f32[16,8,128]{2,1,0:T(8,128)}), f32[16,8,128]{2,1,0:T(8,128)S(1)}, u32[]{:S(2)}, u32[]{:S(2)}) async-start(f32[16,8,128]{2,1,0:T(8,128)} %get-tuple-element.21), calls=%async_computation | async-start | bytes 131072 | tf_op jit(solution)/shard_map/all_to_all | solution.py:288
  12.8 0.8 reshape.10
  13.5 0.7 concatenate.3.table
  14.3 0.9 copy-done.1
  15.2 0.9 copy-done.2
  16.1 0.2 bring_owned.1
  16.4 3.4 %all-to-all-done.facts = f32[16,8,128]{2,1,0:T(8,128)S(1)} async-done(((f32[16,8,128]{2,1,0:T(8,128)}), f32[16,8,128]{2,1,0:T(8,128)S(1)}, u32[]{:S(2)}, u32[]{:S(2)}) %all-to-all-start) | async-done | bytes 65568 | tf_op jit(solution)/shard_map/all_to_all | solution.py:288
  19.8 1.1 first_direction.1
  20.9 15.8 %all_to_all.30.near = bf16[16,64,256]{2,1,0:T(8,128)(2,1)S(1)} all-to-all(bf16[16,64,256]{2,1,0:T(8,128)(2,1)S(1)} %get-tuple-element.24), channel_id=1, replica_groups=mesh['x'=4,'y'=4,'z'=4,'c'=2] {'y','x'}, dimensions={0} | all-to-all | bytes 1048576 | tf_op jit(solution)/shard_map/all_to_all | solution.py:288
  36.7 1.6 %copy-done = bf16[2,1024,512]{2,1,0:T(8,128)(2,1)S(1)} copy-done((bf16[2,1024,512]{2,1,0:T(8,128)(2,1)S(1)}, bf16[2,1024,512]{2,1,0:T(8,128)(2,1)}, u32[]{:S(2)}) %copy-start) | copy-done | bytes 2097176
  38.4 0.2 collective-permute-done.3.far
  38.6 3.5 %slots.2 = (f32[8,64,128]{2,1,0:T(8,128)S(1)}, f32[8,64,128]{2,1,0:T(8,128)S(1)}) custom-call(s32[14]{0:T(128)S(1)} %concatenate.3.table, bf16[16,64,256]{2,1,0:T(8,128)(2,1)S(1)} %all_to_all.30.near, bf16[16,64,256]{2,1,0:T(8,128)(2,1)S(1)} %collective-permute-done.3.far, bf16[1024,512]{1,0:T(8,128)(2,1)S(1)} %bring_coupling.1.coup_a, ...), custom_call_target="tpu_custom_call" | custom-call | flops 1610612736 | bytes 8388608 | tf_op jit(solution)/shard_map/slots/pallas_call | solution.py:304
  42.2 2.1 %collective-permute-start.4 = (f32[8,64,128]{2,1,0:T(8,128)S(1)}, f32[8,64,128]{2,1,0:T(8,128)S(1)}, u32[]{:S(2)}, u32[]{:S(2)}) collective-permute-start(f32[8,64,128]{2,1,0:T(8,128)S(1)} %get-tuple-element.26), channel_id=1, source_target_pairs={{0,1},{1,0},{2,3},{3,2},{4,5},{5,4},{6,7},{7,6},{8,9},{9,8},{10,11... | collective-permute-start | bytes 786440 | tf_op jit(solution)/shard_map/ppermute | solution.py:284
  44.3 1.2 collective-permute-done.4.got
  45.5 1.0 parcels.2
  46.4 26.1 %all_to_all.31.arrived = bf16[64,16,512]{2,1,0:T(8,128)(2,1)S(1)} all-to-all(bf16[64,16,512]{2,1,0:T(8,128)(2,1)S(1)} %parcels.2), channel_id=1, replica_groups=mesh['x'=4,'y'=4,'z'=4,'c'=2] {'y','x','z'}, dimensions={0} | all-to-all | bytes 2097152 | tf_op jit(solution)/shard_map/all_to_all | solution.py:288
  72.6 0.5 second_direction.1
  73.1 16.7 %all_to_all.32 = bf16[64,16,256]{2,1,0:T(8,128)(2,1)S(1)} all-to-all(bf16[64,16,256]{2,1,0:T(8,128)(2,1)S(1)} %get-tuple-element.28), channel_id=1, replica_groups=mesh['x'=4,'y'=4,'z'=4,'c'=2] {'y','x','z'}, dimensions={0} | all-to-all | bytes 1048576 | tf_op jit(solution)/shard_map/all_to_all | solution.py:288
  89.8 1.9 %collective-permute-done.5.far = bf16[16,64,256]{2,1,0:T(8,128)(2,1)S(1)} collective-permute-done((bf16[16,64,256]{2,1,0:T(8,128)(2,1)S(1)}, bf16[16,64,256]{2,1,0:T(8,128)(2,1)S(1)}, u32[]{:S(2)}, u32[]{:S(2)}) %collective-permute-start.5) | collective-permute-done | bytes 524320 | tf_op jit(solution)/shard_map/ppermute | solution.py:284
  91.7 3.5 %slots.3 = (f32[8,64,128]{2,1,0:T(8,128)S(1)}, f32[8,64,128]{2,1,0:T(8,128)S(1)}) custom-call(s32[14]{0:T(128)S(1)} %concatenate.3.table, bf16[16,64,256]{2,1,0:T(8,128)(2,1)S(1)} %bitcast.6, bf16[16,64,256]{2,1,0:T(8,128)(2,1)S(1)} %collective-permute-done.5.far, bf16[1024,512]{1,0:T(8,128)(2,1)S(1)} %bring_coupling.1.coup_a, ...), custom_call_target="tpu_custom_call" | custom-call | flops 1610612736 | bytes 8388608 | tf_op jit(solution)/shard_map/slots/pallas_call | solution.py:304
  95.2 2.0 %collective-permute-start.6 = (f32[8,64,128]{2,1,0:T(8,128)S(1)}, f32[8,64,128]{2,1,0:T(8,128)S(1)}, u32[]{:S(2)}, u32[]{:S(2)}) collective-permute-start(f32[8,64,128]{2,1,0:T(8,128)S(1)} %get-tuple-element.30), channel_id=1, source_target_pairs={{0,1},{1,0},{2,3},{3,2},{4,5},{5,4},{6,7},{7,6},{8,9},{9,8},{10,11... | collective-permute-start | bytes 786440 | tf_op jit(solution)/shard_map/ppermute | solution.py:284
  97.2 1.2 collective-permute-done.6.got
  98.4 0.8 parcels.3
  99.2 18.1 %all_to_all.33.arrived = bf16[64,16,256]{2,1,0:T(8,128)(2,1)S(1)} all-to-all(bf16[64,16,256]{2,1,0:T(8,128)(2,1)S(1)} %parcels.3), channel_id=1, replica_groups=mesh['x'=4,'y'=4,'z'=4,'c'=2] {'y','x','z'}, dimensions={0} | all-to-all | bytes 1048576 | tf_op jit(solution)/shard_map/all_to_all | solution.py:288
  117.3 0.7 products.1
  118.1 15.2 %all_to_all.34.near = f32[64,8,128]{2,1,0:T(8,128)S(1)} all-to-all(f32[64,8,128]{2,1,0:T(8,128)S(1)} %products.1), channel_id=1, replica_groups=mesh['x'=4,'y'=4,'z'=4,'c'=2] {'y','x','z'}, dimensions={0} | all-to-all | bytes 524288 | tf_op jit(solution)/shard_map/all_to_all | solution.py:288
  133.3 1.5 %collective-permute-done.7.far = f32[64,8,128]{2,1,0:T(8,128)S(1)} collective-permute-done((f32[64,8,128]{2,1,0:T(8,128)S(1)}, f32[64,8,128]{2,1,0:T(8,128)S(1)}, u32[]{:S(2)}, u32[]{:S(2)}) %collective-permute-start.7) | collective-permute-done | bytes 262176 | tf_op jit(solution)/shard_map/ppermute | solution.py:284
  134.8 1.3 closing.1
  (16 shorter events, 0.1 us)
Async XLA Ops:
  0.0 19.8 %collective-permute-start.2 = (f32[256,128]{1,0:T(8,128)}, f32[256,128]{1,0:T(8,128)S(1)}, u32[]{:S(2)}, u32[]{:S(2)}) collective-permute-start(f32[256,128]{1,0:T(8,128)} %rhs.1), channel_id=1, source_target_pairs={{0,120},{8,16},{16,8},{24,32},{32,24},{40,48},{48,40},{56,64},{64,... | collective-permute-start | bytes 393224 | tf_op jit(solution)/shard_map/ppermute | solution.py:293
  5.3 14.5 %collective-permute-start.1 = (f32[256,128]{1,0:T(8,128)}, f32[256,128]{1,0:T(8,128)S(1)}, u32[]{:S(2)}, u32[]{:S(2)}) collective-permute-start(f32[256,128]{1,0:T(8,128)} %rhs.1), channel_id=1, source_target_pairs={{0,8},{8,0},{16,24},{24,16},{32,40},{40,32},{48,56},{56,48},{64,72... | collective-permute-start | bytes 393224 | tf_op jit(solution)/shard_map/ppermute | solution.py:292
  5.3 1.0 copy-start.3
  6.3 0.7 copy-start.4
  8.2 11.6 %all-to-all-start = ((f32[16,8,128]{2,1,0:T(8,128)}), f32[16,8,128]{2,1,0:T(8,128)S(1)}, u32[]{:S(2)}, u32[]{:S(2)}) async-start(f32[16,8,128]{2,1,0:T(8,128)} %get-tuple-element.21), calls=%async_computation | async-start | bytes 131072 | tf_op jit(solution)/shard_map/all_to_all | solution.py:288
  14.3 2.1 %collective-permute-start = (s32[14]{0:T(128)S(1)}, s32[14]{0:T(128)S(1)}, u32[]{:S(2)}, u32[]{:S(2)}) collective-permute-start(s32[14]{0:T(128)S(1)} %concatenate.3.table), channel_id=1, source_target_pairs={{0,1},{1,0},{2,3},{3,2},{4,5},{5,4},{6,7},{7,6},{8,9},{9,8},{10,11... | collective-permute-start | bytes 176 | tf_op jit(solution)/shard_map/ppermute | solution.py:284
  14.3 1.0 copy-start.1
  15.2 0.9 copy-start.2
  36.7 1.9 %collective-permute-start.3 = (bf16[16,64,256]{2,1,0:T(8,128)(2,1)S(1)}, bf16[16,64,256]{2,1,0:T(8,128)(2,1)S(1)}, u32[]{:S(2)}, u32[]{:S(2)}) collective-permute-start(bf16[16,64,256]{2,1,0:T(8,128)(2,1)S(1)} %all_to_all.30.near), channel_id=1, source_target_pairs={{0,1},{1,0},{2,3},{3,2},{4,5},{5,4},{6,7},{7,6},{8,9},{9,8},{10,11... | collective-permute-start | bytes 1572872 | tf_op jit(solution)/shard_map/ppermute | solution.py:284
  36.7 1.6 %copy-start = (bf16[2,1024,512]{2,1,0:T(8,128)(2,1)S(1)}, bf16[2,1024,512]{2,1,0:T(8,128)(2,1)}, u32[]{:S(2)}) copy-start(bf16[2,1024,512]{2,1,0:T(8,128)(2,1)} %couplings.5) | copy-start | bytes 6291460
  42.2 3.3 %collective-permute-start.4 = (f32[8,64,128]{2,1,0:T(8,128)S(1)}, f32[8,64,128]{2,1,0:T(8,128)S(1)}, u32[]{:S(2)}, u32[]{:S(2)}) collective-permute-start(f32[8,64,128]{2,1,0:T(8,128)S(1)} %get-tuple-element.26), channel_id=1, source_target_pairs={{0,1},{1,0},{2,3},{3,2},{4,5},{5,4},{6,7},{7,6},{8,9},{9,8},{10,11... | collective-permute-start | bytes 786440 | tf_op jit(solution)/shard_map/ppermute | solution.py:284
  89.8 1.9 %collective-permute-start.5 = (bf16[16,64,256]{2,1,0:T(8,128)(2,1)S(1)}, bf16[16,64,256]{2,1,0:T(8,128)(2,1)S(1)}, u32[]{:S(2)}, u32[]{:S(2)}) collective-permute-start(bf16[16,64,256]{2,1,0:T(8,128)(2,1)S(1)} %bitcast.5), channel_id=1, source_target_pairs={{0,1},{1,0},{2,3},{3,2},{4,5},{5,4},{6,7},{7,6},{8,9},{9,8},{10,11... | collective-permute-start | bytes 1572872 | tf_op jit(solution)/shard_map/ppermute | solution.py:284
  95.2 3.1 %collective-permute-start.6 = (f32[8,64,128]{2,1,0:T(8,128)S(1)}, f32[8,64,128]{2,1,0:T(8,128)S(1)}, u32[]{:S(2)}, u32[]{:S(2)}) collective-permute-start(f32[8,64,128]{2,1,0:T(8,128)S(1)} %get-tuple-element.30), channel_id=1, source_target_pairs={{0,1},{1,0},{2,3},{3,2},{4,5},{5,4},{6,7},{7,6},{8,9},{9,8},{10,11... | collective-permute-start | bytes 786440 | tf_op jit(solution)/shard_map/ppermute | solution.py:284
  133.3 1.5 %collective-permute-start.7 = (f32[64,8,128]{2,1,0:T(8,128)S(1)}, f32[64,8,128]{2,1,0:T(8,128)S(1)}, u32[]{:S(2)}, u32[]{:S(2)}) collective-permute-start(f32[64,8,128]{2,1,0:T(8,128)S(1)} %all_to_all.34.near), channel_id=1, source_target_pairs={{0,1},{1,0},{2,3},{3,2},{4,5},{5,4},{6,7},{7,6},{8,9},{9,8},{10,11... | collective-permute-start | bytes 786440 | tf_op jit(solution)/shard_map/ppermute | solution.py:284

commit v5 on v4

--- a/solution.py
+++ b/solution.py
@@ -58,15 +58,15 @@
     return pl.ds(pl.multiple_of((table[place] & 1) * BI, BI), BI)
 
 
-def opening(halo, rhs, sent, held):
-    field = rhs[...]
-    held[...] = field
-    sums = jnp.sum(field * field, axis=0, keepdims=True)
-    row = lax.broadcasted_iota(jnp.int32, (8, COLS), 0)
+def opening(place, halo, rhs, sent, turned):
+    turned[...] = rhs[...].T
+    part = pl.ds(pl.multiple_of(place[CORE] * HALF + place[DEPTH] * PART, PART), PART)
+    row = lax.broadcasted_iota(jnp.int32, (8, ROWS), 0)
     left = (halo[0, 0] & 1).astype(F32)
     right = (halo[0, 1] & 1).astype(F32)
-    tile = jnp.where(row == 0, sums, jnp.where(row == 1, left, jnp.where(row == 2, right, 0.0)))
-    sent[...] = jnp.broadcast_to(tile[None], sent.shape)
+    tile = jnp.where(row == 0, left, jnp.where(row == 1, right, 0.0))
+    mine = jnp.concatenate([turned[part, :], tile], axis=0)
+    sent[...] = jnp.broadcast_to(mine[None], sent.shape)
 
 
 def bring_owned(precond, diag, precond_v, diag_v, sems):
@@ -86,28 +86,24 @@
     copy.wait()
 
 
-def first_direction(
-    table, table_far, rhs, paired, linked, facts, precond, diag, sent, z_nat, base, basis, turned
-):
-    beta = jnp.sqrt(jnp.sum(facts[:, 0:1, :], axis=0))
-    v = rhs[...] / beta
-    odd = (table[GROUP] & 1) == 1
-    lower = block_at(table, HALO)
-    upper = block_at(table, HALO + 1)
-    left = jnp.where(odd, paired[lower, :], linked[lower, :]) / beta
-    right = jnp.where(odd, linked[upper, :], paired[upper, :]) / beta
-    patch = jnp.concatenate([v, left, right], axis=0).astype(BF16)
-    z = v + dot(precond[...], patch)
-    z_nat[...] = z
-    half = pl.ds(pl.multiple_of(table[CORE] * HALF, HALF), HALF)
-    part = pl.ds(pl.multiple_of(table[CORE] * HALF + table[DEPTH] * PART, PART), PART)
-    turned[...] = z.T
-    mine = turned[half, :].astype(BF16)
-    sent[...] = jnp.broadcast_to(mine[None], sent.shape)
-    turned[...] = (3.0 * z + dot(diag[...], z.astype(BF16))).T
-    base[...] = turned[part, :]
-    turned[...] = v.T
-    basis[...] = turned[part, :]
+def first_direction(table, table_far, facts, precond, diag, sent, base, basis, scale):
+    squares = jnp.zeros((PART, ROWS), F32)
+    for i in range(GROUPS):
+        squares = squares + facts[i, :PART, :] * facts[i, :PART, :]
+    beta = jnp.sqrt(jnp.sum(squares, axis=1, keepdims=True))
+    scale[...] = jnp.broadcast_to(beta, scale.shape)
+    mine = table[GROUP]
+    before = partner((mine + GROUPS - 1) & (GROUPS - 1))
+    after = partner((mine + 1) & (GROUPS - 1))
+    v = facts[partner(mine), :PART, :] / beta
+    left = facts[before, :PART, block_at(table, HALO)] / beta
+    right = facts[after, :PART, block_at(table, HALO + 1)] / beta
+    basis[...] = v
+    patch = jnp.concatenate([v, left, right], axis=1).astype(BF16)
+    z = v + dot(patch, precond[...], NT)
+    low = z.astype(BF16)
+    base[...] = 3.0 * z + dot(low, diag[...], NT)
+    sent[...] = jnp.broadcast_to(low[None], sent.shape)
 
 
 def slots(
@@ -192,8 +188,8 @@
         upper = 2 * ((d + 1) & (GROUPS - 1))
         blocks = [total[2 * d], total[2 * d + 1]]
         if with_halo:
-            left = facts[place, 1:2, :] > 0.5
-            right = facts[place, 2:3, :] > 0.5
+            left = facts[place, PART : PART + 1, :BI] > 0.5
+            right = facts[place, PART + 1 : PART + 2, :BI] > 0.5
             blocks.append(jnp.where(left, total[lower + 1], total[lower]))
             blocks.append(jnp.where(right, total[upper + 1], total[upper]))
         for j, block in enumerate(blocks):
@@ -209,7 +205,7 @@
         part = pl.ds(pl.multiple_of(depth * PART, PART), PART)
         for side, other in ((0, mine + 1), (1, mine + GROUPS - 1)):
             other = partner(other & (GROUPS - 1))
-            upper = facts[other, side + 1 : side + 2, :] > 0.5
+            upper = facts[other, PART + side : PART + side + 1, :BI] > 0.5
             block = jnp.where(upper, total[2 * mine + 1, part, :], total[2 * mine, part, :])
             stays = jnp.where(upper, base[:, BI:], base[:, :BI])
             lanes = slice(ROWS + side * BI, ROWS + (side + 1) * BI)
@@ -236,7 +232,7 @@
     sent[...] = jnp.broadcast_to(low[None], sent.shape)
 
 
-def products(table, arrived, base, w, basis, sent):
+def products(table, arrived, base, w, basis, scale, sent):
     image = (base[...] - summed(arrived)) * SHRINK
     one = w[...]
     v = basis[...]
@@ -250,13 +246,14 @@
         value = jnp.sum(left * right, axis=1, keepdims=True)
         spread = jnp.sum(jnp.where(here, value, 0.0), axis=0, keepdims=True)
         tile = jnp.where(rank == k, spread, tile)
+    beta = jnp.sum(jnp.where(here, scale[...] / GROUPS, 0.0), axis=0, keepdims=True)
+    tile = jnp.where(rank == len(pairs), beta, tile)
     sent[...] = jnp.broadcast_to(tile[None], sent.shape)
 
 
-def closing(table, near, far, facts, z_one, z_near, z_far, answer):
+def closing(table, near, far, one_near, one_far, two_near, two_far, answer):
     sums = jnp.sum(near[...], axis=0) + jnp.sum(far[...], axis=0)
-    beta = jnp.sqrt(jnp.sum(facts[:, 0:1, :], axis=0))
-    h11, ww, vx, wx, xx = (sums[k : k + 1] for k in range(5))
+    h11, ww, vx, wx, xx, beta = (sums[k : k + 1] for k in range(6))
     h21 = jnp.sqrt(ww - h11 * h11)
     small = SHRINK * h11
     h12 = (vx - small * h11) / (SHRINK * h21)
@@ -273,11 +270,14 @@
     y1 = (cosine * beta - top * y2) / rho
     second = y2 / h21
     first = y1 - second * h11
-    a = z_near[0].astype(F32)
-    b = z_far[0].astype(F32)
     swap = table[CORE] == 1
-    stacked = jnp.concatenate([jnp.where(swap, b, a), jnp.where(swap, a, b)], axis=0)
-    answer[...] = first * z_one[...] + second * stacked.T
+    field = []
+    for weight, own, other in ((first, one_near, one_far), (second, two_near, two_far)):
+        a = own[0].astype(F32)
+        b = other[0].astype(F32)
+        stacked = jnp.concatenate([jnp.where(swap, b, a), jnp.where(swap, a, b)], axis=0)
+        field.append(weight * stacked.T)
+    answer[...] = field[0] + field[1]
 
 
 def other_core(array):
@@ -286,12 +286,6 @@
 
 def swap_all(array, axes):
     return lax.all_to_all(array, axes, split_axis=0, concat_axis=0, tiled=True)
-
-
-def neighbours(array):
-    paired = lax.ppermute(array, SUB, [(i, i ^ 1) for i in range(GROUPS)])
-    linked = lax.ppermute(array, SUB, [(i, (i - 1 + 2 * (i & 1)) % GROUPS) for i in range(GROUPS)])
-    return paired, linked
 
 
 def on_device(rhs, schur_diag, precond, halo_ids, factors, couplings, block_ids, counts):
@@ -299,6 +293,12 @@
     place = jnp.stack([group, lax.axis_index("z"), lax.axis_index("c")]).astype(jnp.int32)
     table = jnp.concatenate([place, counts, halo_ids.reshape(-1), block_ids.reshape(-1)])
     table_far = other_core(table)
+
+    def gather(sent):
+        near = swap_all(sent, YXZ).reshape(GROUPS, HALF, ROWS)
+        far = other_core(near)
+        mine = [lax.dynamic_slice_in_dim(half, partner(group), 1, 0) for half in (near, far)]
+        return near, far, mine
 
     def apply_slots(near, far):
         return call(
@@ -331,13 +331,14 @@
         )(table, table_far, kept, got, facts, base)
         return swap_all(sent, YXZ)
 
-    paired, linked = neighbours(rhs)
-    opened, held = call(
+    (opened,) = call(
         opening,
         "opening",
-        [out((GROUPS, 8, COLS), F32), out((ROWS, COLS), F32)],
-        [SMEM, VMEM],
-    )(halo_ids, rhs)
+        [out((GROUPS, PART + 8, ROWS), F32)],
+        [SMEM, SMEM, VMEM],
+        [pltpu.VMEM((COLS, ROWS), F32)],
+        room=67043328,
+    )(place, halo_ids, rhs)
     facts = swap_all(opened, YX)
     precond_v, diag_v = call(
         bring_owned,
@@ -353,21 +354,19 @@
         [HBM],
         [pltpu.SemaphoreType.DMA],
     )(couplings)
-    sent, z_one, base, basis = call(
+    sent, base, basis, scale = call(
         first_direction,
         "first_direction",
         [
-            out((GROUPS, HALF, ROWS), BF16),
-            out((ROWS, COLS), F32),
+            out((64, PART, ROWS), BF16),
             out((PART, ROWS), F32),
             out((PART, ROWS), F32),
+            out((PART, COLS), F32),
         ],
-        [SMEM, SMEM, VMEM, VMEM, VMEM, VMEM, VMEM, VMEM],
-        [pltpu.VMEM((COLS, ROWS), F32)],
+        [SMEM, SMEM, VMEM, VMEM, VMEM],
         flops=1 << 26,
-    )(table, table_far, held, paired, linked, facts, precond_v, diag_v)
-    near = swap_all(sent, YX)
-    far = other_core(near)
+    )(table, table_far, facts, precond_v, diag_v)
+    near, far, mine = gather(sent)
     kept, given = apply_slots(near, far)
     arrived = to_owners(kept, given, 2 * ROWS)
     sent, base, w = call(
@@ -377,19 +376,17 @@
         [VMEM, VMEM, VMEM, VMEM],
         flops=1 << 26,
     )(arrived, base, precond_v, diag_v)
-    near = swap_all(sent, YXZ).reshape(GROUPS, HALF, ROWS)
-    far = other_core(near)
+    near, far, mine_two = gather(sent)
     kept, given = apply_slots(near, far)
     arrived = to_owners(kept, given, ROWS)
     (sent,) = call(
-        products, "products", [out((64, 8, COLS), F32)], [SMEM, VMEM, VMEM, VMEM, VMEM]
-    )(table, arrived, base, w, basis)
+        products, "products", [out((64, 8, COLS), F32)], [SMEM] + [VMEM] * 5
+    )(table, arrived, base, w, basis, scale)
     sums = swap_all(sent, YXZ)
     sums_far = other_core(sums)
-    own = [lax.dynamic_slice_in_dim(half, partner(group), 1, 0) for half in (near, far)]
     (answer,) = call(
         closing, "closing", [out((ROWS, COLS), F32)], [SMEM] + [VMEM] * 6
-    )(table, sums, sums_far, facts, z_one, *own)
+    )(table, sums, sums_far, *mine, *mine_two)
     return answer
 
 

time: 138 us -> 140 us (1.014)
  waiting for transfers between devices: 9.4 us -> 23.7 us
  blocking collectives: 92 us -> 81.7 us
  local copies, waits for them, and re-layouts: 6.57 us -> 4.13 us
    all_to_all x1 -> x2, waiting for transfers between devices: 3.41 us -> 16.4 us  [swap_all(): return lax.all_to_all(array, axes, split_axis=0, concat_axis=0, tiled=True)]
    all_to_all x5 -> x4, blocking collectives: 92 us -> 81.7 us  [swap_all(): return lax.all_to_all(array, axes, split_axis=0, concat_axis=0, tiled=True)]
    all_to_all x1 -> x2, starting transfers between devices: 3.93 us -> 12.1 us  [swap_all(): return lax.all_to_all(array, axes, split_axis=0, concat_axis=0, tiled=True)]
    ppermute x2 -> x0, starting transfers between devices: 5.32 us -> none  [the longest x1 5.32 us: neighbours(): lax.ppermute(array, SUB, [(i, (i - 1 + 2 * (i & 1)) % GROUPS) for i in ra...]
    ppermute x6, starting transfers between devices: 4.14 us -> 0.46 us  [other_core(): return lax.ppermute(array, 'c', [(0, 1), (1, 0)])]
    unnamed x10 -> x8, local copies, waits for them, and re-layouts: 5.06 us -> 1.86 us
  transfers between devices with their start and end apart: 9 -> 8, of which waited for: 6 -> 7; matrix products, arithmetic and copies ran while one was open for 1% -> 2% of each run, Pallas kernels for 1% -> 0%
where the time goes in v5:
time: 140 us; the launch traced here: 139 us
  blocking collectives  81.7 us (58%)
  waiting for transfers between devices  23.7 us (17%)
  Pallas kernels  15.1 us (11%)
  starting transfers between devices  12.6 us (9%)
  local copies, waits for them, and re-layouts  4.13 us (3%)
    all_to_all x4, blocking collectives, swap_all(): return lax.all_to_all(array, axes, split_axis=0, concat_axis=0, tiled=True)  81.7 us
    all_to_all x2, waiting for transfers between devices, swap_all(): return lax.all_to_all(array, axes, split_axis=0, concat_axis=0, tiled=True)  16.4 us
    all_to_all x2, starting transfers between devices, swap_all(): return lax.all_to_all(array, axes, split_axis=0, concat_axis=0, tiled=True)  12.1 us
    ppermute x6, waiting for transfers between devices, other_core(): return lax.ppermute(array, 'c', [(0, 1), (1, 0)])  7.29 us
    pallas_call x2, Pallas kernels, apply_slots(): call(slots, 'slots', [out((8, HALF, BI), F32), out((8, HALF, BI), F32)],...  7.03 us
  transfers between devices with their start and end apart: 8, of which 7 were waited for; matrix products, arithmetic and copies ran while one was open for 2% of the time, Pallas kernels for 0%

profile of v5, /device:TPU:0, one launch (start us, length us, event | category | flops | bytes accessed | tf_op | source)
XLA Modules:
  0.0 138.6 jit_solution(6141498925480583839)
XLA Ops:
  0.0 0.6 pad_add_fusion.place
  0.6 1.8 %opening.1 = f32[16,24,256]{2,1,0:T(8,128)} custom-call(s32[3]{0:T(128)} %pad_add_fusion.place, s32[1,2]{1,0:T(1,128)} %halo.1, f32[256,128]{1,0:T(8,128)} %rhs.1), custom_call_target="tpu_custom_call" | custom-call | bytes 1048576 | tf_op jit(solution)/shard_map/opening/pallas_call | solution.py:334
  2.4 7.3 %all-to-all-start = ((f32[16,24,256]{2,1,0:T(8,128)}), f32[16,24,256]{2,1,0:T(8,128)S(1)}, u32[]{:S(2)}, u32[]{:S(2)}) async-start(f32[16,24,256]{2,1,0:T(8,128)} %opening.1), calls=%async_computation | async-start | bytes 786432 | tf_op jit(solution)/shard_map/all_to_all | solution.py:288
  10.3 0.8 reshape.13
  11.1 0.7 concatenate.4.table
  11.8 0.9 copy-done.2
  12.8 0.9 copy-done.3
  13.7 0.2 bring_owned.1
  13.9 5.8 %all-to-all-done.facts = f32[16,24,256]{2,1,0:T(8,128)S(1)} async-done(((f32[16,24,256]{2,1,0:T(8,128)}), f32[16,24,256]{2,1,0:T(8,128)S(1)}, u32[]{:S(2)}, u32[]{:S(2)}) %all-to-all-start) | async-done | bytes 393248 | tf_op jit(solution)/shard_map/all_to_all | solution.py:288
  19.8 1.0 first_direction.1
  20.7 19.7 %all_to_all.30 = bf16[64,16,256]{2,1,0:T(8,128)(2,1)S(1)} all-to-all(bf16[64,16,256]{2,1,0:T(8,128)(2,1)S(1)} %get-tuple-element.20), channel_id=1, replica_groups=mesh['x'=4,'y'=4,'z'=4,'c'=2] {'y','x','z'}, dimensions={0} | all-to-all | bytes 1048576 | tf_op jit(solution)/shard_map/all_to_all | solution.py:288
  40.4 0.1 bring_coupling.1.coup_a
  40.5 1.8 %collective-permute-done.1.far = bf16[16,64,256]{2,1,0:T(8,128)(2,1)S(1)} collective-permute-done((bf16[16,64,256]{2,1,0:T(8,128)(2,1)S(1)}, bf16[16,64,256]{2,1,0:T(8,128)(2,1)S(1)}, u32[]{:S(2)}, u32[]{:S(2)}) %collective-permute-start.1) | collective-permute-done | bytes 524320 | tf_op jit(solution)/shard_map/ppermute | solution.py:284
  42.3 3.5 %slots.2 = (f32[8,64,128]{2,1,0:T(8,128)S(1)}, f32[8,64,128]{2,1,0:T(8,128)S(1)}) custom-call(s32[14]{0:T(128)S(1)} %concatenate.4.table, bf16[16,64,256]{2,1,0:T(8,128)(2,1)S(1)} %bitcast.7, bf16[16,64,256]{2,1,0:T(8,128)(2,1)S(1)} %collective-permute-done.1.far, bf16[1024,512]{1,0:T(8,128)(2,1)S(1)} %bring_coupling.1.coup_a, ...), custom_call_target="tpu_custom_call" | custom-call | flops 1610612736 | bytes 8388608 | tf_op jit(solution)/shard_map/slots/pallas_call | solution.py:304
  45.8 0.2 collective-permute-start.2
  46.1 1.4 %collective-permute-done.2.got = f32[8,64,128]{2,1,0:T(8,128)S(1)} collective-permute-done((f32[8,64,128]{2,1,0:T(8,128)S(1)}, f32[8,64,128]{2,1,0:T(8,128)S(1)}, u32[]{:S(2)}, u32[]{:S(2)}) %collective-permute-start.2) | collective-permute-done | bytes 262176 | tf_op jit(solution)/shard_map/ppermute | solution.py:284
  47.5 0.9 parcels.2
  48.4 25.4 %all_to_all.31.arrived = bf16[64,16,512]{2,1,0:T(8,128)(2,1)S(1)} all-to-all(bf16[64,16,512]{2,1,0:T(8,128)(2,1)S(1)} %parcels.2), channel_id=1, replica_groups=mesh['x'=4,'y'=4,'z'=4,'c'=2] {'y','x','z'}, dimensions={0} | all-to-all | bytes 2097152 | tf_op jit(solution)/shard_map/all_to_all | solution.py:288
  73.8 0.5 second_direction.1
  74.3 16.7 %all_to_all.32 = bf16[64,16,256]{2,1,0:T(8,128)(2,1)S(1)} all-to-all(bf16[64,16,256]{2,1,0:T(8,128)(2,1)S(1)} %get-tuple-element.24), channel_id=1, replica_groups=mesh['x'=4,'y'=4,'z'=4,'c'=2] {'y','x','z'}, dimensions={0} | all-to-all | bytes 1048576 | tf_op jit(solution)/shard_map/all_to_all | solution.py:288
  91.0 1.9 %collective-permute-done.3.far = bf16[16,64,256]{2,1,0:T(8,128)(2,1)S(1)} collective-permute-done((bf16[16,64,256]{2,1,0:T(8,128)(2,1)S(1)}, bf16[16,64,256]{2,1,0:T(8,128)(2,1)S(1)}, u32[]{:S(2)}, u32[]{:S(2)}) %collective-permute-start.3) | collective-permute-done | bytes 524320 | tf_op jit(solution)/shard_map/ppermute | solution.py:284
  93.0 3.5 %slots.3 = (f32[8,64,128]{2,1,0:T(8,128)S(1)}, f32[8,64,128]{2,1,0:T(8,128)S(1)}) custom-call(s32[14]{0:T(128)S(1)} %concatenate.4.table, bf16[16,64,256]{2,1,0:T(8,128)(2,1)S(1)} %bitcast.10, bf16[16,64,256]{2,1,0:T(8,128)(2,1)S(1)} %collective-permute-done.3.far, bf16[1024,512]{1,0:T(8,128)(2,1)S(1)} %bring_coupling.1.coup_a, ...), custom_call_target="tpu_custom_call" | custom-call | flops 1610612736 | bytes 8388608 | tf_op jit(solution)/shard_map/slots/pallas_call | solution.py:304
  96.5 0.2 collective-permute-start.4
  96.7 1.4 %collective-permute-done.4.got = f32[8,64,128]{2,1,0:T(8,128)S(1)} collective-permute-done((f32[8,64,128]{2,1,0:T(8,128)S(1)}, f32[8,64,128]{2,1,0:T(8,128)S(1)}, u32[]{:S(2)}, u32[]{:S(2)}) %collective-permute-start.4) | collective-permute-done | bytes 262176 | tf_op jit(solution)/shard_map/ppermute | solution.py:284
  98.1 0.8 parcels.3
  98.9 19.9 %all_to_all.33.arrived = bf16[64,16,256]{2,1,0:T(8,128)(2,1)S(1)} all-to-all(bf16[64,16,256]{2,1,0:T(8,128)(2,1)S(1)} %parcels.3), channel_id=1, replica_groups=mesh['x'=4,'y'=4,'z'=4,'c'=2] {'y','x','z'}, dimensions={0} | all-to-all | bytes 1048576 | tf_op jit(solution)/shard_map/all_to_all | solution.py:288
  118.9 1.4 %products.1 = f32[64,8,128]{2,1,0:T(8,128)} custom-call(s32[14]{0:T(128)S(1)} %concatenate.4.table, bf16[64,16,256]{2,1,0:T(8,128)(2,1)S(1)} %all_to_all.33.arrived, f32[16,256]{1,0:T(8,128)S(1)} %get-tuple-element.27.base, f32[16,256]{1,0:T(8,128)S(1)} %get-tuple-element.28.w, f32[16,256]{1,0:T(8,128)S(1)} %get-tuple-element.29.basis, ...), custom_call_target="tpu_custom_call" | custom-call | bytes 1048576 | tf_op jit(solution)/shard_map/products/pallas_call | solution.py:382
  120.3 4.8 %all-to-all-start.5 = ((f32[64,8,128]{2,1,0:T(8,128)}), f32[64,8,128]{2,1,0:T(8,128)S(1)}, u32[]{:S(2)}, u32[]{:S(2)}) async-start(f32[64,8,128]{2,1,0:T(8,128)} %products.1), calls=%async_computation.5 | async-start | bytes 524288 | tf_op jit(solution)/shard_map/all_to_all | solution.py:288
  125.2 10.5 %all-to-all-done.5.near = f32[64,8,128]{2,1,0:T(8,128)S(1)} async-done(((f32[64,8,128]{2,1,0:T(8,128)}), f32[64,8,128]{2,1,0:T(8,128)S(1)}, u32[]{:S(2)}, u32[]{:S(2)}) %all-to-all-start.5) | async-done | bytes 262176 | tf_op jit(solution)/shard_map/all_to_all | solution.py:288
  135.7 0.8 constant_dynamic-slice_fusion.2.one_far
  136.5 0.8 collective-permute-done.5.far
  137.2 1.3 closing.1
  (14 shorter events, 0.1 us)
Async XLA Ops:
  2.4 38.0 %copy-start = (bf16[2,1024,512]{2,1,0:T(8,128)(2,1)S(1)}, bf16[2,1024,512]{2,1,0:T(8,128)(2,1)}, u32[]{:S(2)}) copy-start(bf16[2,1024,512]{2,1,0:T(8,128)(2,1)} %couplings.5) | copy-start | bytes 6291460
  2.4 17.4 %all-to-all-start = ((f32[16,24,256]{2,1,0:T(8,128)}), f32[16,24,256]{2,1,0:T(8,128)S(1)}, u32[]{:S(2)}, u32[]{:S(2)}) async-start(f32[16,24,256]{2,1,0:T(8,128)} %opening.1), calls=%async_computation | async-start | bytes 786432 | tf_op jit(solution)/shard_map/all_to_all | solution.py:288
  11.8 2.1 %collective-permute-start = (s32[14]{0:T(128)S(1)}, s32[14]{0:T(128)S(1)}, u32[]{:S(2)}, u32[]{:S(2)}) collective-permute-start(s32[14]{0:T(128)S(1)} %concatenate.4.table), channel_id=1, source_target_pairs={{0,1},{1,0},{2,3},{3,2},{4,5},{5,4},{6,7},{7,6},{8,9},{9,8},{10,11... | collective-permute-start | bytes 176 | tf_op jit(solution)/shard_map/ppermute | solution.py:284
  11.8 1.0 copy-start.2
  12.8 0.9 copy-start.3
  40.4 1.9 %collective-permute-start.1 = (bf16[16,64,256]{2,1,0:T(8,128)(2,1)S(1)}, bf16[16,64,256]{2,1,0:T(8,128)(2,1)S(1)}, u32[]{:S(2)}, u32[]{:S(2)}) collective-permute-start(bf16[16,64,256]{2,1,0:T(8,128)(2,1)S(1)} %bitcast.6), channel_id=1, source_target_pairs={{0,1},{1,0},{2,3},{3,2},{4,5},{5,4},{6,7},{7,6},{8,9},{9,8},{10,11... | collective-permute-start | bytes 1572872 | tf_op jit(solution)/shard_map/ppermute | solution.py:284
  42.3 3.5 %copy-start.1 = (bf16[16,64,256]{2,1,0:T(8,128)(2,1)}, bf16[16,64,256]{2,1,0:T(8,128)(2,1)S(1)}, u32[]{:S(2)}) copy-start(bf16[16,64,256]{2,1,0:T(8,128)(2,1)S(1)} %collective-permute-done.1.far) | copy-start | bytes 1572868
  45.8 1.6 %collective-permute-start.2 = (f32[8,64,128]{2,1,0:T(8,128)S(1)}, f32[8,64,128]{2,1,0:T(8,128)S(1)}, u32[]{:S(2)}, u32[]{:S(2)}) collective-permute-start(f32[8,64,128]{2,1,0:T(8,128)S(1)} %get-tuple-element.22), channel_id=1, source_target_pairs={{0,1},{1,0},{2,3},{3,2},{4,5},{5,4},{6,7},{7,6},{8,9},{9,8},{10,11... | collective-permute-start | bytes 786440 | tf_op jit(solution)/shard_map/ppermute | solution.py:284
  91.0 1.9 %collective-permute-start.3 = (bf16[16,64,256]{2,1,0:T(8,128)(2,1)S(1)}, bf16[16,64,256]{2,1,0:T(8,128)(2,1)S(1)}, u32[]{:S(2)}, u32[]{:S(2)}) collective-permute-start(bf16[16,64,256]{2,1,0:T(8,128)(2,1)S(1)} %bitcast.9), channel_id=1, source_target_pairs={{0,1},{1,0},{2,3},{3,2},{4,5},{5,4},{6,7},{7,6},{8,9},{9,8},{10,11... | collective-permute-start | bytes 1572872 | tf_op jit(solution)/shard_map/ppermute | solution.py:284
  96.5 1.6 %collective-permute-start.4 = (f32[8,64,128]{2,1,0:T(8,128)S(1)}, f32[8,64,128]{2,1,0:T(8,128)S(1)}, u32[]{:S(2)}, u32[]{:S(2)}) collective-permute-start(f32[8,64,128]{2,1,0:T(8,128)S(1)} %get-tuple-element.26), channel_id=1, source_target_pairs={{0,1},{1,0},{2,3},{3,2},{4,5},{5,4},{6,7},{7,6},{8,9},{9,8},{10,11... | collective-permute-start | bytes 786440 | tf_op jit(solution)/shard_map/ppermute | solution.py:284
  120.3 15.4 %all-to-all-start.5 = ((f32[64,8,128]{2,1,0:T(8,128)}), f32[64,8,128]{2,1,0:T(8,128)S(1)}, u32[]{:S(2)}, u32[]{:S(2)}) async-start(f32[64,8,128]{2,1,0:T(8,128)} %products.1), calls=%async_computation.5 | async-start | bytes 524288 | tf_op jit(solution)/shard_map/all_to_all | solution.py:288
  135.7 1.5 %collective-permute-start.5 = (f32[64,8,128]{2,1,0:T(8,128)S(1)}, f32[64,8,128]{2,1,0:T(8,128)S(1)}, u32[]{:S(2)}, u32[]{:S(2)}) collective-permute-start(f32[64,8,128]{2,1,0:T(8,128)S(1)} %all-to-all-done.5.near), channel_id=1, source_target_pairs={{0,1},{1,0},{2,3},{3,2},{4,5},{5,4},{6,7},{7,6},{8,9},{9,8},{10,11... | collective-permute-start | bytes 786440 | tf_op jit(solution)/shard_map/ppermute | solution.py:284

commit v6 on v4

--- a/solution.py
+++ b/solution.py
@@ -80,10 +80,15 @@
         copy.wait()
 
 
-def bring_coupling(couplings, coup, sem):
-    copy = pltpu.make_async_copy(couplings.at[0], coup, sem)
-    copy.start()
-    copy.wait()
+def bring_slot(couplings, factors, coup, fact, sems):
+    copies = [
+        pltpu.make_async_copy(couplings.at[0], coup, sems.at[0]),
+        pltpu.make_async_copy(factors.at[0], fact, sems.at[1]),
+    ]
+    for copy in copies:
+        copy.start()
+    for copy in copies:
+        copy.wait()
 
 
 def first_direction(
@@ -115,31 +120,29 @@
     near,
     far,
     coup_a,
+    fact_a,
     couplings,
     factors,
     kept,
     given,
     coup_b,
-    fact_a,
     fact_b,
     picked,
     one,
     two,
     sems,
 ):
-    first = pltpu.make_async_copy(factors.at[0], fact_a, sems.at[0])
     second = [
-        pltpu.make_async_copy(couplings.at[1], coup_b, sems.at[1]),
-        pltpu.make_async_copy(factors.at[1], fact_b, sems.at[2]),
+        pltpu.make_async_copy(couplings.at[1], coup_b, sems.at[0]),
+        pltpu.make_async_copy(factors.at[1], fact_b, sems.at[1]),
     ]
-    first.start()
 
     @pl.when(table[LIVE] > 1)
     def _():
         for copy in second:
             copy.start()
 
-    def slot(number, coup, fact, copy):
+    def slot(number, coup, fact):
         for j in range(4):
             block = table[IDS + number * 4 + j]
             place = partner(block >> 1)
@@ -149,7 +152,6 @@
         for n in range(4):
             span = slice(n * 256, (n + 1) * 256)
             one[:, span] = dot(picked[...], coup[span, :], NT).astype(BF16)
-        copy.wait()
         for n in range(4):
             span = slice(n * 256, (n + 1) * 256)
             two[:, span] = dot(one[...], fact[span, :], NT).astype(BF16)
@@ -163,12 +165,13 @@
                 kept[number * 4 + n * 2 + m] = piece[0:HALF, lanes]
                 given[number * 4 + n * 2 + m] = piece[HALF:COLS, lanes]
 
-    slot(0, coup_a, fact_a, first)
+    slot(0, coup_a, fact_a)
 
     @pl.when(table[LIVE] > 1)
     def _():
-        second[0].wait()
-        slot(1, coup_b, fact_b, second[1])
+        for copy in second:
+            copy.wait()
+        slot(1, coup_b, fact_b)
 
     @pl.when(table[LIVE] < 2)
     def _():
@@ -305,20 +308,19 @@
             slots,
             "slots",
             [out((8, HALF, BI), F32), out((8, HALF, BI), F32)],
-            [SMEM] + [VMEM] * 3 + [HBM] * 2,
+            [SMEM] + [VMEM] * 4 + [HBM] * 2,
             [
                 pltpu.VMEM((1024, 512), BF16),
-                pltpu.VMEM((1024, 1024), BF16),
                 pltpu.VMEM((1024, 1024), BF16),
                 pltpu.VMEM((COLS, 512), BF16),
                 pltpu.VMEM((COLS, 1024), BF16),
                 pltpu.VMEM((COLS, 1024), BF16),
-                pltpu.SemaphoreType.DMA((3,)),
+                pltpu.SemaphoreType.DMA((2,)),
             ],
             flops=2 * 805306368,
             moved=8 << 20,
-            room=51000 << 10,
-        )(table, near, far, coupling, couplings, factors)
+            room=50500 << 10,
+        )(table, near, far, *operators, couplings, factors)
 
     def to_owners(kept, given, width):
         got = other_core(given)
@@ -346,13 +348,14 @@
         [HBM, HBM],
         [pltpu.SemaphoreType.DMA((2,))],
     )(precond, schur_diag)
-    (coupling,) = call(
-        bring_coupling,
-        "bring_coupling",
-        [out((1024, 512), BF16)],
-        [HBM],
-        [pltpu.SemaphoreType.DMA],
-    )(couplings)
+    operators = call(
+        bring_slot,
+        "bring_slot",
+        [out((1024, 512), BF16), out((1024, 1024), BF16)],
+        [HBM, HBM],
+        [pltpu.SemaphoreType.DMA((2,))],
+        room=52000 << 10,
+    )(couplings, factors)
     sent, z_one, base, basis = call(
         first_direction,
         "first_direction",

time: 138 us -> 138 us (level)
  starting transfers between devices: 13.4 us -> 16.8 us
  local copies, waits for them, and re-layouts: 6.57 us -> 4.33 us
    ppermute x6, starting transfers between devices: 4.14 us -> 7.57 us  [other_core(): return lax.ppermute(array, 'c', [(0, 1), (1, 0)])]
    pallas_call x2, Pallas kernels: 7.02 us -> 4.43 us  [apply_slots(): call(slots, 'slots', [out((8, HALF, BI), F32), out((8, HALF, BI), F32)],...]
    pallas_call x1, Pallas kernels: 0.08 us -> 1.94 us  [on_device(): call(bring_slot, 'bring_slot', [out((1024, 512), BF16), out((1024, 1024),...]
    unnamed x10 -> x8, local copies, waits for them, and re-layouts: 5.06 us -> 3.47 us
  transfers between devices with their start and end apart: 9 -> 9, of which waited for: 6 -> 5; matrix products, arithmetic and copies ran while one was open for 1% -> 1% of each run, Pallas kernels for 1% -> 2%
where the time goes in v6:
time: 138 us; the launch traced here: 137 us
  blocking collectives  92 us (67%)
  starting transfers between devices  16.8 us (12%)
  Pallas kernels  13.3 us (10%)
  waiting for transfers between devices  9.83 us (7%)
  local copies, waits for them, and re-layouts  4.33 us (3%)
    all_to_all x5, blocking collectives, swap_all(): return lax.all_to_all(array, axes, split_axis=0, concat_axis=0, tiled=True)  92 us
    ppermute x6, starting transfers between devices, other_core(): return lax.ppermute(array, 'c', [(0, 1), (1, 0)])  7.57 us
    ppermute x6, waiting for transfers between devices, other_core(): return lax.ppermute(array, 'c', [(0, 1), (1, 0)])  5.76 us
    ppermute x1, starting transfers between devices, neighbours(): lax.ppermute(array, SUB, [(i, (i - 1 + 2 * (i & 1)) % GROUPS) for i in ra...  5.32 us
    pallas_call x2, Pallas kernels, apply_slots(): call(slots, 'slots', [out((8, HALF, BI), F32), out((8, HALF, BI), F32)],...  4.43 us
    all_to_all x1, waiting for transfers between devices, swap_all(): return lax.all_to_all(array, axes, split_axis=0, concat_axis=0, tiled=True)  4.06 us
    all_to_all x1, starting transfers between devices, swap_all(): return lax.all_to_all(array, axes, split_axis=0, concat_axis=0, tiled=True)  3.93 us
    unnamed x8, local copies, waits for them, and re-layouts  3.47 us
  transfers between devices with their start and end apart: 9, of which 5 were waited for; matrix products, arithmetic and copies ran while one was open for 1% of the time, Pallas kernels for 2%

profile of v6, /device:TPU:0, one launch (start us, length us, event | category | flops | bytes accessed | tf_op | source)
XLA Modules:
  0.0 137.0 jit_solution(10458715667961765922)
XLA Ops:
  0.0 5.3 %collective-permute-start.2 = (f32[256,128]{1,0:T(8,128)}, f32[256,128]{1,0:T(8,128)S(1)}, u32[]{:S(2)}, u32[]{:S(2)}) collective-permute-start(f32[256,128]{1,0:T(8,128)} %rhs.1), channel_id=1, source_target_pairs={{0,120},{8,16},{16,8},{24,32},{32,24},{40,48},{48,40},{56,64},{64,... | collective-permute-start | bytes 393224 | tf_op jit(solution)/shard_map/ppermute | solution.py:296
  5.3 1.0 copy-done.2
  6.3 0.7 copy-done.3
  7.0 1.2 opening.1
  8.2 3.9 %all-to-all-start = ((f32[16,8,128]{2,1,0:T(8,128)}), f32[16,8,128]{2,1,0:T(8,128)S(1)}, u32[]{:S(2)}, u32[]{:S(2)}) async-start(f32[16,8,128]{2,1,0:T(8,128)} %get-tuple-element.23), calls=%async_computation | async-start | bytes 131072 | tf_op jit(solution)/shard_map/all_to_all | solution.py:291
  12.8 0.8 reshape.10
  13.5 0.1 concatenate.3.table
  13.6 0.0 collective-permute-start
  13.6 0.9 copy-done
  14.6 0.9 copy-done.1
  15.5 0.2 bring_owned.1
  15.7 4.1 %all-to-all-done.facts = f32[16,8,128]{2,1,0:T(8,128)S(1)} async-done(((f32[16,8,128]{2,1,0:T(8,128)}), f32[16,8,128]{2,1,0:T(8,128)S(1)}, u32[]{:S(2)}, u32[]{:S(2)}) %all-to-all-start) | async-done | bytes 65568 | tf_op jit(solution)/shard_map/all_to_all | solution.py:291
  19.8 1.1 first_direction.1
  20.9 15.2 %all_to_all.30.near = bf16[16,64,256]{2,1,0:T(8,128)(2,1)S(1)} all-to-all(bf16[16,64,256]{2,1,0:T(8,128)(2,1)S(1)} %get-tuple-element.26), channel_id=1, replica_groups=mesh['x'=4,'y'=4,'z'=4,'c'=2] {'y','x'}, dimensions={0} | all-to-all | bytes 1048576 | tf_op jit(solution)/shard_map/all_to_all | solution.py:291
  36.1 1.9 %bring_slot.1 = (bf16[1024,512]{1,0:T(8,128)(2,1)S(1)}, bf16[1024,1024]{1,0:T(8,128)(2,1)S(1)}) custom-call(bf16[2,1024,512]{2,1,0:T(8,128)(2,1)} %couplings.5, bf16[2,1024,1024]{2,1,0:T(8,128)(2,1)} %factors.5), custom_call_target="tpu_custom_call" | custom-call | bytes 1048576 | tf_op jit(solution)/shard_map/bring_slot/pallas_call | solution.py:351
  38.0 2.2 %slots.2 = (f32[8,64,128]{2,1,0:T(8,128)S(1)}, f32[8,64,128]{2,1,0:T(8,128)S(1)}) custom-call(s32[14]{0:T(128)S(1)} %concatenate.3.table, bf16[16,64,256]{2,1,0:T(8,128)(2,1)S(1)} %all_to_all.30.near, bf16[16,64,256]{2,1,0:T(8,128)(2,1)S(1)} %collective-permute-done.3.far, bf16[1024,512]{1,0:T(8,128)(2,1)S(1)} %get-tuple-element.27.coup_a, ...), custom_call_target="tpu_custom_call" | custom-call | flops 1610612736 | bytes 8388608 | tf_op jit(solution)/shard_map/slots/pallas_call | solution.py:307
  40.3 4.0 %collective-permute-start.4 = (f32[8,64,128]{2,1,0:T(8,128)S(1)}, f32[8,64,128]{2,1,0:T(8,128)S(1)}, u32[]{:S(2)}, u32[]{:S(2)}) collective-permute-start(f32[8,64,128]{2,1,0:T(8,128)S(1)} %get-tuple-element.30), channel_id=1, source_target_pairs={{0,1},{1,0},{2,3},{3,2},{4,5},{5,4},{6,7},{7,6},{8,9},{9,8},{10,11... | collective-permute-start | bytes 786440 | tf_op jit(solution)/shard_map/ppermute | solution.py:287
  44.2 1.2 collective-permute-done.4.got
  45.4 1.0 parcels.2
  46.4 26.3 %all_to_all.31.arrived = bf16[64,16,512]{2,1,0:T(8,128)(2,1)S(1)} all-to-all(bf16[64,16,512]{2,1,0:T(8,128)(2,1)S(1)} %parcels.2), channel_id=1, replica_groups=mesh['x'=4,'y'=4,'z'=4,'c'=2] {'y','x','z'}, dimensions={0} | all-to-all | bytes 2097152 | tf_op jit(solution)/shard_map/all_to_all | solution.py:291
  72.6 0.5 second_direction.1
  73.1 17.1 %all_to_all.32 = bf16[64,16,256]{2,1,0:T(8,128)(2,1)S(1)} all-to-all(bf16[64,16,256]{2,1,0:T(8,128)(2,1)S(1)} %get-tuple-element.32), channel_id=1, replica_groups=mesh['x'=4,'y'=4,'z'=4,'c'=2] {'y','x','z'}, dimensions={0} | all-to-all | bytes 1048576 | tf_op jit(solution)/shard_map/all_to_all | solution.py:291
  90.3 1.9 %collective-permute-done.5.far = bf16[16,64,256]{2,1,0:T(8,128)(2,1)S(1)} collective-permute-done((bf16[16,64,256]{2,1,0:T(8,128)(2,1)S(1)}, bf16[16,64,256]{2,1,0:T(8,128)(2,1)S(1)}, u32[]{:S(2)}, u32[]{:S(2)}) %collective-permute-start.5) | collective-permute-done | bytes 524320 | tf_op jit(solution)/shard_map/ppermute | solution.py:287
  92.2 2.2 %slots.3 = (f32[8,64,128]{2,1,0:T(8,128)S(1)}, f32[8,64,128]{2,1,0:T(8,128)S(1)}) custom-call(s32[14]{0:T(128)S(1)} %concatenate.3.table, bf16[16,64,256]{2,1,0:T(8,128)(2,1)S(1)} %bitcast.6, bf16[16,64,256]{2,1,0:T(8,128)(2,1)S(1)} %collective-permute-done.5.far, bf16[1024,512]{1,0:T(8,128)(2,1)S(1)} %get-tuple-element.27.coup_a, ...), custom_call_target="tpu_custom_call" | custom-call | flops 1610612736 | bytes 8388608 | tf_op jit(solution)/shard_map/slots/pallas_call | solution.py:307
  94.4 3.6 %collective-permute-start.6 = (f32[8,64,128]{2,1,0:T(8,128)S(1)}, f32[8,64,128]{2,1,0:T(8,128)S(1)}, u32[]{:S(2)}, u32[]{:S(2)}) collective-permute-start(f32[8,64,128]{2,1,0:T(8,128)S(1)} %get-tuple-element.34), channel_id=1, source_target_pairs={{0,1},{1,0},{2,3},{3,2},{4,5},{5,4},{6,7},{7,6},{8,9},{9,8},{10,11... | collective-permute-start | bytes 786440 | tf_op jit(solution)/shard_map/ppermute | solution.py:287
  98.0 1.2 collective-permute-done.6.got
  99.2 0.8 parcels.3
  100.0 18.2 %all_to_all.33.arrived = bf16[64,16,256]{2,1,0:T(8,128)(2,1)S(1)} all-to-all(bf16[64,16,256]{2,1,0:T(8,128)(2,1)S(1)} %parcels.3), channel_id=1, replica_groups=mesh['x'=4,'y'=4,'z'=4,'c'=2] {'y','x','z'}, dimensions={0} | all-to-all | bytes 1048576 | tf_op jit(solution)/shard_map/all_to_all | solution.py:291
  118.2 0.7 products.1
  119.0 15.2 %all_to_all.34.near = f32[64,8,128]{2,1,0:T(8,128)S(1)} all-to-all(f32[64,8,128]{2,1,0:T(8,128)S(1)} %products.1), channel_id=1, replica_groups=mesh['x'=4,'y'=4,'z'=4,'c'=2] {'y','x','z'}, dimensions={0} | all-to-all | bytes 524288 | tf_op jit(solution)/shard_map/all_to_all | solution.py:291
  134.1 1.5 %collective-permute-done.7.far = f32[64,8,128]{2,1,0:T(8,128)S(1)} collective-permute-done((f32[64,8,128]{2,1,0:T(8,128)S(1)}, f32[64,8,128]{2,1,0:T(8,128)S(1)}, u32[]{:S(2)}, u32[]{:S(2)}) %collective-permute-start.7) | collective-permute-done | bytes 262176 | tf_op jit(solution)/shard_map/ppermute | solution.py:287
  135.7 1.3 closing.1
  (14 shorter events, 0.0 us)
Async XLA Ops:
  0.0 19.8 %collective-permute-start.2 = (f32[256,128]{1,0:T(8,128)}, f32[256,128]{1,0:T(8,128)S(1)}, u32[]{:S(2)}, u32[]{:S(2)}) collective-permute-start(f32[256,128]{1,0:T(8,128)} %rhs.1), channel_id=1, source_target_pairs={{0,120},{8,16},{16,8},{24,32},{32,24},{40,48},{48,40},{56,64},{64,... | collective-permute-start | bytes 393224 | tf_op jit(solution)/shard_map/ppermute | solution.py:296
  5.3 14.5 %collective-permute-start.1 = (f32[256,128]{1,0:T(8,128)}, f32[256,128]{1,0:T(8,128)S(1)}, u32[]{:S(2)}, u32[]{:S(2)}) collective-permute-start(f32[256,128]{1,0:T(8,128)} %rhs.1), channel_id=1, source_target_pairs={{0,8},{8,0},{16,24},{24,16},{32,40},{40,32},{48,56},{56,48},{64,72... | collective-permute-start | bytes 393224 | tf_op jit(solution)/shard_map/ppermute | solution.py:295
  5.3 1.0 copy-start.2
  6.3 0.7 copy-start.3
  8.2 11.6 %all-to-all-start = ((f32[16,8,128]{2,1,0:T(8,128)}), f32[16,8,128]{2,1,0:T(8,128)S(1)}, u32[]{:S(2)}, u32[]{:S(2)}) async-start(f32[16,8,128]{2,1,0:T(8,128)} %get-tuple-element.23), calls=%async_computation | async-start | bytes 131072 | tf_op jit(solution)/shard_map/all_to_all | solution.py:291
  13.6 2.1 %collective-permute-start = (s32[14]{0:T(128)S(1)}, s32[14]{0:T(128)S(1)}, u32[]{:S(2)}, u32[]{:S(2)}) collective-permute-start(s32[14]{0:T(128)S(1)} %concatenate.3.table), channel_id=1, source_target_pairs={{0,1},{1,0},{2,3},{3,2},{4,5},{5,4},{6,7},{7,6},{8,9},{9,8},{10,11... | collective-permute-start | bytes 176 | tf_op jit(solution)/shard_map/ppermute | solution.py:287
  13.6 1.0 copy-start
  14.6 0.9 copy-start.1
  36.1 1.9 %collective-permute-start.3 = (bf16[16,64,256]{2,1,0:T(8,128)(2,1)S(1)}, bf16[16,64,256]{2,1,0:T(8,128)(2,1)S(1)}, u32[]{:S(2)}, u32[]{:S(2)}) collective-permute-start(bf16[16,64,256]{2,1,0:T(8,128)(2,1)S(1)} %all_to_all.30.near), channel_id=1, source_target_pairs={{0,1},{1,0},{2,3},{3,2},{4,5},{5,4},{6,7},{7,6},{8,9},{9,8},{10,11... | collective-permute-start | bytes 1572872 | tf_op jit(solution)/shard_map/ppermute | solution.py:287
  40.3 5.1 %collective-permute-start.4 = (f32[8,64,128]{2,1,0:T(8,128)S(1)}, f32[8,64,128]{2,1,0:T(8,128)S(1)}, u32[]{:S(2)}, u32[]{:S(2)}) collective-permute-start(f32[8,64,128]{2,1,0:T(8,128)S(1)} %get-tuple-element.30), channel_id=1, source_target_pairs={{0,1},{1,0},{2,3},{3,2},{4,5},{5,4},{6,7},{7,6},{8,9},{9,8},{10,11... | collective-permute-start | bytes 786440 | tf_op jit(solution)/shard_map/ppermute | solution.py:287
  90.3 1.9 %collective-permute-start.5 = (bf16[16,64,256]{2,1,0:T(8,128)(2,1)S(1)}, bf16[16,64,256]{2,1,0:T(8,128)(2,1)S(1)}, u32[]{:S(2)}, u32[]{:S(2)}) collective-permute-start(bf16[16,64,256]{2,1,0:T(8,128)(2,1)S(1)} %bitcast.5), channel_id=1, source_target_pairs={{0,1},{1,0},{2,3},{3,2},{4,5},{5,4},{6,7},{7,6},{8,9},{9,8},{10,11... | collective-permute-start | bytes 1572872 | tf_op jit(solution)/shard_map/ppermute | solution.py:287
  94.4 4.7 %collective-permute-start.6 = (f32[8,64,128]{2,1,0:T(8,128)S(1)}, f32[8,64,128]{2,1,0:T(8,128)S(1)}, u32[]{:S(2)}, u32[]{:S(2)}) collective-permute-start(f32[8,64,128]{2,1,0:T(8,128)S(1)} %get-tuple-element.34), channel_id=1, source_target_pairs={{0,1},{1,0},{2,3},{3,2},{4,5},{5,4},{6,7},{7,6},{8,9},{9,8},{10,11... | collective-permute-start | bytes 786440 | tf_op jit(solution)/shard_map/ppermute | solution.py:287
  134.1 1.5 %collective-permute-start.7 = (f32[64,8,128]{2,1,0:T(8,128)S(1)}, f32[64,8,128]{2,1,0:T(8,128)S(1)}, u32[]{:S(2)}, u32[]{:S(2)}) collective-permute-start(f32[64,8,128]{2,1,0:T(8,128)S(1)} %all_to_all.34.near), channel_id=1, source_target_pairs={{0,1},{1,0},{2,3},{3,2},{4,5},{5,4},{6,7},{7,6},{8,9},{9,8},{10,11... | collective-permute-start | bytes 786440 | tf_op jit(solution)/shard_map/ppermute | solution.py:287

commit v7 on v6

--- a/solution.py
+++ b/solution.py
@@ -80,14 +80,24 @@
         copy.wait()
 
 
-def bring_slot(couplings, factors, coup, fact, sems):
-    copies = [
-        pltpu.make_async_copy(couplings.at[0], coup, sems.at[0]),
-        pltpu.make_async_copy(factors.at[0], fact, sems.at[1]),
-    ]
-    for copy in copies:
+def bring_slots(table, couplings, factors, coup_a, coup_b, fact_a, fact_b, sems):
+    def copies(slot, coup, fact):
+        return (
+            pltpu.make_async_copy(couplings.at[slot], coup, sems.at[slot, 0]),
+            pltpu.make_async_copy(factors.at[slot], fact, sems.at[slot, 1]),
+        )
+
+    for copy in copies(0, coup_a, fact_a):
         copy.start()
-    for copy in copies:
+
+    @pl.when(table[LIVE] > 1)
+    def _():
+        for copy in copies(1, coup_b, fact_b):
+            copy.start()
+        for copy in copies(1, coup_b, fact_b):
+            copy.wait()
+
+    for copy in copies(0, coup_a, fact_a):
         copy.wait()
 
 
@@ -116,32 +126,8 @@
 
 
 def slots(
-    table,
-    near,
-    far,
-    coup_a,
-    fact_a,
-    couplings,
-    factors,
-    kept,
-    given,
-    coup_b,
-    fact_b,
-    picked,
-    one,
-    two,
-    sems,
+    table, near, far, coup_a, coup_b, fact_a, fact_b, kept, given, picked, one, two
 ):
-    second = [
-        pltpu.make_async_copy(couplings.at[1], coup_b, sems.at[0]),
-        pltpu.make_async_copy(factors.at[1], fact_b, sems.at[1]),
-    ]
-
-    @pl.when(table[LIVE] > 1)
-    def _():
-        for copy in second:
-            copy.start()
-
     def slot(number, coup, fact):
         for j in range(4):
             block = table[IDS + number * 4 + j]
@@ -169,8 +155,6 @@
 
     @pl.when(table[LIVE] > 1)
     def _():
-        for copy in second:
-            copy.wait()
         slot(1, coup_b, fact_b)
 
     @pl.when(table[LIVE] < 2)
@@ -308,19 +292,15 @@
             slots,
             "slots",
             [out((8, HALF, BI), F32), out((8, HALF, BI), F32)],
-            [SMEM] + [VMEM] * 4 + [HBM] * 2,
+            [SMEM] + [VMEM] * 6,
             [
-                pltpu.VMEM((1024, 512), BF16),
-                pltpu.VMEM((1024, 1024), BF16),
                 pltpu.VMEM((COLS, 512), BF16),
                 pltpu.VMEM((COLS, 1024), BF16),
                 pltpu.VMEM((COLS, 1024), BF16),
-                pltpu.SemaphoreType.DMA((2,)),
             ],
             flops=2 * 805306368,
             moved=8 << 20,
-            room=50500 << 10,
-        )(table, near, far, *operators, couplings, factors)
+        )(table, near, far, *operators)
 
     def to_owners(kept, given, width):
         got = other_core(given)
@@ -349,13 +329,13 @@
         [pltpu.SemaphoreType.DMA((2,))],
     )(precond, schur_diag)
     operators = call(
-        bring_slot,
-        "bring_slot",
-        [out((1024, 512), BF16), out((1024, 1024), BF16)],
-        [HBM, HBM],
-        [pltpu.SemaphoreType.DMA((2,))],
-        room=52000 << 10,
-    )(couplings, factors)
+        bring_slots,
+        "bring_slots",
+        [out((1024, 512), BF16)] * 2 + [out((1024, 1024), BF16)] * 2,
+        [SMEM, HBM, HBM],
+        [pltpu.SemaphoreType.DMA((2, 2))],
+        room=46000 << 10,
+    )(table, couplings, factors)
     sent, z_one, base, basis = call(
         first_direction,
         "first_direction",

time: 138 us -> 136 us (0.986)
  starting transfers between devices: 16.8 us -> 10.1 us
  blocking collectives: 92 us -> 94.8 us
    ppermute x6, starting transfers between devices: 7.57 us -> 0.84 us  [other_core(): return lax.ppermute(array, 'c', [(0, 1), (1, 0)])]
    all_to_all x5, blocking collectives: 92 us -> 94.8 us  [swap_all(): return lax.all_to_all(array, axes, split_axis=0, concat_axis=0, tiled=True)]
    unnamed x8 -> x10, local copies, waits for them, and re-layouts: 3.47 us -> 3.48 us
  transfers between devices with their start and end apart: 9 -> 9, of which waited for: 5 -> 5; matrix products, arithmetic and copies ran while one was open for 1% -> 1% of each run, Pallas kernels for 2% -> 3%
where the time goes in v7:
time: 136 us; the launch traced here: 134 us
  blocking collectives  94.8 us (70%)
  Pallas kernels  13.6 us (10%)
  starting transfers between devices  10.1 us (7%)
  waiting for transfers between devices  10.1 us (7%)
  local copies, waits for them, and re-layouts  4.33 us (3%)
    all_to_all x5, blocking collectives, swap_all(): return lax.all_to_all(array, axes, split_axis=0, concat_axis=0, tiled=True)  94.8 us
    ppermute x6, waiting for transfers between devices, other_core(): return lax.ppermute(array, 'c', [(0, 1), (1, 0)])  5.98 us
    ppermute x1, starting transfers between devices, neighbours(): lax.ppermute(array, SUB, [(i, (i - 1 + 2 * (i & 1)) % GROUPS) for i in ra...  5.32 us
    pallas_call x2, Pallas kernels, apply_slots(): call(slots, 'slots', [out((8, HALF, BI), F32), out((8, HALF, BI), F32)],...  4.4 us
    all_to_all x1, waiting for transfers between devices, swap_all(): return lax.all_to_all(array, axes, split_axis=0, concat_axis=0, tiled=True)  4.06 us
    all_to_all x1, starting transfers between devices, swap_all(): return lax.all_to_all(array, axes, split_axis=0, concat_axis=0, tiled=True)  3.93 us
    unnamed x10, local copies, waits for them, and re-layouts  3.48 us
  transfers between devices with their start and end apart: 9, of which 5 were waited for; matrix products, arithmetic and copies ran while one was open for 1% of the time, Pallas kernels for 3%

profile of v7, /device:TPU:0, one launch (start us, length us, event | category | flops | bytes accessed | tf_op | source)
XLA Modules:
  0.0 133.7 jit_solution(11246223587285303932)
XLA Ops:
  0.0 5.3 %collective-permute-start.2 = (f32[256,128]{1,0:T(8,128)}, f32[256,128]{1,0:T(8,128)S(1)}, u32[]{:S(2)}, u32[]{:S(2)}) collective-permute-start(f32[256,128]{1,0:T(8,128)} %rhs.1), channel_id=1, source_target_pairs={{0,120},{8,16},{16,8},{24,32},{32,24},{40,48},{48,40},{56,64},{64,... | collective-permute-start | bytes 393224 | tf_op jit(solution)/shard_map/ppermute | solution.py:280
  5.3 1.0 copy-done.3
  6.3 0.7 copy-done.4
  7.0 1.2 opening.1
  8.2 3.9 %all-to-all-start = ((f32[16,8,128]{2,1,0:T(8,128)}), f32[16,8,128]{2,1,0:T(8,128)S(1)}, u32[]{:S(2)}, u32[]{:S(2)}) async-start(f32[16,8,128]{2,1,0:T(8,128)} %get-tuple-element.25), calls=%async_computation | async-start | bytes 131072 | tf_op jit(solution)/shard_map/all_to_all | solution.py:275
  12.8 0.8 reshape.10
  13.5 0.1 concatenate.3.table
  13.6 0.0 collective-permute-start
  13.6 0.9 copy-done.1
  14.6 0.9 copy-done.2
  15.5 0.2 bring_owned.1
  15.7 4.1 %all-to-all-done.facts = f32[16,8,128]{2,1,0:T(8,128)S(1)} async-done(((f32[16,8,128]{2,1,0:T(8,128)}), f32[16,8,128]{2,1,0:T(8,128)S(1)}, u32[]{:S(2)}, u32[]{:S(2)}) %all-to-all-start) | async-done | bytes 65568 | tf_op jit(solution)/shard_map/all_to_all | solution.py:275
  19.8 1.1 first_direction.1
  20.9 15.2 %all_to_all.30.near = bf16[16,64,256]{2,1,0:T(8,128)(2,1)S(1)} all-to-all(bf16[16,64,256]{2,1,0:T(8,128)(2,1)S(1)} %get-tuple-element.28), channel_id=1, replica_groups=mesh['x'=4,'y'=4,'z'=4,'c'=2] {'y','x'}, dimensions={0} | all-to-all | bytes 1048576 | tf_op jit(solution)/shard_map/all_to_all | solution.py:275
  36.1 2.2 %bring_slots.1 = (bf16[1024,512]{1,0:T(8,128)(2,1)S(1)}, bf16[1024,512]{1,0:T(8,128)(2,1)S(1)}, bf16[1024,1024]{1,0:T(8,128)(2,1)S(1)}, bf16[1024,1024]{1,0:T(8,128)(2,1)S(1)}) custom-call(s32[14]{0:T(128)S(1)} %concatenate.3.table, bf16[2,1024,512]{2,1,0:T(8,128)(2,1)S(1)} %copy-done, bf16[2,1024,1024]{2,1,0:T(8,128)(2,1)} %factors.1), custom_call_target="tpu_custom_call" | custom-call | bytes 1048576 | tf_op jit(solution)/shard_map/bring_slots/pallas_call | solution.py:331
  38.3 2.2 %slots.2 = (f32[8,64,128]{2,1,0:T(8,128)S(1)}, f32[8,64,128]{2,1,0:T(8,128)S(1)}) custom-call(s32[14]{0:T(128)S(1)} %concatenate.3.table, bf16[16,64,256]{2,1,0:T(8,128)(2,1)S(1)} %all_to_all.30.near, bf16[16,64,256]{2,1,0:T(8,128)(2,1)S(1)} %collective-permute-done.3.far, bf16[1024,512]{1,0:T(8,128)(2,1)S(1)} %get-tuple-element.29.coup_a, ...), custom_call_target="tpu_custom_call" | custom-call | flops 1610612736 | bytes 8388608 | tf_op jit(solution)/shard_map/slots/pallas_call | solution.py:291
  40.6 0.6 collective-permute-start.4
  41.1 1.2 collective-permute-done.4.got
  42.3 1.0 parcels.2
  43.3 28.3 %all_to_all.31.arrived = bf16[64,16,512]{2,1,0:T(8,128)(2,1)S(1)} all-to-all(bf16[64,16,512]{2,1,0:T(8,128)(2,1)S(1)} %parcels.2), channel_id=1, replica_groups=mesh['x'=4,'y'=4,'z'=4,'c'=2] {'y','x','z'}, dimensions={0} | all-to-all | bytes 2097152 | tf_op jit(solution)/shard_map/all_to_all | solution.py:275
  71.6 0.5 second_direction.1
  72.1 16.7 %all_to_all.32 = bf16[64,16,256]{2,1,0:T(8,128)(2,1)S(1)} all-to-all(bf16[64,16,256]{2,1,0:T(8,128)(2,1)S(1)} %get-tuple-element.36), channel_id=1, replica_groups=mesh['x'=4,'y'=4,'z'=4,'c'=2] {'y','x','z'}, dimensions={0} | all-to-all | bytes 1048576 | tf_op jit(solution)/shard_map/all_to_all | solution.py:275
  88.8 1.9 %collective-permute-done.5.far = bf16[16,64,256]{2,1,0:T(8,128)(2,1)S(1)} collective-permute-done((bf16[16,64,256]{2,1,0:T(8,128)(2,1)S(1)}, bf16[16,64,256]{2,1,0:T(8,128)(2,1)S(1)}, u32[]{:S(2)}, u32[]{:S(2)}) %collective-permute-start.5) | collective-permute-done | bytes 524320 | tf_op jit(solution)/shard_map/ppermute | solution.py:271
  90.8 2.2 %slots.3 = (f32[8,64,128]{2,1,0:T(8,128)S(1)}, f32[8,64,128]{2,1,0:T(8,128)S(1)}) custom-call(s32[14]{0:T(128)S(1)} %concatenate.3.table, bf16[16,64,256]{2,1,0:T(8,128)(2,1)S(1)} %bitcast.6, bf16[16,64,256]{2,1,0:T(8,128)(2,1)S(1)} %collective-permute-done.5.far, bf16[1024,512]{1,0:T(8,128)(2,1)S(1)} %get-tuple-element.29.coup_a, ...), custom_call_target="tpu_custom_call" | custom-call | flops 1610612736 | bytes 8388608 | tf_op jit(solution)/shard_map/slots/pallas_call | solution.py:291
  93.0 0.2 collective-permute-start.6
  93.2 1.4 %collective-permute-done.6.got = f32[8,64,128]{2,1,0:T(8,128)S(1)} collective-permute-done((f32[8,64,128]{2,1,0:T(8,128)S(1)}, f32[8,64,128]{2,1,0:T(8,128)S(1)}, u32[]{:S(2)}, u32[]{:S(2)}) %collective-permute-start.6) | collective-permute-done | bytes 262176 | tf_op jit(solution)/shard_map/ppermute | solution.py:271
  94.6 0.8 parcels.3
  95.4 19.5 %all_to_all.33.arrived = bf16[64,16,256]{2,1,0:T(8,128)(2,1)S(1)} all-to-all(bf16[64,16,256]{2,1,0:T(8,128)(2,1)S(1)} %parcels.3), channel_id=1, replica_groups=mesh['x'=4,'y'=4,'z'=4,'c'=2] {'y','x','z'}, dimensions={0} | all-to-all | bytes 1048576 | tf_op jit(solution)/shard_map/all_to_all | solution.py:275
  114.9 0.7 products.1
  115.6 15.2 %all_to_all.34.near = f32[64,8,128]{2,1,0:T(8,128)S(1)} all-to-all(f32[64,8,128]{2,1,0:T(8,128)S(1)} %products.1), channel_id=1, replica_groups=mesh['x'=4,'y'=4,'z'=4,'c'=2] {'y','x','z'}, dimensions={0} | all-to-all | bytes 524288 | tf_op jit(solution)/shard_map/all_to_all | solution.py:275
  130.8 1.5 %collective-permute-done.7.far = f32[64,8,128]{2,1,0:T(8,128)S(1)} collective-permute-done((f32[64,8,128]{2,1,0:T(8,128)S(1)}, f32[64,8,128]{2,1,0:T(8,128)S(1)}, u32[]{:S(2)}, u32[]{:S(2)}) %collective-permute-start.7) | collective-permute-done | bytes 262176 | tf_op jit(solution)/shard_map/ppermute | solution.py:271
  132.3 1.3 %closing.1 = f32[256,128]{1,0:T(8,128)} custom-call(s32[14]{0:T(128)S(1)} %concatenate.3.table, f32[64,8,128]{2,1,0:T(8,128)S(1)} %all_to_all.34.near, f32[64,8,128]{2,1,0:T(8,128)S(1)} %collective-permute-done.7.far, f32[16,8,128]{2,1,0:T(8,128)S(1)} %all-to-all-done.facts, f32[256,128]{1,0:T(8,128)S(1)} %get-tuple-element.42.z_one, ...), custom_call_target="tpu_custom_call" | custom-call | bytes 1048576 | tf_op jit(solution)/shard_map/closing/pallas_call | solution.py:373
  (16 shorter events, 0.0 us)
Async XLA Ops:
  0.0 36.1 %copy-start = (bf16[2,1024,512]{2,1,0:T(8,128)(2,1)S(1)}, bf16[2,1024,512]{2,1,0:T(8,128)(2,1)}, u32[]{:S(2)}) copy-start(bf16[2,1024,512]{2,1,0:T(8,128)(2,1)} %couplings.1) | copy-start | bytes 6291460
  0.0 19.8 %collective-permute-start.2 = (f32[256,128]{1,0:T(8,128)}, f32[256,128]{1,0:T(8,128)S(1)}, u32[]{:S(2)}, u32[]{:S(2)}) collective-permute-start(f32[256,128]{1,0:T(8,128)} %rhs.1), channel_id=1, source_target_pairs={{0,120},{8,16},{16,8},{24,32},{32,24},{40,48},{48,40},{56,64},{64,... | collective-permute-start | bytes 393224 | tf_op jit(solution)/shard_map/ppermute | solution.py:280
  5.3 14.5 %collective-permute-start.1 = (f32[256,128]{1,0:T(8,128)}, f32[256,128]{1,0:T(8,128)S(1)}, u32[]{:S(2)}, u32[]{:S(2)}) collective-permute-start(f32[256,128]{1,0:T(8,128)} %rhs.1), channel_id=1, source_target_pairs={{0,8},{8,0},{16,24},{24,16},{32,40},{40,32},{48,56},{56,48},{64,72... | collective-permute-start | bytes 393224 | tf_op jit(solution)/shard_map/ppermute | solution.py:279
  5.3 1.0 copy-start.3
  6.3 0.7 copy-start.4
  8.2 11.6 %all-to-all-start = ((f32[16,8,128]{2,1,0:T(8,128)}), f32[16,8,128]{2,1,0:T(8,128)S(1)}, u32[]{:S(2)}, u32[]{:S(2)}) async-start(f32[16,8,128]{2,1,0:T(8,128)} %get-tuple-element.25), calls=%async_computation | async-start | bytes 131072 | tf_op jit(solution)/shard_map/all_to_all | solution.py:275
  13.6 2.1 %collective-permute-start = (s32[14]{0:T(128)S(1)}, s32[14]{0:T(128)S(1)}, u32[]{:S(2)}, u32[]{:S(2)}) collective-permute-start(s32[14]{0:T(128)S(1)} %concatenate.3.table), channel_id=1, source_target_pairs={{0,1},{1,0},{2,3},{3,2},{4,5},{5,4},{6,7},{7,6},{8,9},{9,8},{10,11... | collective-permute-start | bytes 176 | tf_op jit(solution)/shard_map/ppermute | solution.py:271
  13.6 1.0 copy-start.1
  14.6 0.9 copy-start.2
  36.1 2.3 %collective-permute-start.3 = (bf16[16,64,256]{2,1,0:T(8,128)(2,1)S(1)}, bf16[16,64,256]{2,1,0:T(8,128)(2,1)S(1)}, u32[]{:S(2)}, u32[]{:S(2)}) collective-permute-start(bf16[16,64,256]{2,1,0:T(8,128)(2,1)S(1)} %all_to_all.30.near), channel_id=1, source_target_pairs={{0,1},{1,0},{2,3},{3,2},{4,5},{5,4},{6,7},{7,6},{8,9},{9,8},{10,11... | collective-permute-start | bytes 1572872 | tf_op jit(solution)/shard_map/ppermute | solution.py:271
  40.6 1.8 %collective-permute-start.4 = (f32[8,64,128]{2,1,0:T(8,128)S(1)}, f32[8,64,128]{2,1,0:T(8,128)S(1)}, u32[]{:S(2)}, u32[]{:S(2)}) collective-permute-start(f32[8,64,128]{2,1,0:T(8,128)S(1)} %get-tuple-element.34), channel_id=1, source_target_pairs={{0,1},{1,0},{2,3},{3,2},{4,5},{5,4},{6,7},{7,6},{8,9},{9,8},{10,11... | collective-permute-start | bytes 786440 | tf_op jit(solution)/shard_map/ppermute | solution.py:271
  88.8 1.9 %collective-permute-start.5 = (bf16[16,64,256]{2,1,0:T(8,128)(2,1)S(1)}, bf16[16,64,256]{2,1,0:T(8,128)(2,1)S(1)}, u32[]{:S(2)}, u32[]{:S(2)}) collective-permute-start(bf16[16,64,256]{2,1,0:T(8,128)(2,1)S(1)} %bitcast.5), channel_id=1, source_target_pairs={{0,1},{1,0},{2,3},{3,2},{4,5},{5,4},{6,7},{7,6},{8,9},{9,8},{10,11... | collective-permute-start | bytes 1572872 | tf_op jit(solution)/shard_map/ppermute | solution.py:271
  93.0 1.6 %collective-permute-start.6 = (f32[8,64,128]{2,1,0:T(8,128)S(1)}, f32[8,64,128]{2,1,0:T(8,128)S(1)}, u32[]{:S(2)}, u32[]{:S(2)}) collective-permute-start(f32[8,64,128]{2,1,0:T(8,128)S(1)} %get-tuple-element.38), channel_id=1, source_target_pairs={{0,1},{1,0},{2,3},{3,2},{4,5},{5,4},{6,7},{7,6},{8,9},{9,8},{10,11... | collective-permute-start | bytes 786440 | tf_op jit(solution)/shard_map/ppermute | solution.py:271
  130.8 1.5 %collective-permute-start.7 = (f32[64,8,128]{2,1,0:T(8,128)S(1)}, f32[64,8,128]{2,1,0:T(8,128)S(1)}, u32[]{:S(2)}, u32[]{:S(2)}) collective-permute-start(f32[64,8,128]{2,1,0:T(8,128)S(1)} %all_to_all.34.near), channel_id=1, source_target_pairs={{0,1},{1,0},{2,3},{3,2},{4,5},{5,4},{6,7},{7,6},{8,9},{9,8},{10,11... | collective-permute-start | bytes 786440 | tf_op jit(solution)/shard_map/ppermute | solution.py:271

commit v8 on v7

--- a/solution.py
+++ b/solution.py
@@ -33,10 +33,9 @@
     return lax.dot_general(left, right, dims, preferred_element_type=F32)
 
 
-def call(body, name, outs, specs, scratch=(), flops=0, moved=1 << 20, room=4 << 20):
+def call(body, outs, specs, scratch=(), flops=0, moved=1 << 20, room=4 << 20):
     return pl.pallas_call(
         body,
-        name=name,
         out_shape=outs,
         in_specs=specs,
         out_specs=[VMEM] * len(outs),
@@ -102,15 +101,15 @@
 
 
 def first_direction(
-    table, table_far, rhs, paired, linked, facts, precond, diag, sent, z_nat, base, basis, turned
+    table, table_far, rhs, own, other, facts, precond, diag, sent, z_nat, base, basis, turned
 ):
     beta = jnp.sqrt(jnp.sum(facts[:, 0:1, :], axis=0))
     v = rhs[...] / beta
-    odd = (table[GROUP] & 1) == 1
     lower = block_at(table, HALO)
     upper = block_at(table, HALO + 1)
-    left = jnp.where(odd, paired[lower, :], linked[lower, :]) / beta
-    right = jnp.where(odd, linked[upper, :], paired[upper, :]) / beta
+    flip = ((table[GROUP] + table[CORE]) & 1) == 1
+    left = jnp.where(flip, own[lower, :], other[lower, :]) / beta
+    right = jnp.where(flip, other[upper, :], own[upper, :]) / beta
     patch = jnp.concatenate([v, left, right], axis=0).astype(BF16)
     z = v + dot(precond[...], patch)
     z_nat[...] = z
@@ -275,10 +274,12 @@
     return lax.all_to_all(array, axes, split_axis=0, concat_axis=0, tiled=True)
 
 
-def neighbours(array):
-    paired = lax.ppermute(array, SUB, [(i, i ^ 1) for i in range(GROUPS)])
-    linked = lax.ppermute(array, SUB, [(i, (i - 1 + 2 * (i & 1)) % GROUPS) for i in range(GROUPS)])
-    return paired, linked
+def one_neighbour(array):
+    pairs = []
+    for i in range(GROUPS):
+        pairs.append((2 * i, 2 * (i ^ 1)))
+        pairs.append((2 * i + 1, 2 * ((i - 1 + 2 * (i & 1)) % GROUPS) + 1))
+    return lax.ppermute(array, ("x", "y", "c"), pairs)
 
 
 def on_device(rhs, schur_diag, precond, halo_ids, factors, couplings, block_ids, counts):
@@ -290,7 +291,6 @@
     def apply_slots(near, far):
         return call(
             slots,
-            "slots",
             [out((8, HALF, BI), F32), out((8, HALF, BI), F32)],
             [SMEM] + [VMEM] * 6,
             [
@@ -306,31 +306,26 @@
         got = other_core(given)
         (sent,) = call(
             parcels,
-            "parcels",
             [out((64, PART, width), BF16)],
             [SMEM, SMEM, VMEM, VMEM, VMEM, VMEM],
             [pltpu.VMEM((BLOCKS, HALF, BI), F32)],
         )(table, table_far, kept, got, facts, base)
         return swap_all(sent, YXZ)
 
-    paired, linked = neighbours(rhs)
+    own = one_neighbour(rhs)
+    other = other_core(own)
     opened, held = call(
-        opening,
-        "opening",
-        [out((GROUPS, 8, COLS), F32), out((ROWS, COLS), F32)],
-        [SMEM, VMEM],
+        opening, [out((GROUPS, 8, COLS), F32), out((ROWS, COLS), F32)], [SMEM, VMEM]
     )(halo_ids, rhs)
     facts = swap_all(opened, YX)
     precond_v, diag_v = call(
         bring_owned,
-        "bring_owned",
         [out(precond.shape, BF16), out(schur_diag.shape, BF16)],
         [HBM, HBM],
         [pltpu.SemaphoreType.DMA((2,))],
     )(precond, schur_diag)
     operators = call(
         bring_slots,
-        "bring_slots",
         [out((1024, 512), BF16)] * 2 + [out((1024, 1024), BF16)] * 2,
         [SMEM, HBM, HBM],
         [pltpu.SemaphoreType.DMA((2, 2))],
@@ -338,7 +333,6 @@
     )(table, couplings, factors)
     sent, z_one, base, basis = call(
         first_direction,
-        "first_direction",
         [
             out((GROUPS, HALF, ROWS), BF16),
             out((ROWS, COLS), F32),
@@ -348,14 +342,13 @@
         [SMEM, SMEM, VMEM, VMEM, VMEM, VMEM, VMEM, VMEM],
         [pltpu.VMEM((COLS, ROWS), F32)],
         flops=1 << 26,
-    )(table, table_far, held, paired, linked, facts, precond_v, diag_v)
+    )(table, table_far, held, own, other, facts, precond_v, diag_v)
     near = swap_all(sent, YX)
     far = other_core(near)
     kept, given = apply_slots(near, far)
     arrived = to_owners(kept, given, 2 * ROWS)
     sent, base, w = call(
         second_direction,
-        "second_direction",
         [out((64, PART, ROWS), BF16), out((PART, ROWS), F32), out((PART, ROWS), F32)],
         [VMEM, VMEM, VMEM, VMEM],
         flops=1 << 26,
@@ -365,13 +358,13 @@
     kept, given = apply_slots(near, far)
     arrived = to_owners(kept, given, ROWS)
     (sent,) = call(
-        products, "products", [out((64, 8, COLS), F32)], [SMEM, VMEM, VMEM, VMEM, VMEM]
+        products, [out((64, 8, COLS), F32)], [SMEM, VMEM, VMEM, VMEM, VMEM]
     )(table, arrived, base, w, basis)
     sums = swap_all(sent, YXZ)
     sums_far = other_core(sums)
     own = [lax.dynamic_slice_in_dim(half, partner(group), 1, 0) for half in (near, far)]
     (answer,) = call(
-        closing, "closing", [out((ROWS, COLS), F32)], [SMEM] + [VMEM] * 6
+        closing, [out((ROWS, COLS), F32)], [SMEM] + [VMEM] * 6
     )(table, sums, sums_far, facts, z_one, *own)
     return answer
 
@@ -388,6 +381,7 @@
         P(ALL, None),
         P(ALL),
     )
+
     return jax.shard_map(
         on_device, mesh=torus, in_specs=placed, out_specs=P(SUB, None), check_vma=False
     )

time: 136 us -> 141 us (1.037)
  Pallas kernels: 13.6 us -> 17.5 us
  waiting for transfers between devices: 10.1 us -> 14 us
  blocking collectives: 94.8 us -> 92 us
    pallas_call x11, Pallas kernels: 13.6 us -> 17.5 us  [the longest x2 7.63 us: apply_slots(): call(slots, [out((8, HALF, BI), F32), out((8, HALF, BI), F32)], [SMEM] +...]
    ppermute x2 -> x1, starting transfers between devices: 5.32 us -> 1.69 us  [one_neighbour(): return lax.ppermute(array, ('x', 'y', 'c'), pairs)]
    ppermute x2 -> x1, waiting for transfers between devices: 0.01 us -> 3.49 us  [one_neighbour(): return lax.ppermute(array, ('x', 'y', 'c'), pairs)]
    all_to_all x5, blocking collectives: 94.8 us -> 92 us  [swap_all(): return lax.all_to_all(array, axes, split_axis=0, concat_axis=0, tiled=True)]
    all_to_all x1, starting transfers between devices: 3.93 us -> 6.44 us  [swap_all(): return lax.all_to_all(array, axes, split_axis=0, concat_axis=0, tiled=True)]
    ppermute x6 -> x7, starting transfers between devices: 0.84 us -> 2.46 us  [other_core(): return lax.ppermute(array, 'c', [(0, 1), (1, 0)])]
    ppermute x6 -> x7, waiting for transfers between devices: 5.98 us -> 6.48 us  [other_core(): return lax.ppermute(array, 'c', [(0, 1), (1, 0)])]
  transfers between devices with their start and end apart: 9 -> 9, of which waited for: 5 -> 6; matrix products, arithmetic and copies ran while one was open for 1% -> 1% of each run, Pallas kernels for 3% -> 3%
where the time goes in v8:
time: 141 us; the launch traced here: 139 us
  blocking collectives  92 us (65%)
  Pallas kernels  17.5 us (12%)
  waiting for transfers between devices  14 us (10%)
  starting transfers between devices  10.6 us (8%)
  local copies, waits for them, and re-layouts  4.26 us (3%)
    all_to_all x5, blocking collectives, swap_all(): return lax.all_to_all(array, axes, split_axis=0, concat_axis=0, tiled=True)  92 us
    pallas_call x2, Pallas kernels, apply_slots(): call(slots, [out((8, HALF, BI), F32), out((8, HALF, BI), F32)], [SMEM] +...  7.63 us
    ppermute x7, waiting for transfers between devices, other_core(): return lax.ppermute(array, 'c', [(0, 1), (1, 0)])  6.48 us
    all_to_all x1, starting transfers between devices, swap_all(): return lax.all_to_all(array, axes, split_axis=0, concat_axis=0, tiled=True)  6.44 us
    all_to_all x1, waiting for transfers between devices, swap_all(): return lax.all_to_all(array, axes, split_axis=0, concat_axis=0, tiled=True)  4.06 us
    ppermute x1, waiting for transfers between devices, one_neighbour(): return lax.ppermute(array, ('x', 'y', 'c'), pairs)  3.49 us
    unnamed x10, local copies, waits for them, and re-layouts  3.41 us
    pallas_call x1, Pallas kernels, on_device(): call(bring_slots, [out((1024, 512), BF16)] * 2 + [out((1024, 1024), BF16)...  2.89 us
  transfers between devices with their start and end apart: 9, of which 6 were waited for; matrix products, arithmetic and copies ran while one was open for 1% of the time, Pallas kernels for 3%

profile of v8, /device:TPU:0, one launch (start us, length us, event | category | flops | bytes accessed | tf_op | source)
XLA Modules:
  0.0 139.2 jit_solution(1603761504888778876)
XLA Ops:
  0.0 1.7 %collective-permute-start.1 = (f32[256,128]{1,0:T(8,128)}, f32[256,128]{1,0:T(8,128)S(1)}, u32[]{:S(2)}, u32[]{:S(2)}) collective-permute-start(f32[256,128]{1,0:T(8,128)} %rhs.1), channel_id=1, source_target_pairs={{0,8},{1,121},{8,0},{9,17},{16,24},{17,9},{24,16},{25,33},{32,40},... | collective-permute-start | bytes 393224 | tf_op jit(solution)/shard_map/ppermute | solution.py:282
  1.7 3.5 %collective-permute-done.1.own = f32[256,128]{1,0:T(8,128)S(1)} collective-permute-done((f32[256,128]{1,0:T(8,128)}, f32[256,128]{1,0:T(8,128)S(1)}, u32[]{:S(2)}, u32[]{:S(2)}) %collective-permute-start.1) | collective-permute-done | bytes 131104 | tf_op jit(solution)/shard_map/ppermute | solution.py:282
  5.2 2.3 %collective-permute-start.2 = (f32[256,128]{1,0:T(8,128)S(1)}, f32[256,128]{1,0:T(8,128)S(1)}, u32[]{:S(2)}, u32[]{:S(2)}) collective-permute-start(f32[256,128]{1,0:T(8,128)S(1)} %collective-permute-done.1.own), channel_id=1, source_target_pairs={{0,1},{1,0},{2,3},{3,2},{4,5},{5,4},{6,7},{7,6},{8,9},{9,8},{10,11... | collective-permute-start | bytes 393224 | tf_op jit(solution)/shard_map/ppermute | solution.py:270
  7.4 0.9 copy-done.3
  8.4 0.7 copy-done.4
  9.0 1.2 shard_map.82
  10.2 6.4 %all-to-all-start = ((f32[16,8,128]{2,1,0:T(8,128)}), f32[16,8,128]{2,1,0:T(8,128)S(1)}, u32[]{:S(2)}, u32[]{:S(2)}) async-start(f32[16,8,128]{2,1,0:T(8,128)} %get-tuple-element.25), calls=%async_computation | async-start | bytes 131072 | tf_op jit(solution)/shard_map/all_to_all | solution.py:274
  17.3 0.8 reshape.10
  18.2 0.9 copy-done.1
  19.2 0.9 copy-done.2
  20.1 0.2 shard_map.83
  20.3 4.1 %all-to-all-done.facts = f32[16,8,128]{2,1,0:T(8,128)S(1)} async-done(((f32[16,8,128]{2,1,0:T(8,128)}), f32[16,8,128]{2,1,0:T(8,128)S(1)}, u32[]{:S(2)}, u32[]{:S(2)}) %all-to-all-start) | async-done | bytes 65568 | tf_op jit(solution)/shard_map/all_to_all | solution.py:274
  24.3 1.1 shard_map.84
  25.5 15.2 %all_to_all.30.near = bf16[16,64,256]{2,1,0:T(8,128)(2,1)S(1)} all-to-all(bf16[16,64,256]{2,1,0:T(8,128)(2,1)S(1)} %get-tuple-element.28), channel_id=1, replica_groups=mesh['x'=4,'y'=4,'z'=4,'c'=2] {'y','x'}, dimensions={0} | all-to-all | bytes 1048576 | tf_op jit(solution)/shard_map/all_to_all | solution.py:274
  40.6 2.9 %shard_map.85 = (bf16[1024,512]{1,0:T(8,128)(2,1)S(1)}, bf16[1024,512]{1,0:T(8,128)(2,1)S(1)}, bf16[1024,1024]{1,0:T(8,128)(2,1)S(1)}, bf16[1024,1024]{1,0:T(8,128)(2,1)S(1)}) custom-call(s32[14]{0:T(128)S(1)} %concatenate.3.table, bf16[2,1024,512]{2,1,0:T(8,128)(2,1)S(1)} %copy-done, bf16[2,1024,1024]{2,1,0:T(8,128)(2,1)} %factors.1), custom_call_target="tpu_custom_call" | custom-call | bytes 1048576 | tf_op jit(solution)/shard_map/pallas_call | solution.py:327
  43.6 3.8 %shard_map.86 = (f32[8,64,128]{2,1,0:T(8,128)S(1)}, f32[8,64,128]{2,1,0:T(8,128)S(1)}) custom-call(s32[14]{0:T(128)S(1)} %concatenate.3.table, bf16[16,64,256]{2,1,0:T(8,128)(2,1)S(1)} %all_to_all.30.near, bf16[16,64,256]{2,1,0:T(8,128)(2,1)S(1)} %collective-permute-done.3.far, bf16[1024,512]{1,0:T(8,128)(2,1)S(1)} %get-tuple-element.29.coup_a, ...), custom_call_target="tpu_custom_call" | custom-call | flops 1610612736 | bytes 8388608 | tf_op jit(solution)/shard_map/pallas_call | solution.py:292
  47.4 0.1 collective-permute-start.4
  47.5 1.5 %collective-permute-done.4.got = f32[8,64,128]{2,1,0:T(8,128)S(1)} collective-permute-done((f32[8,64,128]{2,1,0:T(8,128)S(1)}, f32[8,64,128]{2,1,0:T(8,128)S(1)}, u32[]{:S(2)}, u32[]{:S(2)}) %collective-permute-start.4) | collective-permute-done | bytes 262176 | tf_op jit(solution)/shard_map/ppermute | solution.py:270
  49.0 1.0 shard_map.87
  50.0 26.4 %all_to_all.31.arrived = bf16[64,16,512]{2,1,0:T(8,128)(2,1)S(1)} all-to-all(bf16[64,16,512]{2,1,0:T(8,128)(2,1)S(1)} %shard_map.87), channel_id=1, replica_groups=mesh['x'=4,'y'=4,'z'=4,'c'=2] {'y','x','z'}, dimensions={0} | all-to-all | bytes 2097152 | tf_op jit(solution)/shard_map/all_to_all | solution.py:274
  76.4 0.5 shard_map.88
  76.9 17.1 %all_to_all.32 = bf16[64,16,256]{2,1,0:T(8,128)(2,1)S(1)} all-to-all(bf16[64,16,256]{2,1,0:T(8,128)(2,1)S(1)} %get-tuple-element.36), channel_id=1, replica_groups=mesh['x'=4,'y'=4,'z'=4,'c'=2] {'y','x','z'}, dimensions={0} | all-to-all | bytes 1048576 | tf_op jit(solution)/shard_map/all_to_all | solution.py:274
  94.0 1.9 %collective-permute-done.5.far = bf16[16,64,256]{2,1,0:T(8,128)(2,1)S(1)} collective-permute-done((bf16[16,64,256]{2,1,0:T(8,128)(2,1)S(1)}, bf16[16,64,256]{2,1,0:T(8,128)(2,1)S(1)}, u32[]{:S(2)}, u32[]{:S(2)}) %collective-permute-start.5) | collective-permute-done | bytes 524320 | tf_op jit(solution)/shard_map/ppermute | solution.py:270
  95.9 3.8 %shard_map.89 = (f32[8,64,128]{2,1,0:T(8,128)S(1)}, f32[8,64,128]{2,1,0:T(8,128)S(1)}) custom-call(s32[14]{0:T(128)S(1)} %concatenate.3.table, bf16[16,64,256]{2,1,0:T(8,128)(2,1)S(1)} %bitcast.6, bf16[16,64,256]{2,1,0:T(8,128)(2,1)S(1)} %collective-permute-done.5.far, bf16[1024,512]{1,0:T(8,128)(2,1)S(1)} %get-tuple-element.29.coup_a, ...), custom_call_target="tpu_custom_call" | custom-call | flops 1610612736 | bytes 8388608 | tf_op jit(solution)/shard_map/pallas_call | solution.py:292
  99.8 0.1 collective-permute-start.6
  99.9 1.5 %collective-permute-done.6.got = f32[8,64,128]{2,1,0:T(8,128)S(1)} collective-permute-done((f32[8,64,128]{2,1,0:T(8,128)S(1)}, f32[8,64,128]{2,1,0:T(8,128)S(1)}, u32[]{:S(2)}, u32[]{:S(2)}) %collective-permute-start.6) | collective-permute-done | bytes 262176 | tf_op jit(solution)/shard_map/ppermute | solution.py:270
  101.4 0.8 shard_map.90
  102.2 18.2 %all_to_all.33.arrived = bf16[64,16,256]{2,1,0:T(8,128)(2,1)S(1)} all-to-all(bf16[64,16,256]{2,1,0:T(8,128)(2,1)S(1)} %shard_map.90), channel_id=1, replica_groups=mesh['x'=4,'y'=4,'z'=4,'c'=2] {'y','x','z'}, dimensions={0} | all-to-all | bytes 1048576 | tf_op jit(solution)/shard_map/all_to_all | solution.py:274
  120.4 0.7 shard_map.91
  121.1 15.2 %all_to_all.34.near = f32[64,8,128]{2,1,0:T(8,128)S(1)} all-to-all(f32[64,8,128]{2,1,0:T(8,128)S(1)} %shard_map.91), channel_id=1, replica_groups=mesh['x'=4,'y'=4,'z'=4,'c'=2] {'y','x','z'}, dimensions={0} | all-to-all | bytes 524288 | tf_op jit(solution)/shard_map/all_to_all | solution.py:274
  136.3 1.5 %collective-permute-done.7.far = f32[64,8,128]{2,1,0:T(8,128)S(1)} collective-permute-done((f32[64,8,128]{2,1,0:T(8,128)S(1)}, f32[64,8,128]{2,1,0:T(8,128)S(1)}, u32[]{:S(2)}, u32[]{:S(2)}) %collective-permute-start.7) | collective-permute-done | bytes 262176 | tf_op jit(solution)/shard_map/ppermute | solution.py:270
  137.8 1.3 shard_map.92
  (16 shorter events, 0.1 us)
Async XLA Ops:
  0.0 40.6 %copy-start = (bf16[2,1024,512]{2,1,0:T(8,128)(2,1)S(1)}, bf16[2,1024,512]{2,1,0:T(8,128)(2,1)}, u32[]{:S(2)}) copy-start(bf16[2,1024,512]{2,1,0:T(8,128)(2,1)} %couplings.1) | copy-start | bytes 6291460
  0.0 5.2 %collective-permute-start.1 = (f32[256,128]{1,0:T(8,128)}, f32[256,128]{1,0:T(8,128)S(1)}, u32[]{:S(2)}, u32[]{:S(2)}) collective-permute-start(f32[256,128]{1,0:T(8,128)} %rhs.1), channel_id=1, source_target_pairs={{0,8},{1,121},{8,0},{9,17},{16,24},{17,9},{24,16},{25,33},{32,40},... | collective-permute-start | bytes 393224 | tf_op jit(solution)/shard_map/ppermute | solution.py:282
  5.2 19.2 %collective-permute-start.2 = (f32[256,128]{1,0:T(8,128)S(1)}, f32[256,128]{1,0:T(8,128)S(1)}, u32[]{:S(2)}, u32[]{:S(2)}) collective-permute-start(f32[256,128]{1,0:T(8,128)S(1)} %collective-permute-done.1.own), channel_id=1, source_target_pairs={{0,1},{1,0},{2,3},{3,2},{4,5},{5,4},{6,7},{7,6},{8,9},{9,8},{10,11... | collective-permute-start | bytes 393224 | tf_op jit(solution)/shard_map/ppermute | solution.py:270
  7.4 0.9 copy-start.3
  8.3 0.7 copy-start.4
  10.2 14.1 %all-to-all-start = ((f32[16,8,128]{2,1,0:T(8,128)}), f32[16,8,128]{2,1,0:T(8,128)S(1)}, u32[]{:S(2)}, u32[]{:S(2)}) async-start(f32[16,8,128]{2,1,0:T(8,128)} %get-tuple-element.25), calls=%async_computation | async-start | bytes 131072 | tf_op jit(solution)/shard_map/all_to_all | solution.py:274
  18.2 2.1 %collective-permute-start = (s32[14]{0:T(128)S(1)}, s32[14]{0:T(128)S(1)}, u32[]{:S(2)}, u32[]{:S(2)}) collective-permute-start(s32[14]{0:T(128)S(1)} %concatenate.3.table), channel_id=1, source_target_pairs={{0,1},{1,0},{2,3},{3,2},{4,5},{5,4},{6,7},{7,6},{8,9},{9,8},{10,11... | collective-permute-start | bytes 176 | tf_op jit(solution)/shard_map/ppermute | solution.py:270
  18.2 1.0 copy-start.1
  19.1 0.9 copy-start.2
  40.6 2.9 %collective-permute-start.3 = (bf16[16,64,256]{2,1,0:T(8,128)(2,1)S(1)}, bf16[16,64,256]{2,1,0:T(8,128)(2,1)S(1)}, u32[]{:S(2)}, u32[]{:S(2)}) collective-permute-start(bf16[16,64,256]{2,1,0:T(8,128)(2,1)S(1)} %all_to_all.30.near), channel_id=1, source_target_pairs={{0,1},{1,0},{2,3},{3,2},{4,5},{5,4},{6,7},{7,6},{8,9},{9,8},{10,11... | collective-permute-start | bytes 1572872 | tf_op jit(solution)/shard_map/ppermute | solution.py:270
  47.4 1.6 %collective-permute-start.4 = (f32[8,64,128]{2,1,0:T(8,128)S(1)}, f32[8,64,128]{2,1,0:T(8,128)S(1)}, u32[]{:S(2)}, u32[]{:S(2)}) collective-permute-start(f32[8,64,128]{2,1,0:T(8,128)S(1)} %get-tuple-element.34), channel_id=1, source_target_pairs={{0,1},{1,0},{2,3},{3,2},{4,5},{5,4},{6,7},{7,6},{8,9},{9,8},{10,11... | collective-permute-start | bytes 786440 | tf_op jit(solution)/shard_map/ppermute | solution.py:270
  94.0 1.9 %collective-permute-start.5 = (bf16[16,64,256]{2,1,0:T(8,128)(2,1)S(1)}, bf16[16,64,256]{2,1,0:T(8,128)(2,1)S(1)}, u32[]{:S(2)}, u32[]{:S(2)}) collective-permute-start(bf16[16,64,256]{2,1,0:T(8,128)(2,1)S(1)} %bitcast.5), channel_id=1, source_target_pairs={{0,1},{1,0},{2,3},{3,2},{4,5},{5,4},{6,7},{7,6},{8,9},{9,8},{10,11... | collective-permute-start | bytes 1572872 | tf_op jit(solution)/shard_map/ppermute | solution.py:270
  99.8 1.6 %collective-permute-start.6 = (f32[8,64,128]{2,1,0:T(8,128)S(1)}, f32[8,64,128]{2,1,0:T(8,128)S(1)}, u32[]{:S(2)}, u32[]{:S(2)}) collective-permute-start(f32[8,64,128]{2,1,0:T(8,128)S(1)} %get-tuple-element.38), channel_id=1, source_target_pairs={{0,1},{1,0},{2,3},{3,2},{4,5},{5,4},{6,7},{7,6},{8,9},{9,8},{10,11... | collective-permute-start | bytes 786440 | tf_op jit(solution)/shard_map/ppermute | solution.py:270
  136.3 1.5 %collective-permute-start.7 = (f32[64,8,128]{2,1,0:T(8,128)S(1)}, f32[64,8,128]{2,1,0:T(8,128)S(1)}, u32[]{:S(2)}, u32[]{:S(2)}) collective-permute-start(f32[64,8,128]{2,1,0:T(8,128)S(1)} %all_to_all.34.near), channel_id=1, source_target_pairs={{0,1},{1,0},{2,3},{3,2},{4,5},{5,4},{6,7},{7,6},{8,9},{9,8},{10,11... | collective-permute-start | bytes 786440 | tf_op jit(solution)/shard_map/ppermute | solution.py:270

commit v9 on v8

--- a/solution.py
+++ b/solution.py
@@ -57,9 +57,11 @@
     return pl.ds(pl.multiple_of((table[place] & 1) * BI, BI), BI)
 
 
-def opening(halo, rhs, sent, held):
-    field = rhs[...]
-    held[...] = field
+def opening(halo, rhs, sent, held, sem):
+    copy = pltpu.make_async_copy(rhs, held, sem)
+    copy.start()
+    copy.wait()
+    field = held[...]
     sums = jnp.sum(field * field, axis=0, keepdims=True)
     row = lax.broadcasted_iota(jnp.int32, (8, COLS), 0)
     left = (halo[0, 0] & 1).astype(F32)
@@ -315,7 +317,11 @@
     own = one_neighbour(rhs)
     other = other_core(own)
     opened, held = call(
-        opening, [out((GROUPS, 8, COLS), F32), out((ROWS, COLS), F32)], [SMEM, VMEM]
+        opening,
+        [out((GROUPS, 8, COLS), F32), out((ROWS, COLS), F32)],
+        [SMEM, HBM],
+        [pltpu.SemaphoreType.DMA],
+        room=55000 << 10,
     )(halo_ids, rhs)
     facts = swap_all(opened, YX)
     precond_v, diag_v = call(

time: 141 us -> 141 us (level)
    unnamed x10 -> x8, local copies, waits for them, and re-layouts: 3.41 us -> 2.51 us
  transfers between devices with their start and end apart: 9 -> 9, of which waited for: 6 -> 6; matrix products, arithmetic and copies ran while one was open for 1% -> 1% of each run, Pallas kernels for 3% -> 4%
where the time goes in v9:
time: 141 us; the launch traced here: 139 us
  blocking collectives  92 us (65%)
  Pallas kernels  18.4 us (13%)
  waiting for transfers between devices  14 us (10%)
  starting transfers between devices  10.6 us (8%)
  local copies, waits for them, and re-layouts  3.36 us (2%)
    all_to_all x5, blocking collectives, swap_all(): return lax.all_to_all(array, axes, split_axis=0, concat_axis=0, tiled=True)  92 us
    pallas_call x2, Pallas kernels, apply_slots(): call(slots, [out((8, HALF, BI), F32), out((8, HALF, BI), F32)], [SMEM] +...  7.63 us
    ppermute x7, waiting for transfers between devices, other_core(): return lax.ppermute(array, 'c', [(0, 1), (1, 0)])  6.48 us
    all_to_all x1, starting transfers between devices, swap_all(): return lax.all_to_all(array, axes, split_axis=0, concat_axis=0, tiled=True)  6.46 us
    all_to_all x1, waiting for transfers between devices, swap_all(): return lax.all_to_all(array, axes, split_axis=0, concat_axis=0, tiled=True)  4.06 us
    ppermute x1, waiting for transfers between devices, one_neighbour(): return lax.ppermute(array, ('x', 'y', 'c'), pairs)  3.49 us
    pallas_call x1, Pallas kernels, on_device(): call(bring_slots, [out((1024, 512), BF16)] * 2 + [out((1024, 1024), BF16)...  2.89 us
  transfers between devices with their start and end apart: 9, of which 6 were waited for; matrix products, arithmetic and copies ran while one was open for 1% of the time, Pallas kernels for 4%

profile of v9, /device:TPU:0, one launch (start us, length us, event | category | flops | bytes accessed | tf_op | source)
XLA Modules:
  0.0 139.2 jit_solution(10376697044052655550)
XLA Ops:
  0.0 1.7 %collective-permute-start.1 = (f32[256,128]{1,0:T(8,128)}, f32[256,128]{1,0:T(8,128)S(1)}, u32[]{:S(2)}, u32[]{:S(2)}) collective-permute-start(f32[256,128]{1,0:T(8,128)} %rhs.1), channel_id=1, source_target_pairs={{0,8},{1,121},{8,0},{9,17},{16,24},{17,9},{24,16},{25,33},{32,40},... | collective-permute-start | bytes 393224 | tf_op jit(solution)/shard_map/ppermute | solution.py:284
  1.7 3.5 %collective-permute-done.1.own = f32[256,128]{1,0:T(8,128)S(1)} collective-permute-done((f32[256,128]{1,0:T(8,128)}, f32[256,128]{1,0:T(8,128)S(1)}, u32[]{:S(2)}, u32[]{:S(2)}) %collective-permute-start.1) | collective-permute-done | bytes 131104 | tf_op jit(solution)/shard_map/ppermute | solution.py:284
  5.2 2.3 %collective-permute-start.2 = (f32[256,128]{1,0:T(8,128)S(1)}, f32[256,128]{1,0:T(8,128)S(1)}, u32[]{:S(2)}, u32[]{:S(2)}) collective-permute-start(f32[256,128]{1,0:T(8,128)S(1)} %collective-permute-done.1.own), channel_id=1, source_target_pairs={{0,1},{1,0},{2,3},{3,2},{4,5},{5,4},{6,7},{7,6},{8,9},{9,8},{10,11... | collective-permute-start | bytes 393224 | tf_op jit(solution)/shard_map/ppermute | solution.py:272
  7.4 0.7 copy-done.3
  8.1 2.1 %shard_map.82 = (f32[16,8,128]{2,1,0:T(8,128)}, f32[256,128]{1,0:T(8,128)S(1)}) custom-call(s32[1,2]{1,0:T(1,128)S(1)} %copy-done.3, f32[256,128]{1,0:T(8,128)} %rhs.1), custom_call_target="tpu_custom_call" | custom-call | bytes 1048576 | tf_op jit(solution)/shard_map/pallas_call | solution.py:319
  10.2 6.5 %all-to-all-start = ((f32[16,8,128]{2,1,0:T(8,128)}), f32[16,8,128]{2,1,0:T(8,128)S(1)}, u32[]{:S(2)}, u32[]{:S(2)}) async-start(f32[16,8,128]{2,1,0:T(8,128)} %get-tuple-element.25), calls=%async_computation | async-start | bytes 131072 | tf_op jit(solution)/shard_map/all_to_all | solution.py:276
  17.4 0.8 reshape.10
  18.1 0.1 concatenate.3.table
  18.2 0.9 copy-done.1
  19.2 0.9 copy-done.2
  20.1 0.2 shard_map.83
  20.3 4.1 %all-to-all-done.facts = f32[16,8,128]{2,1,0:T(8,128)S(1)} async-done(((f32[16,8,128]{2,1,0:T(8,128)}), f32[16,8,128]{2,1,0:T(8,128)S(1)}, u32[]{:S(2)}, u32[]{:S(2)}) %all-to-all-start) | async-done | bytes 65568 | tf_op jit(solution)/shard_map/all_to_all | solution.py:276
  24.4 1.1 shard_map.84
  25.5 15.2 %all_to_all.30.near = bf16[16,64,256]{2,1,0:T(8,128)(2,1)S(1)} all-to-all(bf16[16,64,256]{2,1,0:T(8,128)(2,1)S(1)} %get-tuple-element.28), channel_id=1, replica_groups=mesh['x'=4,'y'=4,'z'=4,'c'=2] {'y','x'}, dimensions={0} | all-to-all | bytes 1048576 | tf_op jit(solution)/shard_map/all_to_all | solution.py:276
  40.7 2.9 %shard_map.85 = (bf16[1024,512]{1,0:T(8,128)(2,1)S(1)}, bf16[1024,512]{1,0:T(8,128)(2,1)S(1)}, bf16[1024,1024]{1,0:T(8,128)(2,1)S(1)}, bf16[1024,1024]{1,0:T(8,128)(2,1)S(1)}) custom-call(s32[14]{0:T(128)S(1)} %concatenate.3.table, bf16[2,1024,512]{2,1,0:T(8,128)(2,1)S(1)} %copy-done, bf16[2,1024,1024]{2,1,0:T(8,128)(2,1)} %factors.1), custom_call_target="tpu_custom_call" | custom-call | bytes 1048576 | tf_op jit(solution)/shard_map/pallas_call | solution.py:333
  43.6 3.8 %shard_map.86 = (f32[8,64,128]{2,1,0:T(8,128)S(1)}, f32[8,64,128]{2,1,0:T(8,128)S(1)}) custom-call(s32[14]{0:T(128)S(1)} %concatenate.3.table, bf16[16,64,256]{2,1,0:T(8,128)(2,1)S(1)} %all_to_all.30.near, bf16[16,64,256]{2,1,0:T(8,128)(2,1)S(1)} %collective-permute-done.3.far, bf16[1024,512]{1,0:T(8,128)(2,1)S(1)} %get-tuple-element.29.coup_a, ...), custom_call_target="tpu_custom_call" | custom-call | flops 1610612736 | bytes 8388608 | tf_op jit(solution)/shard_map/pallas_call | solution.py:294
  47.4 0.1 collective-permute-start.4
  47.5 1.5 %collective-permute-done.4.got = f32[8,64,128]{2,1,0:T(8,128)S(1)} collective-permute-done((f32[8,64,128]{2,1,0:T(8,128)S(1)}, f32[8,64,128]{2,1,0:T(8,128)S(1)}, u32[]{:S(2)}, u32[]{:S(2)}) %collective-permute-start.4) | collective-permute-done | bytes 262176 | tf_op jit(solution)/shard_map/ppermute | solution.py:272
  49.0 1.0 shard_map.87
  50.0 26.4 %all_to_all.31.arrived = bf16[64,16,512]{2,1,0:T(8,128)(2,1)S(1)} all-to-all(bf16[64,16,512]{2,1,0:T(8,128)(2,1)S(1)} %shard_map.87), channel_id=1, replica_groups=mesh['x'=4,'y'=4,'z'=4,'c'=2] {'y','x','z'}, dimensions={0} | all-to-all | bytes 2097152 | tf_op jit(solution)/shard_map/all_to_all | solution.py:276
  76.4 0.5 shard_map.88
  76.9 17.1 %all_to_all.32 = bf16[64,16,256]{2,1,0:T(8,128)(2,1)S(1)} all-to-all(bf16[64,16,256]{2,1,0:T(8,128)(2,1)S(1)} %get-tuple-element.36), channel_id=1, replica_groups=mesh['x'=4,'y'=4,'z'=4,'c'=2] {'y','x','z'}, dimensions={0} | all-to-all | bytes 1048576 | tf_op jit(solution)/shard_map/all_to_all | solution.py:276
  94.0 1.9 %collective-permute-done.5.far = bf16[16,64,256]{2,1,0:T(8,128)(2,1)S(1)} collective-permute-done((bf16[16,64,256]{2,1,0:T(8,128)(2,1)S(1)}, bf16[16,64,256]{2,1,0:T(8,128)(2,1)S(1)}, u32[]{:S(2)}, u32[]{:S(2)}) %collective-permute-start.5) | collective-permute-done | bytes 524320 | tf_op jit(solution)/shard_map/ppermute | solution.py:272
  96.0 3.8 %shard_map.89 = (f32[8,64,128]{2,1,0:T(8,128)S(1)}, f32[8,64,128]{2,1,0:T(8,128)S(1)}) custom-call(s32[14]{0:T(128)S(1)} %concatenate.3.table, bf16[16,64,256]{2,1,0:T(8,128)(2,1)S(1)} %bitcast.6, bf16[16,64,256]{2,1,0:T(8,128)(2,1)S(1)} %collective-permute-done.5.far, bf16[1024,512]{1,0:T(8,128)(2,1)S(1)} %get-tuple-element.29.coup_a, ...), custom_call_target="tpu_custom_call" | custom-call | flops 1610612736 | bytes 8388608 | tf_op jit(solution)/shard_map/pallas_call | solution.py:294
  99.8 0.1 collective-permute-start.6
  99.9 1.5 %collective-permute-done.6.got = f32[8,64,128]{2,1,0:T(8,128)S(1)} collective-permute-done((f32[8,64,128]{2,1,0:T(8,128)S(1)}, f32[8,64,128]{2,1,0:T(8,128)S(1)}, u32[]{:S(2)}, u32[]{:S(2)}) %collective-permute-start.6) | collective-permute-done | bytes 262176 | tf_op jit(solution)/shard_map/ppermute | solution.py:272
  101.4 0.8 shard_map.90
  102.2 18.2 %all_to_all.33.arrived = bf16[64,16,256]{2,1,0:T(8,128)(2,1)S(1)} all-to-all(bf16[64,16,256]{2,1,0:T(8,128)(2,1)S(1)} %shard_map.90), channel_id=1, replica_groups=mesh['x'=4,'y'=4,'z'=4,'c'=2] {'y','x','z'}, dimensions={0} | all-to-all | bytes 1048576 | tf_op jit(solution)/shard_map/all_to_all | solution.py:276
  120.4 0.7 shard_map.91
  121.1 15.2 %all_to_all.34.near = f32[64,8,128]{2,1,0:T(8,128)S(1)} all-to-all(f32[64,8,128]{2,1,0:T(8,128)S(1)} %shard_map.91), channel_id=1, replica_groups=mesh['x'=4,'y'=4,'z'=4,'c'=2] {'y','x','z'}, dimensions={0} | all-to-all | bytes 524288 | tf_op jit(solution)/shard_map/all_to_all | solution.py:276
  136.3 1.5 %collective-permute-done.7.far = f32[64,8,128]{2,1,0:T(8,128)S(1)} collective-permute-done((f32[64,8,128]{2,1,0:T(8,128)S(1)}, f32[64,8,128]{2,1,0:T(8,128)S(1)}, u32[]{:S(2)}, u32[]{:S(2)}) %collective-permute-start.7) | collective-permute-done | bytes 262176 | tf_op jit(solution)/shard_map/ppermute | solution.py:272
  137.9 1.3 shard_map.92
  (14 shorter events, 0.0 us)
Async XLA Ops:
  0.0 40.7 %copy-start = (bf16[2,1024,512]{2,1,0:T(8,128)(2,1)S(1)}, bf16[2,1024,512]{2,1,0:T(8,128)(2,1)}, u32[]{:S(2)}) copy-start(bf16[2,1024,512]{2,1,0:T(8,128)(2,1)} %couplings.1) | copy-start | bytes 6291460
  0.0 5.2 %collective-permute-start.1 = (f32[256,128]{1,0:T(8,128)}, f32[256,128]{1,0:T(8,128)S(1)}, u32[]{:S(2)}, u32[]{:S(2)}) collective-permute-start(f32[256,128]{1,0:T(8,128)} %rhs.1), channel_id=1, source_target_pairs={{0,8},{1,121},{8,0},{9,17},{16,24},{17,9},{24,16},{25,33},{32,40},... | collective-permute-start | bytes 393224 | tf_op jit(solution)/shard_map/ppermute | solution.py:284
  5.2 19.2 %collective-permute-start.2 = (f32[256,128]{1,0:T(8,128)S(1)}, f32[256,128]{1,0:T(8,128)S(1)}, u32[]{:S(2)}, u32[]{:S(2)}) collective-permute-start(f32[256,128]{1,0:T(8,128)S(1)} %collective-permute-done.1.own), channel_id=1, source_target_pairs={{0,1},{1,0},{2,3},{3,2},{4,5},{5,4},{6,7},{7,6},{8,9},{9,8},{10,11... | collective-permute-start | bytes 393224 | tf_op jit(solution)/shard_map/ppermute | solution.py:272
  7.4 0.7 copy-start.3
  10.2 14.1 %all-to-all-start = ((f32[16,8,128]{2,1,0:T(8,128)}), f32[16,8,128]{2,1,0:T(8,128)S(1)}, u32[]{:S(2)}, u32[]{:S(2)}) async-start(f32[16,8,128]{2,1,0:T(8,128)} %get-tuple-element.25), calls=%async_computation | async-start | bytes 131072 | tf_op jit(solution)/shard_map/all_to_all | solution.py:276
  18.2 2.1 %collective-permute-start = (s32[14]{0:T(128)S(1)}, s32[14]{0:T(128)S(1)}, u32[]{:S(2)}, u32[]{:S(2)}) collective-permute-start(s32[14]{0:T(128)S(1)} %concatenate.3.table), channel_id=1, source_target_pairs={{0,1},{1,0},{2,3},{3,2},{4,5},{5,4},{6,7},{7,6},{8,9},{9,8},{10,11... | collective-permute-start | bytes 176 | tf_op jit(solution)/shard_map/ppermute | solution.py:272
  18.2 1.0 copy-start.1
  19.2 0.9 copy-start.2
  40.7 2.9 %collective-permute-start.3 = (bf16[16,64,256]{2,1,0:T(8,128)(2,1)S(1)}, bf16[16,64,256]{2,1,0:T(8,128)(2,1)S(1)}, u32[]{:S(2)}, u32[]{:S(2)}) collective-permute-start(bf16[16,64,256]{2,1,0:T(8,128)(2,1)S(1)} %all_to_all.30.near), channel_id=1, source_target_pairs={{0,1},{1,0},{2,3},{3,2},{4,5},{5,4},{6,7},{7,6},{8,9},{9,8},{10,11... | collective-permute-start | bytes 1572872 | tf_op jit(solution)/shard_map/ppermute | solution.py:272
  47.4 1.6 %collective-permute-start.4 = (f32[8,64,128]{2,1,0:T(8,128)S(1)}, f32[8,64,128]{2,1,0:T(8,128)S(1)}, u32[]{:S(2)}, u32[]{:S(2)}) collective-permute-start(f32[8,64,128]{2,1,0:T(8,128)S(1)} %get-tuple-element.34), channel_id=1, source_target_pairs={{0,1},{1,0},{2,3},{3,2},{4,5},{5,4},{6,7},{7,6},{8,9},{9,8},{10,11... | collective-permute-start | bytes 786440 | tf_op jit(solution)/shard_map/ppermute | solution.py:272
  94.0 1.9 %collective-permute-start.5 = (bf16[16,64,256]{2,1,0:T(8,128)(2,1)S(1)}, bf16[16,64,256]{2,1,0:T(8,128)(2,1)S(1)}, u32[]{:S(2)}, u32[]{:S(2)}) collective-permute-start(bf16[16,64,256]{2,1,0:T(8,128)(2,1)S(1)} %bitcast.5), channel_id=1, source_target_pairs={{0,1},{1,0},{2,3},{3,2},{4,5},{5,4},{6,7},{7,6},{8,9},{9,8},{10,11... | collective-permute-start | bytes 1572872 | tf_op jit(solution)/shard_map/ppermute | solution.py:272
  99.8 1.6 %collective-permute-start.6 = (f32[8,64,128]{2,1,0:T(8,128)S(1)}, f32[8,64,128]{2,1,0:T(8,128)S(1)}, u32[]{:S(2)}, u32[]{:S(2)}) collective-permute-start(f32[8,64,128]{2,1,0:T(8,128)S(1)} %get-tuple-element.38), channel_id=1, source_target_pairs={{0,1},{1,0},{2,3},{3,2},{4,5},{5,4},{6,7},{7,6},{8,9},{9,8},{10,11... | collective-permute-start | bytes 786440 | tf_op jit(solution)/shard_map/ppermute | solution.py:272
  136.3 1.5 %collective-permute-start.7 = (f32[64,8,128]{2,1,0:T(8,128)S(1)}, f32[64,8,128]{2,1,0:T(8,128)S(1)}, u32[]{:S(2)}, u32[]{:S(2)}) collective-permute-start(f32[64,8,128]{2,1,0:T(8,128)S(1)} %all_to_all.34.near), channel_id=1, source_target_pairs={{0,1},{1,0},{2,3},{3,2},{4,5},{5,4},{6,7},{7,6},{8,9},{9,8},{10,11... | collective-permute-start | bytes 786440 | tf_op jit(solution)/shard_map/ppermute | solution.py:272

commit v10 on v8

--- a/solution.py
+++ b/solution.py
@@ -148,7 +148,7 @@
             for m in range(2):
                 lanes = slice(m * BI, (m + 1) * BI)
                 kept[number * 4 + n * 2 + m] = piece[0:HALF, lanes]
-                given[number * 4 + n * 2 + m] = piece[HALF:COLS, lanes]
+                given[number * 4 + n * 2 + m] = piece[HALF:COLS, lanes].astype(BF16)
 
     slot(0, coup_a, fact_a)
 
@@ -159,7 +159,7 @@
     @pl.when(table[LIVE] < 2)
     def _():
         kept[4:8] = jnp.zeros((4, HALF, BI), F32)
-        given[4:8] = jnp.zeros((4, HALF, BI), F32)
+        given[4:8] = jnp.zeros((4, HALF, BI), BF16)
 
 
 def parcels(table, table_far, kept, got, facts, base, sent, total):
@@ -169,7 +169,7 @@
         total[block] = total[block] + kept[i]
     for i in range(8):
         block = table_far[IDS + i]
-        total[block] = total[block] + got[i]
+        total[block] = total[block] + got[i].astype(F32)
     with_halo = sent.shape[2] > ROWS
 
     def group(d, carry):
@@ -291,7 +291,7 @@
     def apply_slots(near, far):
         return call(
             slots,
-            [out((8, HALF, BI), F32), out((8, HALF, BI), F32)],
+            [out((8, HALF, BI), F32), out((8, HALF, BI), BF16)],
             [SMEM] + [VMEM] * 6,
             [
                 pltpu.VMEM((COLS, 512), BF16),

time: 141 us -> 140 us (level)
  no operation moved by 1% of the time
where the time goes in v10:
time: 140 us; the launch traced here: 139 us
  blocking collectives  92.1 us (66%)
  Pallas kernels  17.5 us (12%)
  waiting for transfers between devices  13.7 us (10%)
  starting transfers between devices  10.6 us (8%)
  local copies, waits for them, and re-layouts  4.26 us (3%)
    all_to_all x5, blocking collectives, swap_all(): return lax.all_to_all(array, axes, split_axis=0, concat_axis=0, tiled=True)  92.1 us
    pallas_call x2, Pallas kernels, apply_slots(): call(slots, [out((8, HALF, BI), F32), out((8, HALF, BI), BF16)], [SMEM] +...  7.63 us
    all_to_all x1, starting transfers between devices, swap_all(): return lax.all_to_all(array, axes, split_axis=0, concat_axis=0, tiled=True)  6.44 us
    ppermute x7, waiting for transfers between devices, other_core(): return lax.ppermute(array, 'c', [(0, 1), (1, 0)])  6.11 us
    all_to_all x1, waiting for transfers between devices, swap_all(): return lax.all_to_all(array, axes, split_axis=0, concat_axis=0, tiled=True)  4.06 us
    ppermute x1, waiting for transfers between devices, one_neighbour(): return lax.ppermute(array, ('x', 'y', 'c'), pairs)  3.49 us
    unnamed x10, local copies, waits for them, and re-layouts  3.41 us
    pallas_call x1, Pallas kernels, on_device(): call(bring_slots, [out((1024, 512), BF16)] * 2 + [out((1024, 1024), BF16)...  2.89 us
  transfers between devices with their start and end apart: 9, of which 6 were waited for; matrix products, arithmetic and copies ran while one was open for 1% of the time, Pallas kernels for 3%

profile of v10, /device:TPU:0, one launch (start us, length us, event | category | flops | bytes accessed | tf_op | source)
XLA Modules:
  0.0 138.8 jit_solution(4158778608760429345)
XLA Ops:
  0.0 1.7 %collective-permute-start.1 = (f32[256,128]{1,0:T(8,128)}, f32[256,128]{1,0:T(8,128)S(1)}, u32[]{:S(2)}, u32[]{:S(2)}) collective-permute-start(f32[256,128]{1,0:T(8,128)} %rhs.1), channel_id=1, source_target_pairs={{0,8},{1,121},{8,0},{9,17},{16,24},{17,9},{24,16},{25,33},{32,40},... | collective-permute-start | bytes 393224 | tf_op jit(solution)/shard_map/ppermute | solution.py:282
  1.7 3.5 %collective-permute-done.1.own = f32[256,128]{1,0:T(8,128)S(1)} collective-permute-done((f32[256,128]{1,0:T(8,128)}, f32[256,128]{1,0:T(8,128)S(1)}, u32[]{:S(2)}, u32[]{:S(2)}) %collective-permute-start.1) | collective-permute-done | bytes 131104 | tf_op jit(solution)/shard_map/ppermute | solution.py:282
  5.2 2.3 %collective-permute-start.2 = (f32[256,128]{1,0:T(8,128)S(1)}, f32[256,128]{1,0:T(8,128)S(1)}, u32[]{:S(2)}, u32[]{:S(2)}) collective-permute-start(f32[256,128]{1,0:T(8,128)S(1)} %collective-permute-done.1.own), channel_id=1, source_target_pairs={{0,1},{1,0},{2,3},{3,2},{4,5},{5,4},{6,7},{7,6},{8,9},{9,8},{10,11... | collective-permute-start | bytes 393224 | tf_op jit(solution)/shard_map/ppermute | solution.py:270
  7.4 0.9 copy-done.3
  8.4 0.7 copy-done.4
  9.0 1.2 shard_map.82
  10.2 6.4 %all-to-all-start = ((f32[16,8,128]{2,1,0:T(8,128)}), f32[16,8,128]{2,1,0:T(8,128)S(1)}, u32[]{:S(2)}, u32[]{:S(2)}) async-start(f32[16,8,128]{2,1,0:T(8,128)} %get-tuple-element.25), calls=%async_computation | async-start | bytes 131072 | tf_op jit(solution)/shard_map/all_to_all | solution.py:274
  17.3 0.8 reshape.10
  18.2 0.9 copy-done.1
  19.2 0.9 copy-done.2
  20.1 0.2 shard_map.83
  20.3 4.1 %all-to-all-done.facts = f32[16,8,128]{2,1,0:T(8,128)S(1)} async-done(((f32[16,8,128]{2,1,0:T(8,128)}), f32[16,8,128]{2,1,0:T(8,128)S(1)}, u32[]{:S(2)}, u32[]{:S(2)}) %all-to-all-start) | async-done | bytes 65568 | tf_op jit(solution)/shard_map/all_to_all | solution.py:274
  24.3 1.1 shard_map.84
  25.5 15.2 %all_to_all.30.near = bf16[16,64,256]{2,1,0:T(8,128)(2,1)S(1)} all-to-all(bf16[16,64,256]{2,1,0:T(8,128)(2,1)S(1)} %get-tuple-element.28), channel_id=1, replica_groups=mesh['x'=4,'y'=4,'z'=4,'c'=2] {'y','x'}, dimensions={0} | all-to-all | bytes 1048576 | tf_op jit(solution)/shard_map/all_to_all | solution.py:274
  40.6 2.9 %shard_map.85 = (bf16[1024,512]{1,0:T(8,128)(2,1)S(1)}, bf16[1024,512]{1,0:T(8,128)(2,1)S(1)}, bf16[1024,1024]{1,0:T(8,128)(2,1)S(1)}, bf16[1024,1024]{1,0:T(8,128)(2,1)S(1)}) custom-call(s32[14]{0:T(128)S(1)} %concatenate.3.table, bf16[2,1024,512]{2,1,0:T(8,128)(2,1)S(1)} %copy-done, bf16[2,1024,1024]{2,1,0:T(8,128)(2,1)} %factors.1), custom_call_target="tpu_custom_call" | custom-call | bytes 1048576 | tf_op jit(solution)/shard_map/pallas_call | solution.py:327
  43.6 3.8 %shard_map.86 = (f32[8,64,128]{2,1,0:T(8,128)S(1)}, bf16[8,64,128]{2,1,0:T(8,128)(2,1)S(1)}) custom-call(s32[14]{0:T(128)S(1)} %concatenate.3.table, bf16[16,64,256]{2,1,0:T(8,128)(2,1)S(1)} %all_to_all.30.near, bf16[16,64,256]{2,1,0:T(8,128)(2,1)S(1)} %collective-permute-done.3.far, bf16[1024,512]{1,0:T(8,128)(2,1)S(1)} %get-tuple-element.29.coup_a, ...), custom_call_target="tpu_custom_call" | custom-call | flops 1610612736 | bytes 8388608 | tf_op jit(solution)/shard_map/pallas_call | solution.py:292
  47.4 0.1 collective-permute-start.4
  47.5 1.3 collective-permute-done.4.got
  48.8 1.0 shard_map.87
  49.8 26.4 %all_to_all.31.arrived = bf16[64,16,512]{2,1,0:T(8,128)(2,1)S(1)} all-to-all(bf16[64,16,512]{2,1,0:T(8,128)(2,1)S(1)} %shard_map.87), channel_id=1, replica_groups=mesh['x'=4,'y'=4,'z'=4,'c'=2] {'y','x','z'}, dimensions={0} | all-to-all | bytes 2097152 | tf_op jit(solution)/shard_map/all_to_all | solution.py:274
  76.2 0.5 shard_map.88
  76.7 17.1 %all_to_all.32 = bf16[64,16,256]{2,1,0:T(8,128)(2,1)S(1)} all-to-all(bf16[64,16,256]{2,1,0:T(8,128)(2,1)S(1)} %get-tuple-element.36), channel_id=1, replica_groups=mesh['x'=4,'y'=4,'z'=4,'c'=2] {'y','x','z'}, dimensions={0} | all-to-all | bytes 1048576 | tf_op jit(solution)/shard_map/all_to_all | solution.py:274
  93.9 1.9 %collective-permute-done.5.far = bf16[16,64,256]{2,1,0:T(8,128)(2,1)S(1)} collective-permute-done((bf16[16,64,256]{2,1,0:T(8,128)(2,1)S(1)}, bf16[16,64,256]{2,1,0:T(8,128)(2,1)S(1)}, u32[]{:S(2)}, u32[]{:S(2)}) %collective-permute-start.5) | collective-permute-done | bytes 524320 | tf_op jit(solution)/shard_map/ppermute | solution.py:270
  95.8 3.8 %shard_map.89 = (f32[8,64,128]{2,1,0:T(8,128)S(1)}, bf16[8,64,128]{2,1,0:T(8,128)(2,1)S(1)}) custom-call(s32[14]{0:T(128)S(1)} %concatenate.3.table, bf16[16,64,256]{2,1,0:T(8,128)(2,1)S(1)} %bitcast.6, bf16[16,64,256]{2,1,0:T(8,128)(2,1)S(1)} %collective-permute-done.5.far, bf16[1024,512]{1,0:T(8,128)(2,1)S(1)} %get-tuple-element.29.coup_a, ...), custom_call_target="tpu_custom_call" | custom-call | flops 1610612736 | bytes 8388608 | tf_op jit(solution)/shard_map/pallas_call | solution.py:292
  99.6 0.1 collective-permute-start.6
  99.7 1.3 collective-permute-done.6.got
  101.0 0.8 shard_map.90
  101.8 18.2 %all_to_all.33.arrived = bf16[64,16,256]{2,1,0:T(8,128)(2,1)S(1)} all-to-all(bf16[64,16,256]{2,1,0:T(8,128)(2,1)S(1)} %shard_map.90), channel_id=1, replica_groups=mesh['x'=4,'y'=4,'z'=4,'c'=2] {'y','x','z'}, dimensions={0} | all-to-all | bytes 1048576 | tf_op jit(solution)/shard_map/all_to_all | solution.py:274
  120.0 0.7 shard_map.91
  120.8 15.2 %all_to_all.34.near = f32[64,8,128]{2,1,0:T(8,128)S(1)} all-to-all(f32[64,8,128]{2,1,0:T(8,128)S(1)} %shard_map.91), channel_id=1, replica_groups=mesh['x'=4,'y'=4,'z'=4,'c'=2] {'y','x','z'}, dimensions={0} | all-to-all | bytes 524288 | tf_op jit(solution)/shard_map/all_to_all | solution.py:274
  136.0 1.5 %collective-permute-done.7.far = f32[64,8,128]{2,1,0:T(8,128)S(1)} collective-permute-done((f32[64,8,128]{2,1,0:T(8,128)S(1)}, f32[64,8,128]{2,1,0:T(8,128)S(1)}, u32[]{:S(2)}, u32[]{:S(2)}) %collective-permute-start.7) | collective-permute-done | bytes 262176 | tf_op jit(solution)/shard_map/ppermute | solution.py:270
  137.5 1.3 shard_map.92
  (16 shorter events, 0.1 us)
Async XLA Ops:
  0.0 40.6 %copy-start = (bf16[2,1024,512]{2,1,0:T(8,128)(2,1)S(1)}, bf16[2,1024,512]{2,1,0:T(8,128)(2,1)}, u32[]{:S(2)}) copy-start(bf16[2,1024,512]{2,1,0:T(8,128)(2,1)} %couplings.1) | copy-start | bytes 6291460
  0.0 5.2 %collective-permute-start.1 = (f32[256,128]{1,0:T(8,128)}, f32[256,128]{1,0:T(8,128)S(1)}, u32[]{:S(2)}, u32[]{:S(2)}) collective-permute-start(f32[256,128]{1,0:T(8,128)} %rhs.1), channel_id=1, source_target_pairs={{0,8},{1,121},{8,0},{9,17},{16,24},{17,9},{24,16},{25,33},{32,40},... | collective-permute-start | bytes 393224 | tf_op jit(solution)/shard_map/ppermute | solution.py:282
  5.2 19.2 %collective-permute-start.2 = (f32[256,128]{1,0:T(8,128)S(1)}, f32[256,128]{1,0:T(8,128)S(1)}, u32[]{:S(2)}, u32[]{:S(2)}) collective-permute-start(f32[256,128]{1,0:T(8,128)S(1)} %collective-permute-done.1.own), channel_id=1, source_target_pairs={{0,1},{1,0},{2,3},{3,2},{4,5},{5,4},{6,7},{7,6},{8,9},{9,8},{10,11... | collective-permute-start | bytes 393224 | tf_op jit(solution)/shard_map/ppermute | solution.py:270
  7.4 0.9 copy-start.3
  8.3 0.7 copy-start.4
  10.2 14.1 %all-to-all-start = ((f32[16,8,128]{2,1,0:T(8,128)}), f32[16,8,128]{2,1,0:T(8,128)S(1)}, u32[]{:S(2)}, u32[]{:S(2)}) async-start(f32[16,8,128]{2,1,0:T(8,128)} %get-tuple-element.25), calls=%async_computation | async-start | bytes 131072 | tf_op jit(solution)/shard_map/all_to_all | solution.py:274
  18.2 2.1 %collective-permute-start = (s32[14]{0:T(128)S(1)}, s32[14]{0:T(128)S(1)}, u32[]{:S(2)}, u32[]{:S(2)}) collective-permute-start(s32[14]{0:T(128)S(1)} %concatenate.3.table), channel_id=1, source_target_pairs={{0,1},{1,0},{2,3},{3,2},{4,5},{5,4},{6,7},{7,6},{8,9},{9,8},{10,11... | collective-permute-start | bytes 176 | tf_op jit(solution)/shard_map/ppermute | solution.py:270
  18.2 1.0 copy-start.1
  19.1 0.9 copy-start.2
  40.6 2.9 %collective-permute-start.3 = (bf16[16,64,256]{2,1,0:T(8,128)(2,1)S(1)}, bf16[16,64,256]{2,1,0:T(8,128)(2,1)S(1)}, u32[]{:S(2)}, u32[]{:S(2)}) collective-permute-start(bf16[16,64,256]{2,1,0:T(8,128)(2,1)S(1)} %all_to_all.30.near), channel_id=1, source_target_pairs={{0,1},{1,0},{2,3},{3,2},{4,5},{5,4},{6,7},{7,6},{8,9},{9,8},{10,11... | collective-permute-start | bytes 1572872 | tf_op jit(solution)/shard_map/ppermute | solution.py:270
  47.4 1.4 %collective-permute-start.4 = (bf16[8,64,128]{2,1,0:T(8,128)(2,1)S(1)}, bf16[8,64,128]{2,1,0:T(8,128)(2,1)S(1)}, u32[]{:S(2)}, u32[]{:S(2)}) collective-permute-start(bf16[8,64,128]{2,1,0:T(8,128)(2,1)S(1)} %get-tuple-element.34), channel_id=1, source_target_pairs={{0,1},{1,0},{2,3},{3,2},{4,5},{5,4},{6,7},{7,6},{8,9},{9,8},{10,11... | collective-permute-start | bytes 393224 | tf_op jit(solution)/shard_map/ppermute | solution.py:270
  93.9 1.9 %collective-permute-start.5 = (bf16[16,64,256]{2,1,0:T(8,128)(2,1)S(1)}, bf16[16,64,256]{2,1,0:T(8,128)(2,1)S(1)}, u32[]{:S(2)}, u32[]{:S(2)}) collective-permute-start(bf16[16,64,256]{2,1,0:T(8,128)(2,1)S(1)} %bitcast.5), channel_id=1, source_target_pairs={{0,1},{1,0},{2,3},{3,2},{4,5},{5,4},{6,7},{7,6},{8,9},{9,8},{10,11... | collective-permute-start | bytes 1572872 | tf_op jit(solution)/shard_map/ppermute | solution.py:270
  99.6 1.4 %collective-permute-start.6 = (bf16[8,64,128]{2,1,0:T(8,128)(2,1)S(1)}, bf16[8,64,128]{2,1,0:T(8,128)(2,1)S(1)}, u32[]{:S(2)}, u32[]{:S(2)}) collective-permute-start(bf16[8,64,128]{2,1,0:T(8,128)(2,1)S(1)} %get-tuple-element.38), channel_id=1, source_target_pairs={{0,1},{1,0},{2,3},{3,2},{4,5},{5,4},{6,7},{7,6},{8,9},{9,8},{10,11... | collective-permute-start | bytes 393224 | tf_op jit(solution)/shard_map/ppermute | solution.py:270
  136.0 1.5 %collective-permute-start.7 = (f32[64,8,128]{2,1,0:T(8,128)S(1)}, f32[64,8,128]{2,1,0:T(8,128)S(1)}, u32[]{:S(2)}, u32[]{:S(2)}) collective-permute-start(f32[64,8,128]{2,1,0:T(8,128)S(1)} %all_to_all.34.near), channel_id=1, source_target_pairs={{0,1},{1,0},{2,3},{3,2},{4,5},{5,4},{6,7},{7,6},{8,9},{9,8},{10,11... | collective-permute-start | bytes 786440 | tf_op jit(solution)/shard_map/ppermute | solution.py:270
